TPU v7x, 256 devices: a whole 4x4x8 slice. The times are simulated.
256 devices in a mesh: doc: 64 (over z, y, core), feat: 4 (over x).
Axes of the slice: x: 4, y: 4, z: 8, core: 2. Of those that a mesh axis runs over, the one named last changes fastest.
Arguments:
- scores: float32 [768, 128], P('doc'), may hold values from -6 to 6
- clicks: int32 [768, 128], P('doc'), may hold values from 0 to 1, as said below
- lengths: int32 [768], P('doc'), may hold values from 2 to 128, as said below
- t_plus_old: float32 [128], replicated, may hold values from 0.1 to 1
- t_minus_old: float32 [128], replicated, may hold values from 0.1 to 1
- leaf: int32 [98304], P('doc'), may hold values from 0 to 31
- bins: int32 [512, 98304], P('feat', 'doc'), may hold values from 0 to 255
Outputs:
- t_plus: float32 [128], replicated
- t_minus: float32 [128], replicated
- gradients: float32 [2, 98304], P(None, 'doc')
- hist: float32 [512, 64, 256], P(('feat', 'doc'))
Inputs may be any that keep to these rules, and one draw needn't show every extreme that they name: Query q shows its first lengths[q] slots; the first two queries of each block of 12 queries show all 128. `clicks`: values at or beyond a query's length carry no meaning. In the first query of each block of 12 queries the even positions are clicked and the odd ones not; in the second the reverse.
All inputs are finite; a program needn't handle non-finite values.
Results may differ from a plain program's by a relative error of at most 0.0024.
Values may be sent and summed in bfloat16 or wider, within the bound.
No kernel may reach another device: no remote copies, remote signals or barrier semaphores. Data moves between devices by JAX's collectives and lax.ppermute only.
A program may use at most 64 MiB of HBM per device.

v0:
```python
import jax
import jax.numpy as jnp
from jax import lax
from jax.sharding import PartitionSpec as P

BINS = 256
LEAVES = 32


def pair_terms(scores, clicks, lengths, t_plus_old, t_minus_old):
    npos = scores.shape[1]
    places = jnp.arange(npos)
    shown_mask = places[None, :] < lengths[:, None]
    clicked = jnp.where((clicks == 1) & shown_mask, 1.0, 0.0).astype(jnp.float32)
    skipped = jnp.where((clicks == 0) & shown_mask, 1.0, 0.0).astype(jnp.float32)
    paired = clicked[:, :, None] * skipped[:, None, :]
    discount = 1.0 / jnp.log2(2.0 + places.astype(jnp.float32))
    clicks_count = jnp.sum(clicked, axis=1)
    ideal_gain = jnp.sum(
        jnp.where(
            places[None, :].astype(jnp.float32) < clicks_count[:, None], discount[None, :], 0.0
        ),
        axis=1,
    )
    ideal_gain = jnp.maximum(ideal_gain, 1.0)
    change = (
        paired * jnp.abs(discount[:, None] - discount[None, :])[None] / ideal_gain[:, None, None]
    )
    spread = scores[:, :, None] - scores[:, None, :]
    weighted = change * jax.nn.softplus(-spread)
    plus_part = jnp.sum(weighted / t_minus_old[None, None, :], axis=(0, 2))
    minus_part = jnp.sum(weighted / t_plus_old[None, :, None], axis=(0, 1))
    return (change, spread, plus_part, minus_part)


def lambda_rows(change, spread, plus_sum, minus_sum):
    t_plus = jnp.sqrt(plus_sum / plus_sum[0])
    t_minus = jnp.sqrt(minus_sum / minus_sum[0])
    scaled = change / (t_plus[None, :, None] * t_minus[None, None, :])
    chance = jax.nn.sigmoid(-spread)
    lambda_pair = scaled * chance
    second = lambda_pair * (1.0 - chance)
    slopes = jnp.sum(lambda_pair, axis=1) - jnp.sum(lambda_pair, axis=2)
    curvature = jnp.sum(second, axis=1) + jnp.sum(second, axis=2)
    own_rows = jnp.stack([slopes.reshape(-1), curvature.reshape(-1)])
    return (t_plus, t_minus, own_rows)


def leaf_weights(slope_row, curve_row, leaf_row):
    leaf_hit = (leaf_row[None, :] == jnp.arange(LEAVES)[:, None]).astype(jnp.bfloat16)
    return jnp.concatenate([leaf_hit * slope_row[None, :], leaf_hit * curve_row[None, :]], axis=0)


def block_hist(bin_rows, weights, levels):
    one_hot = (bin_rows[:, None, :] == levels[None, :, None]).astype(jnp.bfloat16)
    return jnp.einsum("gr,nbr->ngb", weights, one_hot, preferred_element_type=jnp.float32)


def feature_hist(bin_rows, weights):
    levels = jnp.arange(BINS, dtype=jnp.int32)
    row_count = bin_rows.shape[0]
    block_size = 1
    for option in (8, 4, 2):
        if block_size == 1 and row_count % option == 0:
            block_size = option

    def one_block(block):
        return block_hist(block, weights, levels)

    stacked = lax.map(
        one_block, bin_rows.reshape(row_count // block_size, block_size, bin_rows.shape[1])
    )
    return stacked.reshape(row_count, weights.shape[0], BINS)


def body(scores, clicks, lengths, t_plus_old, t_minus_old, leaf, bins):
    per_feat = scores.shape[0] // lax.axis_size("feat")
    start_row = lax.axis_index("feat") * per_feat
    my_scores = lax.dynamic_slice_in_dim(scores, start_row, per_feat, 0)
    my_clicks = lax.dynamic_slice_in_dim(clicks, start_row, per_feat, 0)
    my_lengths = lax.dynamic_slice_in_dim(lengths, start_row, per_feat, 0)
    change, spread, plus_part, minus_part = pair_terms(
        my_scores, my_clicks, my_lengths, t_plus_old, t_minus_old
    )
    plus_sum, minus_sum = lax.psum((plus_part, minus_part), ("doc", "feat"))
    t_plus, t_minus, own_rows = lambda_rows(change, spread, plus_sum, minus_sum)
    gradients = lax.all_gather(own_rows, "feat", axis=1, tiled=True)
    rounded = gradients.astype(jnp.bfloat16)
    weights = leaf_weights(rounded[0], rounded[1], leaf)
    hist = lax.psum_scatter(feature_hist(bins, weights), "doc", scatter_dimension=0, tiled=True)
    return (t_plus, t_minus, gradients, hist)


def solution(mesh):
    placed = (P("doc", None), P("doc", None), P("doc"), P(), P(), P("doc"), P("feat", "doc"))
    return jax.shard_map(
        body,
        mesh=mesh,
        in_specs=placed,
        out_specs=(P(), P(), P(None, "doc"), P(("feat", "doc"), None, None)),
        check_vma=False,
    )
```

profile of v0, /device:TPU:1, one launch (start us, length us, event | category | flops | bytes accessed | tf_op | source)
XLA Modules:
  0.0 317.6 jit_solution(5064826501937953063)
XLA Ops:
  8.1 0.9 fusion.26
  9.2 1.0 divide_reduce_fusion
  10.2 81.4 %all-reduce = (f32[128]{0:T(128)S(1)}, f32[128]{0:T(128)S(1)}) all-reduce(f32[128]{0:T(128)S(1)} %get-tuple-element.47, f32[128]{0:T(128)S(1)} %get-tuple-element.46), channel_id=1, replica_groups=mesh['doc'=64,'feat'=4] {'doc','feat'}, use_global_device_ids=true, to_apply=%region_3.4 | all-reduce | flops 256 | bytes 2048 | tf_op jit(solution)/shard_map/psum | solution.py:85
  92.1 9.0 %all_gather.3 = f32[2,1536]{1,0:T(2,128)S(1)} all-gather(f32[2,384]{1,0:T(2,128)S(1)} %pad_maximum_fusion.1), channel_id=1, replica_groups=mesh['doc'=64,'feat'=4] {'feat'}, dimensions={1}, use_global_device_ids=true | all-gather | bytes 15360 | tf_op jit(solution)/shard_map/all_gather | solution.py:87
  102.0 61.6 %while.11 = (s32[]{:T(128)}, f32[16,8,64,256]{3,2,1,0:T(8,128)}, s32[16,8,1536]{2,1,0:T(8,128)}, bf16[64,1536]{1,0:T(8,128)(2,1)S(1)}, s32[]{:T(128)}) while((s32[]{:T(128)}, f32[16,8,64,256]{3,2,1,0:T(8,128)}, s32[16,8,1536]{2,1,0:T(8,128)}, bf16[64,1536]{1,0:T(8,128)(2,1)S(1)}, s32[]{:T(128)}) %tuple.41), condition=%wide.region_11.12_spmd.clone, body=%wide.region_10.11_spmd.clone.sunk | while | flops 405798912 | bytes 868929 | solution.py:70
  102.0 0.8 dynamic-slice_bitcast_fusion.2
  102.8 3.0 fusion.31
  105.9 0.8 dynamic-slice_bitcast_fusion.2
  106.7 3.1 fusion.31
  109.7 0.8 dynamic-slice_bitcast_fusion.2
  110.5 3.1 fusion.31
  113.6 0.8 dynamic-slice_bitcast_fusion.2
  114.4 3.1 fusion.31
  117.4 0.8 dynamic-slice_bitcast_fusion.2
  118.2 3.0 fusion.31
  121.3 0.8 dynamic-slice_bitcast_fusion.2
  122.1 3.1 fusion.31
  125.1 0.8 dynamic-slice_bitcast_fusion.2
  125.9 3.0 fusion.31
  129.0 0.8 dynamic-slice_bitcast_fusion.2
  129.8 3.1 fusion.31
  133.6 3.0 fusion.31
  136.6 0.8 dynamic-slice_bitcast_fusion.2
  137.4 3.1 fusion.31
  140.5 0.8 dynamic-slice_bitcast_fusion.2
  141.3 3.0 fusion.31
  145.2 3.1 fusion.31
  149.0 3.0 fusion.31
  152.9 3.1 fusion.31
  156.7 3.0 fusion.31
  160.6 3.1 fusion.31
  163.6 146.5 %reduce-scatter.2.cloned.1.call-done = f32[2,64,256]{2,1,0:T(8,128)} async-done(((f32[128,64,256]{2,1,0:T(8,128)}), f32[2,64,256]{2,1,0:T(8,128)}) %reduce-scatter.2.cloned.1.call-update) | async-done | bytes 131088 | tf_op jit(solution)/shard_map/reduce_scatter | solution.py:90
  (33 shorter events, 7.8 us)
Async XLA Ops:
  7.2 303.0 %reduce-scatter.2.cloned.1.call-start = ((), (), s32[]{:S(2)}) async-start(), calls=%async_computation.1 | async-start | bytes 8519680 | tf_op jit(solution)/shard_map/reduce_scatter | solution.py:90
  91.6 10.4 %copy-start = (f32[128]{0:T(128)}, f32[128]{0:T(128)S(1)}, u32[]{:S(2)}) copy-start(f32[128]{0:T(128)S(1)} %divide_sqrt_fusion) | copy-start | bytes 1540
  91.6 10.4 %copy-start.1 = (f32[128]{0:T(128)}, f32[128]{0:T(128)S(1)}, u32[]{:S(2)}) copy-start(f32[128]{0:T(128)S(1)} %divide_sqrt_fusion.1) | copy-start | bytes 1540
Sparse Core Ops, SparseCore 0:
  163.8 146.3 reduce-scatter.1
where the time goes:
time: 322 us; the launch traced here: 318 us
  waiting for transfers between devices  147 us (46%)
  blocking collectives  90.4 us (28%)
  matrix products  48.7 us (15%)
  local copies, waits for them, and re-layouts  14.2 us (4%)
  between operations  14.2 us (4%)
  other arithmetic  3.45 us (1%)
    reduce_scatter x1, waiting for transfers between devices, body(): lax.psum_scatter(feature_hist(bins, weights), 'doc', scatter_dimension=0,...  146 us
    psum x1, blocking collectives, body(): plus_sum, minus_sum = lax.psum((plus_part, minus_part), ('doc', 'feat'))  81.4 us
    dot_general x16, matrix products, block_hist(): jnp.einsum('gr,nbr->ngb', weights, one_hot, preferred_element_type=jnp.fl...  48.7 us
    eq x16, local copies, waits for them, and re-layouts, block_hist(): bin_rows[:, None, :] == levels[None, :, None]  12.8 us
    all_gather x1, blocking collectives, body(): gradients = lax.all_gather(own_rows, 'feat', axis=1, tiled=True)  9.05 us
  transfers between devices with their start and end apart: 1, of which 1 were waited for; matrix products, arithmetic and copies ran while one was open for 0% of the time, Pallas kernels for 0%

commit v1 on v0

v1 whole, which is shorter than its diff:
```python
import jax
import jax.numpy as jnp
from jax import lax
from jax.experimental import pallas as pl
from jax.experimental.pallas import tpu as pltpu
from jax.sharding import PartitionSpec as P

BINS = 256
LEAVES = 32
POS = 128


def pair_terms(scores, clicks, lengths, t_plus_old, t_minus_old):
    npos = scores.shape[1]
    places = jnp.arange(npos)
    shown_mask = places[None, :] < lengths[:, None]
    clicked = jnp.where((clicks == 1) & shown_mask, 1.0, 0.0).astype(jnp.float32)
    skipped = jnp.where((clicks == 0) & shown_mask, 1.0, 0.0).astype(jnp.float32)
    paired = clicked[:, :, None] * skipped[:, None, :]
    discount = 1.0 / jnp.log2(2.0 + places.astype(jnp.float32))
    clicks_count = jnp.sum(clicked, axis=1)
    ideal_gain = jnp.sum(
        jnp.where(
            places[None, :].astype(jnp.float32) < clicks_count[:, None], discount[None, :], 0.0
        ),
        axis=1,
    )
    ideal_gain = jnp.maximum(ideal_gain, 1.0)
    change = (
        paired * jnp.abs(discount[:, None] - discount[None, :])[None] / ideal_gain[:, None, None]
    )
    spread = scores[:, :, None] - scores[:, None, :]
    weighted = change * jax.nn.softplus(-spread)
    plus_part = jnp.sum(weighted / t_minus_old[None, None, :], axis=(0, 2))
    minus_part = jnp.sum(weighted / t_plus_old[None, :, None], axis=(0, 1))
    return (change, spread, plus_part, minus_part)


def lambda_rows(change, spread, plus_sum, minus_sum):
    t_plus = jnp.sqrt(plus_sum / plus_sum[0])
    t_minus = jnp.sqrt(minus_sum / minus_sum[0])
    scaled = change / (t_plus[None, :, None] * t_minus[None, None, :])
    chance = jax.nn.sigmoid(-spread)
    lambda_pair = scaled * chance
    second = lambda_pair * (1.0 - chance)
    slopes = jnp.sum(lambda_pair, axis=1) - jnp.sum(lambda_pair, axis=2)
    curvature = jnp.sum(second, axis=1) + jnp.sum(second, axis=2)
    own_rows = jnp.stack([slopes.reshape(-1), curvature.reshape(-1)])
    return (t_plus, t_minus, own_rows)


def hist_kernel(data_ref, grad_ref, out_ref):
    blocks, rows, width = data_ref.shape
    owned = rows - 1
    out_ref[...] = jnp.zeros_like(out_ref)
    leaves = lax.broadcasted_iota(jnp.int32, (LEAVES, width), 0).astype(jnp.bfloat16)
    levels = lax.broadcasted_iota(jnp.int32, (BINS, width), 0).astype(jnp.bfloat16)

    def one_block(block, carry):
        rows_here = data_ref[block]
        grads = grad_ref[block]
        hit = rows_here[owned : owned + 1] == leaves
        zero = jnp.zeros((), jnp.bfloat16)
        one = jnp.ones((), jnp.bfloat16)
        weights = jnp.concatenate(
            [jnp.where(hit, grads[0:1], zero), jnp.where(hit, grads[1:2], zero)], axis=0
        )
        for feature in range(owned):
            one_hot = jnp.where(rows_here[feature : feature + 1] == levels, one, zero)
            out_ref[feature] += lax.dot_general(
                weights, one_hot, (((1,), (1,)), ((), ())), preferred_element_type=jnp.float32
            )
        return carry

    lax.fori_loop(0, blocks, one_block, 0)


def owned_hist(data, grads):
    owned = data.shape[1] - 1
    vmem = pl.BlockSpec(memory_space=pltpu.VMEM)
    return pl.pallas_call(
        hist_kernel,
        out_shape=jax.ShapeDtypeStruct((owned, 2 * LEAVES, BINS), jnp.float32),
        in_specs=[vmem, vmem],
        out_specs=vmem,
        name="hist",
    )(data, grads)


def body(scores, clicks, lengths, t_plus_old, t_minus_old, leaf, bins):
    shards = lax.axis_size("doc")
    width = leaf.shape[0]
    owned = bins.shape[0] // shards
    rows = jnp.concatenate(
        [
            bins.reshape(shards, owned, width),
            jnp.broadcast_to(leaf[None, None, :], (shards, 1, width)),
        ],
        axis=1,
    ).astype(jnp.bfloat16)
    data = lax.all_to_all(rows, "doc", 0, 0, tiled=True)
    change, spread, plus_part, minus_part = pair_terms(
        scores, clicks, lengths, t_plus_old, t_minus_old
    )
    parts = jnp.concatenate([plus_part, minus_part])
    parts = lax.all_to_all(
        jnp.broadcast_to(parts[None], (shards,) + parts.shape), "doc", 0, 0, tiled=True
    )
    sums = jnp.sum(parts, axis=0)
    t_plus, t_minus, gradients = lambda_rows(change, spread, sums[:POS], sums[POS:])
    rounded = gradients.astype(jnp.bfloat16)
    grads = lax.all_to_all(
        jnp.broadcast_to(rounded[None], (shards,) + rounded.shape), "doc", 0, 0, tiled=True
    )
    hist = owned_hist(data, grads)
    return (t_plus, t_minus, gradients, hist)


def solution(mesh):
    placed = (P("doc", None), P("doc", None), P("doc"), P(), P(), P("doc"), P("feat", "doc"))
    return jax.shard_map(
        body,
        mesh=mesh,
        in_specs=placed,
        out_specs=(P(), P(), P(None, "doc"), P(("feat", "doc"), None, None)),
        check_vma=False,
    )
```

time: 322 us -> 121 us (0.38); the launches traced: 318 us -> 120 us
  waiting for transfers between devices: 147 us -> 14.1 us
  matrix products: 48.7 us -> 0 us
  Pallas kernels: 0 us -> 41 us
  blocking collectives: 90.4 us -> 51.3 us
  between operations: 14.2 us -> 0.83 us
  local copies, waits for them, and re-layouts: 14.2 us -> 1.9 us
  starting transfers between devices: 0.04 us -> 4.46 us
  other arithmetic: 3.45 us -> 6.78 us
    reduce_scatter x1 -> x0, waiting for transfers between devices: 146 us -> none  [body(): lax.psum_scatter(feature_hist(bins, weights), 'doc', scatter_dimension=0,...]
    psum x1 -> x0, blocking collectives: 81.4 us -> none  [body(): plus_sum, minus_sum = lax.psum((plus_part, minus_part), ('doc', 'feat'))]
    all_to_all x0 -> x2, blocking collectives: none -> 51.3 us  [the longest x1 28.3 us: body(): data = lax.all_to_all(rows, 'doc', 0, 0, tiled=True)]
    dot_general x16 -> x0, matrix products: 48.7 us -> none  [block_hist(): jnp.einsum('gr,nbr->ngb', weights, one_hot, preferred_element_type=jnp.fl...]
    pallas_call x0 -> x1, Pallas kernels: none -> 41 us  [owned_hist(): pl.pallas_call(hist_kernel, out_shape=jax.ShapeDtypeStruct((owned, 2 * LE...]
    all_to_all x0 -> x1, waiting for transfers between devices: none -> 14.1 us  [body(): lax.all_to_all(jnp.broadcast_to(rounded[None], (shards,) + rounded.shape)...]
    eq x16 -> x0, local copies, waits for them, and re-layouts: 12.8 us -> none  [block_hist(): bin_rows[:, None, :] == levels[None, :, None]]
    all_gather x1 -> x0, blocking collectives: 9.05 us -> none  [body(): gradients = lax.all_gather(own_rows, 'feat', axis=1, tiled=True)]
  transfers between devices with their start and end apart: 1 -> 1, of which waited for: 1 -> 1; matrix products, arithmetic and copies ran while one was open for 0% -> 1% of each run, Pallas kernels for 0% -> 0%
where the time goes in v1:
time: 121 us; the launch traced here: 120 us
  blocking collectives  51.3 us (42%)
  Pallas kernels  41 us (34%)
  waiting for transfers between devices  14.1 us (12%)
  other arithmetic  6.78 us (6%)
  starting transfers between devices  4.46 us (4%)
  local copies, waits for them, and re-layouts  1.9 us (2%)
    pallas_call x1, Pallas kernels, owned_hist(): pl.pallas_call(hist_kernel, out_shape=jax.ShapeDtypeStruct((owned, 2 * LE...  41 us
    all_to_all x1, blocking collectives, body(): data = lax.all_to_all(rows, 'doc', 0, 0, tiled=True)  28.3 us
    all_to_all x1, blocking collectives, body(): lax.all_to_all(jnp.broadcast_to(parts[None], (shards,) + parts.shape), 'd...  23 us
    all_to_all x1, waiting for transfers between devices, body(): lax.all_to_all(jnp.broadcast_to(rounded[None], (shards,) + rounded.shape)...  14.1 us
    all_to_all x1, starting transfers between devices, body(): lax.all_to_all(jnp.broadcast_to(rounded[None], (shards,) + rounded.shape)...  4.46 us
  transfers between devices with their start and end apart: 1, of which 1 were waited for; matrix products, arithmetic and copies ran while one was open for 1% of the time, Pallas kernels for 0%

profile of v1, /device:TPU:1, one launch (start us, length us, event | category | flops | bytes accessed | tf_op | source)
XLA Modules:
  0.0 120.3 jit_solution(6256195046772861750)
XLA Ops:
  0.6 0.0 copy-start.5
  0.7 0.1 subtract_abs_fusion
  0.8 0.9 fusion.18
  1.7 0.2 select_reduce_fusion
  1.8 1.6 %divide_reduce_fusion.1 = (f32[128]{0:T(128)S(1)}, f32[128]{0:T(128)S(1)}) fusion(f32[128]{0:T(128)} %param.11, f32[12,128]{1,0:T(8,128)} %param.7, f32[12]{0:T(128)S(1)} %broadcast_maximum_fusion, f32[128,128]{1,0:T(8,128)S(1)} %subtract_abs_fusion, f32[12,128]{1,0:T(8,128)S(1)} %get-tuple-element.14, f32[12,128]{1,0:T(8,128)S(1)} %get-tuple-element.13, ...), kind=kLoop, calls=%fused_computation.17 | loop fusion | flops 3145472 | bytes 86064 | tf_op jit(solution)/shard_map/reduce_sum | solution.py:34
  3.5 23.0 %all_to_all.16 = f32[64,1,256]{2,1,0:T(1,128)S(1)} all-to-all(f32[64,1,256]{2,1,0:T(1,128)S(1)} %broadcast_in_dim.29), channel_id=1, replica_groups=mesh['doc'=64,'feat'=4] {'doc'}, dimensions={0} | all-to-all | bytes 131072 | tf_op jit(solution)/shard_map/all_to_all | solution.py:106
  26.6 0.1 reduce_sum.85
  26.7 0.5 fusion.20
  27.2 1.3 %divide_sqrt_fusion = (f32[128]{0:T(128)S(1)}, f32[128]{0:T(128)S(1)}) fusion(f32[256]{0:T(256)S(1)} %reduce_sum.85, f32[]{:T(128)} %bitcast.1, f32[]{:T(128)} %bitcast), kind=kLoop, calls=%fused_computation.36 | loop fusion | flops 256 | bytes 2056 | tf_op jit(solution)/shard_map/sqrt | solution.py:41
  28.5 0.0 copy-start.3
  28.5 0.0 copy-start.4
  28.5 0.1 broadcast_multiply_fusion
  28.6 0.0 copy-done.5
  28.6 0.0 copy-start.2
  28.6 0.0 copy-start.1
  28.6 1.0 fusion.9
  29.7 0.6 fusion.17
  30.3 0.9 broadcast_in_dim.31
  31.2 0.0 copy-done.3
  31.3 0.0 copy-done.4
  31.3 4.5 %all-to-all-start.2 = ((bf16[64,2,1536]{2,1,0:T(2,128)(2,1)}), bf16[64,2,1536]{2,1,0:T(2,128)(2,1)S(1)}, u32[]{:S(2)}, u32[]{:S(2)}) async-start(bf16[64,2,1536]{2,1,0:T(2,128)(2,1)} %broadcast_in_dim.31), calls=%async_computation.2 | async-start | bytes 786432 | tf_op jit(solution)/shard_map/all_to_all | solution.py:112
  35.7 0.0 copy-done.2
  35.7 0.0 copy-done.1
  35.8 0.1 reshape.166
  36.0 0.2 broadcast_in_dim.30
  36.2 0.8 pad_maximum_fusion
  37.0 14.1 %all-to-all-done.2.grad_ref = bf16[64,2,1536]{2,1,0:T(2,128)(2,1)S(1)} async-done(((bf16[64,2,1536]{2,1,0:T(2,128)(2,1)}), bf16[64,2,1536]{2,1,0:T(2,128)(2,1)S(1)}, u32[]{:S(2)}, u32[]{:S(2)}) %all-to-all-start.2) | async-done | bytes 393248 | tf_op jit(solution)/shard_map/all_to_all | solution.py:112
  51.0 0.0 copy-start
  51.1 28.3 %all_to_all.17.data_ref = bf16[64,3,1536]{2,1,0:T(4,128)(2,1)} all-to-all(bf16[64,3,1536]{2,1,0:T(4,128)(2,1)S(1)} %pad_maximum_fusion), channel_id=1, replica_groups=mesh['doc'=64,'feat'=4] {'doc'}, dimensions={0} | all-to-all | bytes 1179648 | tf_op jit(solution)/shard_map/all_to_all | solution.py:101
  79.3 0.0 copy-done
  79.3 41.0 %hist.1 = f32[2,64,256]{2,1,0:T(8,128)} custom-call(bf16[64,3,1536]{2,1,0:T(4,128)(2,1)} %all_to_all.17.data_ref, bf16[64,2,1536]{2,1,0:T(2,128)(2,1)} %copy-done), custom_call_target="tpu_custom_call" | custom-call | tf_op jit(solution)/shard_map/hist/pallas_call | solution.py:81
  (10 shorter events, 0.1 us)
Async XLA Ops:
  0.6 28.0 %copy-start.5 = (f32[12,128]{1,0:T(8,128)S(1)}, f32[12,128]{1,0:T(8,128)}, u32[]{:S(2)}) copy-start(f32[12,128]{1,0:T(8,128)} %param.7) | copy-start | bytes 18436
  28.5 2.8 %copy-start.3 = (f32[128]{0:T(128)}, f32[128]{0:T(128)S(1)}, u32[]{:S(2)}) copy-start(f32[128]{0:T(128)S(1)} %get-tuple-element.15) | copy-start | bytes 1540
  28.5 2.8 %copy-start.4 = (f32[128]{0:T(128)}, f32[128]{0:T(128)S(1)}, u32[]{:S(2)}) copy-start(f32[128]{0:T(128)S(1)} %get-tuple-element.16) | copy-start | bytes 1540
  28.6 7.1 %copy-start.2 = (s32[1536]{0:T(1024)S(1)}, s32[1536]{0:T(1024)}, u32[]{:S(2)}) copy-start(s32[1536]{0:T(1024)} %param.12) | copy-start | bytes 18436
  28.6 7.1 %copy-start.1 = (s32[128,1536]{1,0:T(8,128)S(1)}, s32[128,1536]{1,0:T(8,128)}, u32[]{:S(2)}) copy-start(s32[128,1536]{1,0:T(8,128)} %param.13) | copy-start | bytes 2359300
  31.3 19.8 %all-to-all-start.2 = ((bf16[64,2,1536]{2,1,0:T(2,128)(2,1)}), bf16[64,2,1536]{2,1,0:T(2,128)(2,1)S(1)}, u32[]{:S(2)}, u32[]{:S(2)}) async-start(bf16[64,2,1536]{2,1,0:T(2,128)(2,1)} %broadcast_in_dim.31), calls=%async_computation.2 | async-start | bytes 786432 | tf_op jit(solution)/shard_map/all_to_all | solution.py:112
  51.0 28.3 %copy-start = (bf16[64,2,1536]{2,1,0:T(2,128)(2,1)}, bf16[64,2,1536]{2,1,0:T(2,128)(2,1)S(1)}, u32[]{:S(2)}) copy-start(bf16[64,2,1536]{2,1,0:T(2,128)(2,1)S(1)} %all-to-all-done.2.grad_ref) | copy-start | bytes 1179652

commit v2 on v1

v2 whole, which is shorter than its diff:
```python
import jax
import jax.numpy as jnp
from jax import lax
from jax.experimental import pallas as pl
from jax.experimental.pallas import tpu as pltpu
from jax.sharding import PartitionSpec as P

BINS = 256
LEAVES = 32
POS = 128
HALF = BINS // 2
PER = 4


def pair_terms(scores, clicks, lengths, t_plus_old, t_minus_old):
    npos = scores.shape[1]
    places = jnp.arange(npos)
    shown_mask = places[None, :] < lengths[:, None]
    clicked = jnp.where((clicks == 1) & shown_mask, 1.0, 0.0).astype(jnp.float32)
    skipped = jnp.where((clicks == 0) & shown_mask, 1.0, 0.0).astype(jnp.float32)
    paired = clicked[:, :, None] * skipped[:, None, :]
    discount = 1.0 / jnp.log2(2.0 + places.astype(jnp.float32))
    clicks_count = jnp.sum(clicked, axis=1)
    ideal_gain = jnp.sum(
        jnp.where(
            places[None, :].astype(jnp.float32) < clicks_count[:, None], discount[None, :], 0.0
        ),
        axis=1,
    )
    ideal_gain = jnp.maximum(ideal_gain, 1.0)
    change = (
        paired * jnp.abs(discount[:, None] - discount[None, :])[None] / ideal_gain[:, None, None]
    )
    spread = scores[:, :, None] - scores[:, None, :]
    weighted = change * jax.nn.softplus(-spread)
    plus_part = jnp.sum(weighted / t_minus_old[None, None, :], axis=(0, 2))
    minus_part = jnp.sum(weighted / t_plus_old[None, :, None], axis=(0, 1))
    return (change, spread, plus_part, minus_part)


def lambda_rows(change, spread, plus_sum, minus_sum):
    t_plus = jnp.sqrt(plus_sum / plus_sum[0])
    t_minus = jnp.sqrt(minus_sum / minus_sum[0])
    scaled = change / (t_plus[None, :, None] * t_minus[None, None, :])
    chance = jax.nn.sigmoid(-spread)
    lambda_pair = scaled * chance
    second = lambda_pair * (1.0 - chance)
    slopes = jnp.sum(lambda_pair, axis=1) - jnp.sum(lambda_pair, axis=2)
    curvature = jnp.sum(second, axis=1) + jnp.sum(second, axis=2)
    own_rows = jnp.stack([slopes.reshape(-1), curvature.reshape(-1)])
    return (t_plus, t_minus, own_rows)


def accumulate(core, data_ref, side_ref, acc):
    blocks, _, wide = side_ref.shape
    width = wide * 2 // 3
    rows_a = lax.broadcasted_iota(jnp.int32, (2 * LEAVES, width), 0).astype(jnp.bfloat16)
    rows_b = lax.broadcasted_iota(jnp.int32, (HALF, width), 0).astype(jnp.bfloat16)
    zero = jnp.zeros((), jnp.bfloat16)
    one = jnp.ones((), jnp.bfloat16)

    def some_blocks(step, carry):
        left = [[], []]
        right = [[], []]
        for at in range(PER):
            block = step * PER + at
            side = side_ref[block]
            bins = data_ref[2 * block + core][:, :width]
            leaf = jnp.concatenate([side[0:1, width:], side[1:2, width:]], axis=1)
            for feature in range(2):
                row = bins[feature : feature + 1]
                high = row >= jnp.asarray(HALF, jnp.bfloat16)
                hit = jnp.where(high, leaf + jnp.asarray(LEAVES, jnp.bfloat16), leaf) == rows_a
                low = jnp.where(high, row - jnp.asarray(HALF, jnp.bfloat16), row)
                left[feature].append(
                    jnp.concatenate(
                        [
                            jnp.where(hit, side[0:1, :width], zero),
                            jnp.where(hit, side[1:2, :width], zero),
                        ],
                        axis=0,
                    )
                )
                right[feature].append(jnp.where(low == rows_b, one, zero))
        for feature in range(2):
            acc[feature] += lax.dot_general(
                jnp.concatenate(left[feature], axis=1),
                jnp.concatenate(right[feature], axis=1),
                (((1,), (1,)), ((), ())),
                preferred_element_type=jnp.float32,
            )
        return carry

    lax.fori_loop(0, blocks // PER, some_blocks, 0)


def first_kernel(core_ref, data_ref, side_ref, out_ref):
    out_ref[...] = jnp.zeros_like(out_ref)
    accumulate(core_ref[0], data_ref, side_ref, out_ref)


def second_kernel(core_ref, data_ref, side_ref, before_ref, out_ref, acc):
    acc[...] = before_ref[...]
    accumulate(core_ref[0], data_ref, side_ref, acc)
    for feature in range(2):
        for which in range(2):
            for high in range(2):
                out_ref[
                    feature,
                    which * LEAVES : (which + 1) * LEAVES,
                    high * HALF : (high + 1) * HALF,
                ] = acc[feature, (2 * which + high) * LEAVES : (2 * which + high + 1) * LEAVES, :]


def hist_of(core, data, side, before=None):
    vmem = pl.BlockSpec(memory_space=pltpu.VMEM)
    smem = pl.BlockSpec(memory_space=pltpu.SMEM)
    part = (2, 4 * LEAVES, HALF)
    if before is None:
        return pl.pallas_call(
            first_kernel,
            out_shape=jax.ShapeDtypeStruct(part, jnp.float32),
            in_specs=[smem, vmem, vmem],
            out_specs=vmem,
            name="first_half",
        )(core, data, side)
    return pl.pallas_call(
        second_kernel,
        out_shape=jax.ShapeDtypeStruct((2, 2 * LEAVES, BINS), jnp.float32),
        in_specs=[smem, vmem, vmem, vmem],
        out_specs=vmem,
        scratch_shapes=[pltpu.VMEM(part, jnp.float32)],
        name="second_half",
    )(core, data, side, before)


def body(scores, clicks, lengths, t_plus_old, t_minus_old, leaf, bins):
    shards = lax.axis_size("doc")
    width = leaf.shape[0]
    change, spread, plus_part, minus_part = pair_terms(
        scores, clicks, lengths, t_plus_old, t_minus_old
    )
    parts = jnp.concatenate([plus_part, minus_part])
    parts_high = parts.astype(jnp.bfloat16)
    parts_rest = (parts - parts_high.astype(jnp.float32)).astype(jnp.bfloat16)
    parts = jnp.stack([parts_high, parts_rest])
    sent = jnp.concatenate(
        [
            bins.astype(jnp.bfloat16).reshape(shards, 2, width),
            jnp.broadcast_to(parts[None], (shards,) + parts.shape),
        ],
        axis=2,
    )
    data = lax.all_to_all(sent, "doc", 0, 0, tiled=True)
    sums = jnp.sum(data[:, :, width:].astype(jnp.float32), axis=(0, 1))
    t_plus, t_minus, gradients = lambda_rows(change, spread, sums[:POS], sums[POS:])
    side = jnp.concatenate(
        [gradients.astype(jnp.bfloat16), leaf.astype(jnp.bfloat16).reshape(2, width // 2)], axis=1
    )
    same_core = [[2 * chip + core for chip in range(shards // 2)] for core in range(2)]
    side = lax.all_to_all(
        jnp.broadcast_to(side[None], (shards // 2,) + side.shape),
        "doc",
        0,
        0,
        axis_index_groups=same_core,
        tiled=True,
    )
    other_side = lax.ppermute(side, "doc", [(at, at ^ 1) for at in range(shards)])
    core = lax.axis_index("doc") % 2
    partial = hist_of(core.reshape(1), data, side)
    hist = hist_of((1 - core).reshape(1), data, other_side, partial)
    return (t_plus, t_minus, gradients, hist)


def solution(mesh):
    placed = (P("doc", None), P("doc", None), P("doc"), P(), P(), P("doc"), P("feat", "doc"))
    return jax.shard_map(
        body,
        mesh=mesh,
        in_specs=placed,
        out_specs=(P(), P(), P(None, "doc"), P(("feat", "doc"), None, None)),
        check_vma=False,
    )
```

time: 121 us -> 78.9 us (0.65)
  blocking collectives: 51.3 us -> 16.3 us
  Pallas kernels: 41 us -> 19.6 us
  starting transfers between devices: 4.46 us -> 15.5 us
  waiting for transfers between devices: 14.1 us -> 16.3 us
    all_to_all x2 -> x1, blocking collectives: 51.3 us -> 16.3 us  [body(): lax.all_to_all(jnp.broadcast_to(side[None], (shards // 2,) + side.shape),...]
    pallas_call x1 -> x2, Pallas kernels: 41 us -> 19.6 us  [the longest x1 9.8 us: hist_of(): pl.pallas_call(second_kernel, out_shape=jax.ShapeDtypeStruct((2, 2 * LEAV...]
    all_to_all x1, starting transfers between devices: 4.46 us -> 13.3 us  [body(): data = lax.all_to_all(sent, 'doc', 0, 0, tiled=True)]
    all_to_all x1, waiting for transfers between devices: 14.1 us -> 16.3 us  [body(): data = lax.all_to_all(sent, 'doc', 0, 0, tiled=True)]
    ppermute x0 -> x1, starting transfers between devices: none -> 2.18 us  [body(): lax.ppermute(side, 'doc', [(at, at ^ 1) for at in range(shards)])]
    unnamed x14 -> x18, local copies, waits for them, and re-layouts: 0.05 us -> 1.86 us
  transfers between devices with their start and end apart: 1 -> 2, of which waited for: 1 -> 1; matrix products, arithmetic and copies ran while one was open for 1% -> 0% of each run, Pallas kernels for 0% -> 12%
where the time goes in v2:
time: 78.9 us; the launch traced here: 78.5 us
  Pallas kernels  19.6 us (25%)
  waiting for transfers between devices  16.3 us (21%)
  blocking collectives  16.3 us (21%)
  starting transfers between devices  15.5 us (20%)
  other arithmetic  7.26 us (9%)
  local copies, waits for them, and re-layouts  2.79 us (4%)
  between operations  0.82 us (1%)
    all_to_all x1, waiting for transfers between devices, body(): data = lax.all_to_all(sent, 'doc', 0, 0, tiled=True)  16.3 us
    all_to_all x1, blocking collectives, body(): lax.all_to_all(jnp.broadcast_to(side[None], (shards // 2,) + side.shape),...  16.3 us
    all_to_all x1, starting transfers between devices, body(): data = lax.all_to_all(sent, 'doc', 0, 0, tiled=True)  13.3 us
    pallas_call x1, Pallas kernels, hist_of(): pl.pallas_call(second_kernel, out_shape=jax.ShapeDtypeStruct((2, 2 * LEAV...  9.8 us
    pallas_call x1, Pallas kernels, hist_of(): pl.pallas_call(first_kernel, out_shape=jax.ShapeDtypeStruct(part, jnp.flo...  9.76 us
    ppermute x1, starting transfers between devices, body(): lax.ppermute(side, 'doc', [(at, at ^ 1) for at in range(shards)])  2.18 us
    unnamed x18, local copies, waits for them, and re-layouts  1.86 us
    reduce_sum x1, other arithmetic, pair_terms(): plus_part = jnp.sum(weighted / t_minus_old[None, None, :], axis=(0, 2))  1.62 us
  transfers between devices with their start and end apart: 2, of which 1 were waited for; matrix products, arithmetic and copies ran while one was open for 0% of the time, Pallas kernels for 12%

profile of v2, /device:TPU:1, one launch (start us, length us, event | category | flops | bytes accessed | tf_op | source)
XLA Modules:
  0.0 78.5 jit_solution(2653985481859589378)
XLA Ops:
  0.6 0.0 copy-start.2
  0.7 0.1 subtract_abs_fusion
  0.8 1.0 %fusion.19 = (f32[12]{0:T(128)S(1)}, f32[12,128]{1,0:T(8,128)S(1)}, f32[12,128]{1,0:T(8,128)S(1)}) fusion(s32[12]{0:T(128)} %param.9, s32[12,128]{1,0:T(8,128)} %param.8), kind=kLoop, calls=%fused_computation.47 | loop fusion | flops 12276 | bytes 18528 | tf_op jit(solution)/shard_map/reduce_sum | solution.py:23
  1.7 0.2 select_reduce_fusion
  1.9 1.6 %divide_reduce_fusion.1 = (f32[128]{0:T(128)S(1)}, f32[128]{0:T(128)S(1)}) fusion(f32[128]{0:T(128)} %param.11, f32[12,128]{1,0:T(8,128)} %param.7, f32[12]{0:T(128)S(1)} %broadcast_maximum_fusion, f32[128,128]{1,0:T(8,128)S(1)} %subtract_abs_fusion, f32[12,128]{1,0:T(8,128)S(1)} %get-tuple-element.14, f32[12,128]{1,0:T(8,128)S(1)} %get-tuple-element.13, ...), kind=kLoop, calls=%fused_computation.16 | loop fusion | flops 3145472 | bytes 86064 | tf_op jit(solution)/shard_map/reduce_sum | solution.py:36
  3.6 0.0 copy-done.2
  3.6 0.1 reshape.218
  3.8 1.2 %pad_maximum_fusion = bf16[64,2,1792]{2,1,0:T(2,128)(2,1)} fusion(bf16[64,2,256]{2,1,0:T(2,128)(2,1)S(1)} %broadcast_in_dim.27, bf16[64,2,1536]{2,1,0:T(2,128)(2,1)S(1)} %reshape.218), kind=kLoop, calls=%fused_computation.17 | loop fusion | flops 917504 | bytes 917504 | tf_op jit(solution)/shard_map/concatenate | solution.py:147
  5.0 0.0 copy-start.4
  5.0 13.3 %all-to-all-start = ((bf16[64,2,1792]{2,1,0:T(2,128)(2,1)}), bf16[64,2,1792]{2,1,0:T(2,128)(2,1)S(1)}, u32[]{:S(2)}, u32[]{:S(2)}) async-start(bf16[64,2,1792]{2,1,0:T(2,128)(2,1)} %pad_maximum_fusion), calls=%async_computation | async-start | bytes 917504 | tf_op jit(solution)/shard_map/all_to_all | solution.py:154
  18.3 0.0 copy-done.4
  18.3 16.3 %all-to-all-done.data_ref = bf16[64,2,1792]{2,1,0:T(2,128)(2,1)S(1)} async-done(((bf16[64,2,1792]{2,1,0:T(2,128)(2,1)}), bf16[64,2,1792]{2,1,0:T(2,128)(2,1)S(1)}, u32[]{:S(2)}, u32[]{:S(2)}) %all-to-all-start) | async-done | bytes 458784 | tf_op jit(solution)/shard_map/all_to_all | solution.py:154
  34.7 0.1 convert_reduce_fusion
  34.8 0.6 fusion.21
  35.3 1.3 %divide_sqrt_fusion = (f32[128]{0:T(128)S(1)}, f32[128]{0:T(128)S(1)}) fusion(f32[256]{0:T(256)S(1)} %convert_reduce_fusion, f32[]{:T(128)} %bitcast.3, f32[]{:T(128)} %bitcast.2), kind=kLoop, calls=%fused_computation.40 | loop fusion | flops 256 | bytes 2056 | tf_op jit(solution)/shard_map/sqrt | solution.py:43
  36.6 0.0 copy-start.5
  36.7 0.0 copy-start.6
  36.7 0.5 copy-done.5
  37.2 0.0 copy-done.6
  37.2 0.1 broadcast_multiply_fusion
  37.3 0.6 copy-done.7
  37.9 1.0 %fusion.9 = (f32[12,128]{1,0:T(8,128)S(1)}, f32[12,128]{1,0:T(8,128)S(1)}, f32[12,128]{1,0:T(8,128)S(1)}, f32[12,128]{1,0:T(8,128)S(1)}) fusion(f32[12,128]{1,0:T(8,128)S(1)} %copy-done.7, f32[128,128]{1,0:T(8,128)S(1)} %broadcast_multiply_fusion, f32[12]{0:T(128)S(1)} %broadcast_maximum_fusion, f32[128,128]{1,0:T(8,128)S(1)} %subtract_abs_fusion, ...), kind=kLoop, calls=%fused_computation.18 | loop fusion | flops 2746368 | bytes 174128 | tf_op jit(solution)/shard_map/reduce_sum | solution.py:48
  38.9 0.6 fusion.18
  39.6 0.2 broadcast_in_dim.28
  39.7 0.0 copy-done
  39.8 16.3 %all_to_all.10.side_ref = bf16[32,2,2304]{2,1,0:T(2,128)(2,1)S(1)} all-to-all(bf16[32,2,2304]{2,1,0:T(2,128)(2,1)S(1)} %broadcast_in_dim.28), channel_id=1, replica_groups={{0,8,16,24,32,40,48,56,64,72,80,88,96,104,112,120,128,136,144,152,160,1..., dimensions={0} | all-to-all | bytes 589824 | tf_op jit(solution)/shard_map/all_to_all | solution.py:161
  56.1 2.2 %collective-permute-start = (bf16[32,2,2304]{2,1,0:T(2,128)(2,1)S(1)}, bf16[32,2,2304]{2,1,0:T(2,128)(2,1)S(1)}, u32[]{:S(2)}, u32[]{:S(2)}) collective-permute-start(bf16[32,2,2304]{2,1,0:T(2,128)(2,1)S(1)} %all_to_all.10.side_ref), channel_id=1, source_target_pairs={{0,4},{4,0},{8,12},{12,8},{16,20},{20,16},{24,28},{28,24},{32,36},... | collective-permute-start | bytes 884744 | tf_op jit(solution)/shard_map/ppermute | solution.py:169
  58.2 0.0 copy-done.1
  58.2 9.8 %first_half.1.before_ref = f32[2,128,128]{2,1,0:T(8,128)} custom-call(s32[1]{0:T(128)} %bitcast.5.core_ref, bf16[64,2,1792]{2,1,0:T(2,128)(2,1)} %copy-done, bf16[32,2,2304]{2,1,0:T(2,128)(2,1)} %copy-done.1), custom_call_target="tpu_custom_call" | custom-call | tf_op jit(solution)/shard_map/first_half/pallas_call | solution.py:120
  68.0 0.0 collective-permute-done.side_ref
  68.0 0.7 copy-done.3
  68.7 9.8 %second_half.1 = f32[2,64,256]{2,1,0:T(8,128)} custom-call(s32[1]{0:T(128)} %bitcast.4.core_ref, bf16[64,2,1792]{2,1,0:T(2,128)(2,1)} %copy-done, bf16[32,2,2304]{2,1,0:T(2,128)(2,1)} %copy-done.3, f32[2,128,128]{2,1,0:T(8,128)} %first_half.1.before_ref), custom_call_target="tpu_custom_call" | custom-call | tf_op jit(solution)/shard_map/second_half/pallas_call | solution.py:127
  (18 shorter events, 0.2 us)
Async XLA Ops:
  0.6 2.9 %copy-start.2 = (s32[128,1536]{1,0:T(8,128)S(1)}, s32[128,1536]{1,0:T(8,128)}, u32[]{:S(2)}) copy-start(s32[128,1536]{1,0:T(8,128)} %param.13) | copy-start | bytes 2359300
  5.0 13.3 %copy-start.4 = (s32[1536]{0:T(1024)S(1)}, s32[1536]{0:T(1024)}, u32[]{:S(2)}) copy-start(s32[1536]{0:T(1024)} %param.12) | copy-start | bytes 18436
  5.0 29.6 %all-to-all-start = ((bf16[64,2,1792]{2,1,0:T(2,128)(2,1)}), bf16[64,2,1792]{2,1,0:T(2,128)(2,1)S(1)}, u32[]{:S(2)}, u32[]{:S(2)}) async-start(bf16[64,2,1792]{2,1,0:T(2,128)(2,1)} %pad_maximum_fusion), calls=%async_computation | async-start | bytes 917504 | tf_op jit(solution)/shard_map/all_to_all | solution.py:154
  34.7 5.1 %copy-start = (bf16[64,2,1792]{2,1,0:T(2,128)(2,1)}, bf16[64,2,1792]{2,1,0:T(2,128)(2,1)S(1)}, u32[]{:S(2)}) copy-start(bf16[64,2,1792]{2,1,0:T(2,128)(2,1)S(1)} %all-to-all-done.data_ref) | copy-start | bytes 1376260
  36.6 0.5 copy-start.5
  36.7 0.5 copy-start.6
  37.2 0.7 copy-start.7
  56.1 2.2 %copy-start.1 = (bf16[32,2,2304]{2,1,0:T(2,128)(2,1)}, bf16[32,2,2304]{2,1,0:T(2,128)(2,1)S(1)}, u32[]{:S(2)}) copy-start(bf16[32,2,2304]{2,1,0:T(2,128)(2,1)S(1)} %all_to_all.10.side_ref) | copy-start | bytes 884740
  56.1 11.9 %collective-permute-start = (bf16[32,2,2304]{2,1,0:T(2,128)(2,1)S(1)}, bf16[32,2,2304]{2,1,0:T(2,128)(2,1)S(1)}, u32[]{:S(2)}, u32[]{:S(2)}) collective-permute-start(bf16[32,2,2304]{2,1,0:T(2,128)(2,1)S(1)} %all_to_all.10.side_ref), channel_id=1, source_target_pairs={{0,4},{4,0},{8,12},{12,8},{16,20},{20,16},{24,28},{28,24},{32,36},... | collective-permute-start | bytes 884744 | tf_op jit(solution)/shard_map/ppermute | solution.py:169
  68.0 0.7 copy-start.3

commit v3 on v2

v3 whole, which is shorter than its diff:
```python
import jax
import jax.numpy as jnp
import numpy as np
from jax import lax
from jax.experimental import pallas as pl
from jax.experimental.pallas import tpu as pltpu
from jax.sharding import PartitionSpec as P

BINS = 256
LEAVES = 32
POS = 128
HALF = BINS // 2
TILE = 256
STEP = 4


def query_rows(scores, clicks, lengths_ref, queries, discount_row):
    lane = lax.broadcasted_iota(jnp.int32, (queries, POS), 1)
    row = lax.broadcasted_iota(jnp.int32, (queries, POS), 0)
    length = jnp.zeros((queries, POS), jnp.int32)
    for query in range(queries):
        length = jnp.where(row == query, lengths_ref[query], length)
    shown = lane < length
    clicked = shown & (clicks == 1)
    skipped = shown & (clicks == 0)
    count = jnp.sum(jnp.where(clicked, 1.0, 0.0), axis=1, keepdims=True)
    ideal = jnp.sum(
        jnp.where(lane.astype(jnp.float32) < count, discount_row, 0.0), axis=1, keepdims=True
    )
    ideal = jnp.maximum(ideal, 1.0)
    side = jnp.where(clicked, 1.0, jnp.where(skipped, -1.0, 0.0))
    return clicked, skipped, side, side * scores, ideal


def turned(rows):
    queries = rows[0].shape[0]
    pad = jnp.zeros((POS - queries * len(rows), POS), jnp.float32)
    return jnp.transpose(jnp.concatenate(list(rows) + [pad], axis=0))


def pair_kernel(gap_ref, discount_ref, scores_ref, clicks_ref, lengths_ref, plus_ref, minus_ref, bins_ref, parts_ref,
                bins_out_ref, packed):
    queries = scores_ref.shape[0]
    discount_row = discount_ref[...]
    clicked, skipped, side, signed, ideal = query_rows(
        scores_ref[...], clicks_ref[...], lengths_ref, queries, discount_row
    )
    weight = jnp.where(clicked, 1.0 / plus_ref[...], jnp.where(skipped, -1.0 / minus_ref[...], 0.0))
    columns = turned([signed, weight])
    scale = 1.0 / ideal
    plus = jnp.zeros((1, POS), jnp.float32)
    minus = jnp.zeros((1, POS), jnp.float32)
    for query in range(queries):
        other = columns[:, query : query + 1]
        strength = columns[:, queries + query : queries + query + 1]
        spread = other + signed[query : query + 1]
        cross = jnp.maximum(strength * -side[query : query + 1], 0.0)
        loss = jnp.maximum(-spread, 0.0) + jnp.log1p(jnp.exp(-jnp.abs(spread)))
        total = jnp.sum(cross * gap_ref[...] * loss, axis=0, keepdims=True)
        total = total * scale[query : query + 1]
        plus += jnp.where(side[query : query + 1] > 0.0, total, 0.0)
        minus += jnp.where(side[query : query + 1] < 0.0, total, 0.0)
    parts_ref[0:1] = plus
    parts_ref[1:2] = minus

    features, slots = bins_ref.shape
    packed[...] = jnp.full(packed.shape, -1.0, jnp.float32)
    lane = lax.broadcasted_iota(jnp.int32, (1, POS), 1)
    start = jnp.int32(0)
    for query in range(queries):
        group = start // POS
        shift = start - group * POS
        length = lengths_ref[query]
        moved = pltpu.roll(
            bins_ref[:, query * POS : (query + 1) * POS].astype(jnp.float32), shift, 1
        )
        here = (lane >= shift) & (lane < shift + length)
        there = lane < shift + length - POS
        packed[group] = jnp.where(here, moved, packed[group])
        packed[group + 1] = jnp.where(there, moved, packed[group + 1])
        start += length
    for group in range(slots // POS):
        bins_out_ref[:, group * POS : (group + 1) * POS] = packed[group].astype(jnp.bfloat16)


def lambda_kernel(gap_ref, discount_ref, scores_ref, clicks_ref, lengths_ref, leaf_ref, sums_ref, plus_ref, minus_ref,
                  grad_ref, side_ref, packed, flat):
    queries = scores_ref.shape[0]
    discount_row = discount_ref[...]
    plus_sum = sums_ref[:, :POS]
    minus_sum = sums_ref[:, POS:]
    plus = jnp.sqrt(plus_sum / plus_sum[:, 0:1])
    minus = jnp.sqrt(minus_sum / minus_sum[:, 0:1])
    plus_ref[...] = plus
    minus_ref[...] = minus
    clicked, skipped, side, signed, ideal = query_rows(
        scores_ref[...], clicks_ref[...], lengths_ref, queries, discount_row
    )
    weight = jnp.where(clicked, 1.0 / plus, jnp.where(skipped, -1.0 / minus, 0.0))
    columns = turned([signed, weight])
    outer = jnp.abs(weight) / ideal
    packed[...] = jnp.zeros_like(packed)
    lane = lax.broadcasted_iota(jnp.int32, (1, POS), 1)
    start = jnp.int32(0)
    for query in range(queries):
        other = columns[:, query : query + 1]
        strength = columns[:, queries + query : queries + query + 1]
        spread = other + signed[query : query + 1]
        cross = jnp.maximum(strength * -side[query : query + 1], 0.0)
        grown = jnp.exp(spread)
        chance = 1.0 / (1.0 + grown)
        first = cross * gap_ref[...] * chance
        second = first * (grown * chance)
        slope = jnp.sum(first, axis=0, keepdims=True) * outer[query : query + 1]
        slope = slope * -side[query : query + 1]
        curve = jnp.sum(second, axis=0, keepdims=True) * outer[query : query + 1]
        grad_ref[0:1, query * POS : (query + 1) * POS] = slope
        grad_ref[1:2, query * POS : (query + 1) * POS] = curve
        group = start // POS
        shift = start - group * POS
        length = lengths_ref[query]
        rows = jnp.concatenate(
            [slope, curve, leaf_ref[query : query + 1].astype(jnp.float32),
             jnp.zeros((5, POS), jnp.float32)], axis=0
        )
        moved = pltpu.roll(rows, shift, 1)
        here = (lane >= shift) & (lane < shift + length)
        there = lane < shift + length - POS
        packed[group] = jnp.where(here, moved, packed[group])
        packed[group + 1] = jnp.where(there, moved, packed[group + 1])
        start += length
    for tile in range(queries * POS // TILE):
        at = 3 * POS * tile
        for half in range(2):
            rows = packed[2 * tile + half]
            flat[:, at + half * POS : at + (half + 1) * POS] = rows[0:2]
            flat[half : half + 1, at + 2 * POS : at + 3 * POS] = rows[2:3]
    side_ref[...] = flat[...].astype(jnp.bfloat16)


def plan_kernel(filled_ref, list_ref, total_ref):
    chips = filled_ref.shape[0] // 2
    tiles = (list_ref.shape[0] // 2 - STEP) // chips
    for core in range(2):
        base = core * (chips * tiles + STEP)

        def one_block(chip, carry):
            at, spare = carry
            used = filled_ref[2 * chip + core]
            for tile in range(tiles):
                list_ref[base + at] = chip * 8 + tile
                at = at + jnp.where(tile < used, 1, 0)
            return at, jnp.where(used < tiles, chip * 8 + tiles - 1, spare)

        at, spare = lax.fori_loop(0, chips, one_block, (jnp.int32(0), jnp.int32(0)))
        for extra in range(STEP):
            list_ref[base + at + extra] = spare
        total_ref[core] = (at + STEP - 1) // STEP


def accumulate(core, list_ref, total_ref, data_ref, side_ref, acc):
    base = core * (list_ref.shape[0] // 2)
    rows_a = lax.broadcasted_iota(jnp.int32, (2 * LEAVES, TILE), 0).astype(jnp.bfloat16)
    rows_b = lax.broadcasted_iota(jnp.int32, (HALF, TILE), 0).astype(jnp.bfloat16)
    zero = jnp.zeros((), jnp.bfloat16)
    one = jnp.ones((), jnp.bfloat16)

    def some_tiles(step, carry):
        left = [[], []]
        right = [[], []]
        for at in range(STEP):
            entry = list_ref[base + step * STEP + at]
            chip = entry // 8
            tile = entry - chip * 8
            bins = data_ref[2 * chip + core, :, pl.ds(pl.multiple_of(tile * TILE, TILE), TILE)]
            side = side_ref[chip, :, pl.ds(pl.multiple_of(tile * 3 * POS, POS), 3 * POS)]
            leaf = jnp.concatenate([side[0:1, TILE:], side[1:2, TILE:]], axis=1)
            for feature in range(2):
                row = bins[feature : feature + 1]
                high = row >= jnp.asarray(HALF, jnp.bfloat16)
                hit = jnp.where(high, leaf + jnp.asarray(LEAVES, jnp.bfloat16), leaf) == rows_a
                low = jnp.where(high, row - jnp.asarray(HALF, jnp.bfloat16), row)
                left[feature].append(
                    jnp.concatenate(
                        [
                            jnp.where(hit, side[0:1, :TILE], zero),
                            jnp.where(hit, side[1:2, :TILE], zero),
                        ],
                        axis=0,
                    )
                )
                right[feature].append(jnp.where(low == rows_b, one, zero))
        for feature in range(2):
            acc[feature] += lax.dot_general(
                jnp.concatenate(left[feature], axis=1),
                jnp.concatenate(right[feature], axis=1),
                (((1,), (1,)), ((), ())),
                preferred_element_type=jnp.float32,
            )
        return carry

    lax.fori_loop(0, total_ref[core], some_tiles, 0)


def first_kernel(core_ref, list_ref, total_ref, data_ref, side_ref, out_ref):
    out_ref[...] = jnp.zeros_like(out_ref)
    accumulate(core_ref[0], list_ref, total_ref, data_ref, side_ref, out_ref)


def second_kernel(core_ref, list_ref, total_ref, data_ref, side_ref, before_ref, out_ref, acc):
    acc[...] = before_ref[...]
    accumulate(core_ref[0], list_ref, total_ref, data_ref, side_ref, acc)
    for feature in range(2):
        for which in range(2):
            for high in range(2):
                out_ref[
                    feature,
                    which * LEAVES : (which + 1) * LEAVES,
                    high * HALF : (high + 1) * HALF,
                ] = acc[feature, (2 * which + high) * LEAVES : (2 * which + high + 1) * LEAVES, :]


VMEM = pl.BlockSpec(memory_space=pltpu.VMEM)
SMEM = pl.BlockSpec(memory_space=pltpu.SMEM)


def hist_of(core, plan, data, side, before=None):
    part = (2, 4 * LEAVES, HALF)
    if before is None:
        return pl.pallas_call(
            first_kernel,
            out_shape=jax.ShapeDtypeStruct(part, jnp.float32),
            in_specs=[SMEM, SMEM, SMEM, VMEM, VMEM],
            out_specs=VMEM,
            name="first_half",
        )(core, *plan, data, side)
    return pl.pallas_call(
        second_kernel,
        out_shape=jax.ShapeDtypeStruct((2, 2 * LEAVES, BINS), jnp.float32),
        in_specs=[SMEM, SMEM, SMEM, VMEM, VMEM, VMEM],
        out_specs=VMEM,
        scratch_shapes=[pltpu.VMEM(part, jnp.float32)],
        name="second_half",
    )(core, *plan, data, side, before)


def body(scores, clicks, lengths, t_plus_old, t_minus_old, leaf, bins):
    shards = lax.axis_size("doc")
    queries = scores.shape[0]
    slots = leaf.shape[0]
    tiles = slots // TILE
    places = np.arange(POS, dtype=np.float32)
    discount = (1.0 / np.log2(2.0 + places)).astype(np.float32)
    gap = jnp.asarray(np.abs(discount[:, None] - discount[None, :]))
    discount = jnp.asarray(discount[None])
    f32 = jnp.float32
    parts, packed = pl.pallas_call(
        pair_kernel,
        out_shape=(
            jax.ShapeDtypeStruct((2, POS), f32),
            jax.ShapeDtypeStruct(bins.shape, jnp.bfloat16),
        ),
        in_specs=[VMEM, VMEM, VMEM, VMEM, SMEM, VMEM, VMEM, VMEM],
        out_specs=(VMEM, VMEM),
        scratch_shapes=[pltpu.VMEM((slots // POS + 1, bins.shape[0], POS), f32)],
        name="pair_terms",
    )(gap, discount, scores, clicks, lengths, t_plus_old[None], t_minus_old[None], bins)
    parts = parts.reshape(2 * POS)
    parts_high = parts.astype(jnp.bfloat16)
    parts_rest = (parts - parts_high.astype(f32)).astype(jnp.bfloat16)
    parts = jnp.stack([parts_high, parts_rest])
    sent = jnp.concatenate(
        [
            packed.reshape(shards, 2, slots),
            jnp.broadcast_to(parts[None], (shards,) + parts.shape),
        ],
        axis=2,
    )
    data = lax.all_to_all(sent, "doc", 0, 0, tiled=True)
    sums = jnp.sum(data[:, :, slots:].astype(f32), axis=(0, 1))
    t_plus, t_minus, gradients, side = pl.pallas_call(
        lambda_kernel,
        out_shape=(
            jax.ShapeDtypeStruct((1, POS), f32),
            jax.ShapeDtypeStruct((1, POS), f32),
            jax.ShapeDtypeStruct((2, slots), f32),
            jax.ShapeDtypeStruct((2, 3 * slots // 2), jnp.bfloat16),
        ),
        in_specs=[VMEM, VMEM, VMEM, VMEM, SMEM, VMEM, VMEM],
        out_specs=(VMEM,) * 4,
        scratch_shapes=[
            pltpu.VMEM((queries + 1, 8, POS), f32),
            pltpu.VMEM((2, 3 * slots // 2), f32),
        ],
        name="lambdas",
    )(gap, discount, scores, clicks, lengths, leaf.reshape(queries, POS), sums[None])
    same_core = [[2 * chip + core for chip in range(shards // 2)] for core in range(2)]
    side = lax.all_to_all(
        jnp.broadcast_to(side[None], (shards // 2,) + side.shape),
        "doc",
        0,
        0,
        axis_index_groups=same_core,
        tiled=True,
    )
    shown = jnp.sum((data[:, 0, :slots] >= 0).astype(f32), axis=1).astype(jnp.int32)
    plan = pl.pallas_call(
        plan_kernel,
        out_shape=(
            jax.ShapeDtypeStruct((shards * tiles + 2 * STEP,), jnp.int32),
            jax.ShapeDtypeStruct((2,), jnp.int32),
        ),
        in_specs=[SMEM],
        out_specs=(SMEM, SMEM),
        name="plan",
    )((shown + (TILE - 1)) // TILE)
    other_side = lax.ppermute(side, "doc", [(at, at ^ 1) for at in range(shards)])
    core = lax.axis_index("doc") % 2
    partial = hist_of(core.reshape(1), plan, data, side)
    hist = hist_of((1 - core).reshape(1), plan, data, other_side, partial)
    return (t_plus[0], t_minus[0], gradients, hist)


def solution(mesh):
    placed = (P("doc", None), P("doc", None), P("doc"), P(), P(), P("doc"), P("feat", "doc"))
    return jax.shard_map(
        body,
        mesh=mesh,
        in_specs=placed,
        out_specs=(P(), P(), P(None, "doc"), P(("feat", "doc"), None, None)),
        check_vma=False,
    )
```

time: 78.9 us -> 89 us (1.13)
  Pallas kernels: 19.6 us -> 33.4 us
  blocking collectives: 16.3 us -> 29.3 us
  starting transfers between devices: 15.5 us -> 6.62 us
  other arithmetic: 7.26 us -> 2.48 us
  waiting for transfers between devices: 16.3 us -> 12.1 us
  local copies, waits for them, and re-layouts: 2.79 us -> 4.13 us
    all_to_all x1, blocking collectives: 16.3 us -> 29.3 us  [body(): data = lax.all_to_all(sent, 'doc', 0, 0, tiled=True)]
    all_to_all x1, starting transfers between devices: 13.3 us -> 4.45 us  [body(): lax.all_to_all(jnp.broadcast_to(side[None], (shards // 2,) + side.shape),...]
    pallas_call x0 -> x3, Pallas kernels: none -> 8.13 us  [the longest x1 3.08 us: body(): pl.pallas_call(pair_kernel, out_shape=(jax.ShapeDtypeStruct((2, POS), f32...]
    all_to_all x1, waiting for transfers between devices: 16.3 us -> 12.1 us  [body(): lax.all_to_all(jnp.broadcast_to(side[None], (shards // 2,) + side.shape),...]
    pallas_call x1, Pallas kernels: 9.76 us -> 12.9 us  [hist_of(): pl.pallas_call(first_kernel, out_shape=jax.ShapeDtypeStruct(part, jnp.flo...]
    pallas_call x1, Pallas kernels: 9.8 us -> 12.3 us  [hist_of(): pl.pallas_call(second_kernel, out_shape=jax.ShapeDtypeStruct((2, 2 * LEAV...]
    reduce_sum x5 -> x2, other arithmetic: 3.89 us -> 1.47 us  [the longest x1 0.75 us: body(): jnp.sum((data[:, 0, :slots] >= 0).astype(f32), axis=1).astype(jnp.int32)]
    broadcast_in_dim x1, local copies, waits for them, and re-layouts: 0.16 us -> 1.56 us  [body(): jnp.broadcast_to(side[None], (shards // 2,) + side.shape)]
  transfers between devices with their start and end apart: 2 -> 2, of which waited for: 1 -> 1; matrix products, arithmetic and copies ran while one was open for 0% -> 2% of each run, Pallas kernels for 12% -> 17%
where the time goes in v3:
time: 89 us; the launch traced here: 88.7 us
  Pallas kernels  33.4 us (38%)
  blocking collectives  29.3 us (33%)
  waiting for transfers between devices  12.1 us (14%)
  starting transfers between devices  6.62 us (7%)
  local copies, waits for them, and re-layouts  4.13 us (5%)
  other arithmetic  2.48 us (3%)
    all_to_all x1, blocking collectives, body(): data = lax.all_to_all(sent, 'doc', 0, 0, tiled=True)  29.3 us
    pallas_call x1, Pallas kernels, hist_of(): pl.pallas_call(first_kernel, out_shape=jax.ShapeDtypeStruct(part, jnp.flo...  12.9 us
    pallas_call x1, Pallas kernels, hist_of(): pl.pallas_call(second_kernel, out_shape=jax.ShapeDtypeStruct((2, 2 * LEAV...  12.3 us
    all_to_all x1, waiting for transfers between devices, body(): lax.all_to_all(jnp.broadcast_to(side[None], (shards // 2,) + side.shape),...  12.1 us
    all_to_all x1, starting transfers between devices, body(): lax.all_to_all(jnp.broadcast_to(side[None], (shards // 2,) + side.shape),...  4.45 us
    pallas_call x1, Pallas kernels, body(): pl.pallas_call(pair_kernel, out_shape=(jax.ShapeDtypeStruct((2, POS), f32...  3.08 us
    pallas_call x1, Pallas kernels, body(): pl.pallas_call(lambda_kernel, out_shape=(jax.ShapeDtypeStruct((1, POS), f...  2.77 us
    pallas_call x1, Pallas kernels, body(): pl.pallas_call(plan_kernel, out_shape=(jax.ShapeDtypeStruct((shards * til...  2.27 us
  transfers between devices with their start and end apart: 2, of which 1 were waited for; matrix products, arithmetic and copies ran while one was open for 2% of the time, Pallas kernels for 17%

profile of v3, /device:TPU:1, one launch (start us, length us, event | category | flops | bytes accessed | tf_op | source)
XLA Modules:
  0.0 88.7 jit_solution(5874505430342632742)
XLA Ops:
  0.6 3.1 %pair_terms.1 = (f32[2,128]{1,0:T(2,128)}, bf16[128,1536]{1,0:T(8,128)(2,1)}) custom-call(f32[128,128]{1,0:T(8,128)} %constant.43.clone.gap_ref, f32[1,128]{1,0:T(1,128)} %constant.44.clone.discount_ref, f32[12,128]{1,0:T(8,128)} %scores_ref.3, s32[12,128]{1,0:T(8,128)} %clicks_ref.3, s32[12]{0:T(128)} %lengths_ref.3, f32[1,128]{1,0:T(1,128)} %bitcast.13, ...), custom_call_target="tpu_custom_call" | custom-call | tf_op jit(solution)/shard_map/pair_terms/pallas_call | solution.py:257
  3.7 0.0 copy-start.3
  3.7 0.7 copy-done.3
  4.4 1.1 %reshape.58 = bf16[64,2,1536]{2,1,0:T(2,128)(2,1)S(1)} reshape(bf16[128,1536]{1,0:T(8,128)(2,1)} %get-tuple-element.12) | data formatting | bytes 786432 | tf_op jit(solution)/shard_map/reshape | solution.py:274
  5.6 0.4 pad_maximum_fusion
  6.0 29.3 %all_to_all.10.data_ref = bf16[64,2,1792]{2,1,0:T(2,128)(2,1)S(1)} all-to-all(bf16[64,2,1792]{2,1,0:T(2,128)(2,1)S(1)} %pad_maximum_fusion), channel_id=1, replica_groups=mesh['doc'=64,'feat'=4] {'doc'}, dimensions={0} | all-to-all | bytes 917504 | tf_op jit(solution)/shard_map/all_to_all | solution.py:279
  35.3 0.0 copy-start
  35.3 0.7 convert_reduce_fusion
  36.1 2.8 %lambdas.1 = (f32[1,128]{1,0:T(1,128)}, f32[1,128]{1,0:T(1,128)}, f32[2,1536]{1,0:T(2,128)}, bf16[2,2304]{1,0:T(2,128)(2,1)}) custom-call(f32[128,128]{1,0:T(8,128)} %constant.43.clone.gap_ref, f32[1,128]{1,0:T(1,128)} %constant.44.clone.discount_ref, f32[12,128]{1,0:T(8,128)} %scores_ref.3, s32[12,128]{1,0:T(8,128)} %clicks_ref.3, s32[12]{0:T(128)} %lengths_ref.3, ...), custom_call_target="tpu_custom_call" | custom-call | tf_op jit(solution)/shard_map/lambdas/pallas_call | solution.py:281
  38.8 1.6 %broadcast_in_dim.25 = bf16[32,2,2304]{2,1,0:T(2,128)(2,1)} broadcast(bf16[2,2304]{1,0:T(2,128)(2,1)} %get-tuple-element.19), dimensions={1,2} | broadcast | bytes 304128 | tf_op jit(solution)/shard_map/broadcast_in_dim | solution.py:299
  40.4 4.4 %all-to-all-start.1 = ((bf16[32,2,2304]{2,1,0:T(2,128)(2,1)}), bf16[32,2,2304]{2,1,0:T(2,128)(2,1)S(1)}, u32[]{:S(2)}, u32[]{:S(2)}) async-start(bf16[32,2,2304]{2,1,0:T(2,128)(2,1)} %broadcast_in_dim.25), calls=%async_computation.1 | async-start | bytes 589824 | tf_op jit(solution)/shard_map/all_to_all | solution.py:298
  44.9 12.1 %all-to-all-done.1.side_ref = bf16[32,2,2304]{2,1,0:T(2,128)(2,1)S(1)} async-done(((bf16[32,2,2304]{2,1,0:T(2,128)(2,1)}), bf16[32,2,2304]{2,1,0:T(2,128)(2,1)S(1)}, u32[]{:S(2)}, u32[]{:S(2)}) %all-to-all-start.1) | async-done | bytes 294944 | tf_op jit(solution)/shard_map/all_to_all | solution.py:298
  56.9 0.0 copy-start.1
  56.9 2.2 %collective-permute-start = (bf16[32,2,2304]{2,1,0:T(2,128)(2,1)S(1)}, bf16[32,2,2304]{2,1,0:T(2,128)(2,1)S(1)}, u32[]{:S(2)}, u32[]{:S(2)}) collective-permute-start(bf16[32,2,2304]{2,1,0:T(2,128)(2,1)S(1)} %all-to-all-done.1.side_ref), channel_id=1, source_target_pairs={{0,4},{4,0},{8,12},{12,8},{16,20},{20,16},{24,28},{28,24},{32,36},... | collective-permute-start | bytes 884744 | tf_op jit(solution)/shard_map/ppermute | solution.py:317
  59.1 0.0 copy-done
  59.1 0.7 fusion
  59.8 0.6 and_select_fusion.filled_ref
  60.4 2.3 %plan.1 = (s32[392]{0:T(512)}, s32[2]{0:T(128)}) custom-call(s32[64]{0:T(128)} %and_select_fusion.filled_ref), custom_call_target="tpu_custom_call" | custom-call | tf_op jit(solution)/shard_map/plan/pallas_call | solution.py:307
  62.7 0.0 copy-done.1
  62.7 12.9 %first_half.1.before_ref = f32[2,128,128]{2,1,0:T(8,128)} custom-call(s32[1]{0:T(128)} %bitcast.8.core_ref, s32[392]{0:T(512)} %get-tuple-element.17.list_ref, s32[2]{0:T(128)} %get-tuple-element.18.total_ref, bf16[64,2,1792]{2,1,0:T(2,128)(2,1)} %copy-done, bf16[32,2,2304]{2,1,0:T(2,128)(2,1)} %copy-done.1), custom_call_target="tpu_custom_call" | custom-call | tf_op jit(solution)/shard_map/first_half/pallas_call | solution.py:230
  75.7 0.0 collective-permute-done.side_ref
  75.7 0.0 copy-start.2
  75.7 0.7 copy-done.2
  76.4 12.3 %second_half.1 = f32[2,64,256]{2,1,0:T(8,128)} custom-call(s32[1]{0:T(128)} %bitcast.7.core_ref, s32[392]{0:T(512)} %get-tuple-element.17.list_ref, s32[2]{0:T(128)} %get-tuple-element.18.total_ref, bf16[64,2,1792]{2,1,0:T(2,128)(2,1)} %copy-done, bf16[32,2,2304]{2,1,0:T(2,128)(2,1)} %copy-done.2, f32[2,128,128]{2,1,0:T(8,128)} %first_half.1.before_ref), custom_call_target="tpu_custom_call" | custom-call | tf_op jit(solution)/shard_map/second_half/pallas_call | solution.py:237
  (4 shorter events, 0.1 us)
Async XLA Ops:
  3.7 0.7 copy-start.3
  35.3 23.8 %copy-start = (bf16[64,2,1792]{2,1,0:T(2,128)(2,1)}, bf16[64,2,1792]{2,1,0:T(2,128)(2,1)S(1)}, u32[]{:S(2)}) copy-start(bf16[64,2,1792]{2,1,0:T(2,128)(2,1)S(1)} %all_to_all.10.data_ref) | copy-start | bytes 1376260
  40.4 16.5 %all-to-all-start.1 = ((bf16[32,2,2304]{2,1,0:T(2,128)(2,1)}), bf16[32,2,2304]{2,1,0:T(2,128)(2,1)S(1)}, u32[]{:S(2)}, u32[]{:S(2)}) async-start(bf16[32,2,2304]{2,1,0:T(2,128)(2,1)} %broadcast_in_dim.25), calls=%async_computation.1 | async-start | bytes 589824 | tf_op jit(solution)/shard_map/all_to_all | solution.py:298
  56.9 5.8 %copy-start.1 = (bf16[32,2,2304]{2,1,0:T(2,128)(2,1)}, bf16[32,2,2304]{2,1,0:T(2,128)(2,1)S(1)}, u32[]{:S(2)}) copy-start(bf16[32,2,2304]{2,1,0:T(2,128)(2,1)S(1)} %all-to-all-done.1.side_ref) | copy-start | bytes 884740
  56.9 18.7 %collective-permute-start = (bf16[32,2,2304]{2,1,0:T(2,128)(2,1)S(1)}, bf16[32,2,2304]{2,1,0:T(2,128)(2,1)S(1)}, u32[]{:S(2)}, u32[]{:S(2)}) collective-permute-start(bf16[32,2,2304]{2,1,0:T(2,128)(2,1)S(1)} %all-to-all-done.1.side_ref), channel_id=1, source_target_pairs={{0,4},{4,0},{8,12},{12,8},{16,20},{20,16},{24,28},{28,24},{32,36},... | collective-permute-start | bytes 884744 | tf_op jit(solution)/shard_map/ppermute | solution.py:317
  75.7 0.7 copy-start.2

commit v4 on v3

--- a/solution.py
+++ b/solution.py
@@ -6,12 +6,13 @@
 from jax.experimental.pallas import tpu as pltpu
 from jax.sharding import PartitionSpec as P
 
+
 BINS = 256
 LEAVES = 32
 POS = 128
 HALF = BINS // 2
 TILE = 256
-STEP = 4
+STEP = 8
 
 
 def query_rows(scores, clicks, lengths_ref, queries, discount_row):
@@ -38,8 +39,8 @@
     return jnp.transpose(jnp.concatenate(list(rows) + [pad], axis=0))
 
 
-def pair_kernel(gap_ref, discount_ref, scores_ref, clicks_ref, lengths_ref, plus_ref, minus_ref, bins_ref, parts_ref,
-                bins_out_ref, packed):
+def pair_kernel(gap_ref, discount_ref, scores_ref, clicks_ref, lengths_ref, plus_ref, minus_ref, bins_ref,
+                sent_ref, packed):
     queries = scores_ref.shape[0]
     discount_row = discount_ref[...]
     clicked, skipped, side, signed, ideal = query_rows(
@@ -60,10 +61,13 @@
         total = total * scale[query : query + 1]
         plus += jnp.where(side[query : query + 1] > 0.0, total, 0.0)
         minus += jnp.where(side[query : query + 1] < 0.0, total, 0.0)
-    parts_ref[0:1] = plus
-    parts_ref[1:2] = minus
-
     features, slots = bins_ref.shape
+    for at, part in enumerate((plus, minus)):
+        high = part.astype(jnp.bfloat16).astype(jnp.float32)
+        pieces = jnp.concatenate([high, part - high], axis=0).astype(jnp.bfloat16)
+        sent_ref[:, :, slots + at * POS : slots + (at + 1) * POS] = jnp.broadcast_to(
+            pieces[None], (features // 2, 2, POS)
+        )
     packed[...] = jnp.full(packed.shape, -1.0, jnp.float32)
     lane = lax.broadcasted_iota(jnp.int32, (1, POS), 1)
     start = jnp.int32(0)
@@ -80,7 +84,10 @@
         packed[group + 1] = jnp.where(there, moved, packed[group + 1])
         start += length
     for group in range(slots // POS):
-        bins_out_ref[:, group * POS : (group + 1) * POS] = packed[group].astype(jnp.bfloat16)
+        for owner in range(features // 2):
+            sent_ref[owner, :, group * POS : (group + 1) * POS] = packed[
+                group, 2 * owner : 2 * owner + 2
+            ].astype(jnp.bfloat16)
 
 
 def lambda_kernel(gap_ref, discount_ref, scores_ref, clicks_ref, lengths_ref, leaf_ref, sums_ref, plus_ref, minus_ref,
@@ -135,7 +142,7 @@
             rows = packed[2 * tile + half]
             flat[:, at + half * POS : at + (half + 1) * POS] = rows[0:2]
             flat[half : half + 1, at + 2 * POS : at + 3 * POS] = rows[2:3]
-    side_ref[...] = flat[...].astype(jnp.bfloat16)
+    side_ref[...] = jnp.broadcast_to(flat[...].astype(jnp.bfloat16)[None], side_ref.shape)
 
 
 def plan_kernel(filled_ref, list_ref, total_ref):
@@ -158,7 +165,7 @@
         total_ref[core] = (at + STEP - 1) // STEP
 
 
-def accumulate(core, list_ref, total_ref, data_ref, side_ref, acc):
+def accumulate(core, list_ref, total_ref, data_ref, side_ref, accs):
     base = core * (list_ref.shape[0] // 2)
     rows_a = lax.broadcasted_iota(jnp.int32, (2 * LEAVES, TILE), 0).astype(jnp.bfloat16)
     rows_b = lax.broadcasted_iota(jnp.int32, (HALF, TILE), 0).astype(jnp.bfloat16)
@@ -166,58 +173,71 @@
     one = jnp.ones((), jnp.bfloat16)
 
     def some_tiles(step, carry):
-        left = [[], []]
-        right = [[], []]
         for at in range(STEP):
             entry = list_ref[base + step * STEP + at]
-            chip = entry // 8
-            tile = entry - chip * 8
+            chip = lax.shift_right_logical(entry, 3)
+            tile = lax.bitwise_and(entry, 7)
             bins = data_ref[2 * chip + core, :, pl.ds(pl.multiple_of(tile * TILE, TILE), TILE)]
             side = side_ref[chip, :, pl.ds(pl.multiple_of(tile * 3 * POS, POS), 3 * POS)]
             leaf = jnp.concatenate([side[0:1, TILE:], side[1:2, TILE:]], axis=1)
+            left = []
+            right = []
             for feature in range(2):
                 row = bins[feature : feature + 1]
                 high = row >= jnp.asarray(HALF, jnp.bfloat16)
                 hit = jnp.where(high, leaf + jnp.asarray(LEAVES, jnp.bfloat16), leaf) == rows_a
                 low = jnp.where(high, row - jnp.asarray(HALF, jnp.bfloat16), row)
-                left[feature].append(
-                    jnp.concatenate(
-                        [
-                            jnp.where(hit, side[0:1, :TILE], zero),
-                            jnp.where(hit, side[1:2, :TILE], zero),
-                        ],
-                        axis=0,
-                    )
-                )
-                right[feature].append(jnp.where(low == rows_b, one, zero))
+                left.append(jnp.where(hit, side[0:1, :TILE], zero))
+                left.append(jnp.where(hit, side[1:2, :TILE], zero))
+                right.append(jnp.where(low == rows_b, one, zero))
+            unit = at % 2
+            register = (at // 2) % 2
+            pltpu.matmul_push_rhs(jnp.concatenate(right, axis=0), register, unit, transpose=True)
+            pltpu.matmul_acc_lhs(accs[unit], jnp.concatenate(left, axis=0), register)
+        return carry
+
+    lax.fori_loop(0, total_ref[core], some_tiles, 0)
+
+
+def summed(core, list_ref, total_ref, data_ref, side_ref, finish):
+    def run(acc_a, acc_b):
+        accumulate(core, list_ref, total_ref, data_ref, side_ref, (acc_a, acc_b))
+        finish(pltpu.matmul_pop(acc_a) + pltpu.matmul_pop(acc_b))
+
+    shape = (8 * LEAVES, BINS)
+    pl.run_scoped(run, pltpu.ACC(0)(shape, jnp.float32), pltpu.ACC(1)(shape, jnp.float32))
+
+
+def first_kernel(core_ref, list_ref, total_ref, data_ref, side_ref, out_ref):
+    rows = 4 * LEAVES
+
+    def finish(total):
         for feature in range(2):
-            acc[feature] += lax.dot_general(
-                jnp.concatenate(left[feature], axis=1),
-                jnp.concatenate(right[feature], axis=1),
-                (((1,), (1,)), ((), ())),
-                preferred_element_type=jnp.float32,
-            )
-        return carry
-
-    lax.fori_loop(0, total_ref[core], some_tiles, 0)
-
-
-def first_kernel(core_ref, list_ref, total_ref, data_ref, side_ref, out_ref):
-    out_ref[...] = jnp.zeros_like(out_ref)
-    accumulate(core_ref[0], list_ref, total_ref, data_ref, side_ref, out_ref)
-
-
-def second_kernel(core_ref, list_ref, total_ref, data_ref, side_ref, before_ref, out_ref, acc):
-    acc[...] = before_ref[...]
-    accumulate(core_ref[0], list_ref, total_ref, data_ref, side_ref, acc)
-    for feature in range(2):
-        for which in range(2):
-            for high in range(2):
-                out_ref[
-                    feature,
-                    which * LEAVES : (which + 1) * LEAVES,
-                    high * HALF : (high + 1) * HALF,
-                ] = acc[feature, (2 * which + high) * LEAVES : (2 * which + high + 1) * LEAVES, :]
+            out_ref[feature] = total[
+                feature * rows : (feature + 1) * rows, feature * HALF : (feature + 1) * HALF
+            ]
+
+    summed(core_ref[0], list_ref, total_ref, data_ref, side_ref, finish)
+
+
+def second_kernel(core_ref, list_ref, total_ref, data_ref, side_ref, before_ref, out_ref):
+    rows = 4 * LEAVES
+
+    def finish(total):
+        for feature in range(2):
+            mine = total[
+                feature * rows : (feature + 1) * rows, feature * HALF : (feature + 1) * HALF
+            ] + before_ref[feature]
+            for which in range(2):
+                for high in range(2):
+                    at = (2 * which + high) * LEAVES
+                    out_ref[
+                        feature,
+                        which * LEAVES : (which + 1) * LEAVES,
+                        high * HALF : (high + 1) * HALF,
+                    ] = mine[at : at + LEAVES]
+
+    summed(core_ref[0], list_ref, total_ref, data_ref, side_ref, finish)
 
 
 VMEM = pl.BlockSpec(memory_space=pltpu.VMEM)
@@ -239,7 +259,6 @@
         out_shape=jax.ShapeDtypeStruct((2, 2 * LEAVES, BINS), jnp.float32),
         in_specs=[SMEM, SMEM, SMEM, VMEM, VMEM, VMEM],
         out_specs=VMEM,
-        scratch_shapes=[pltpu.VMEM(part, jnp.float32)],
         name="second_half",
     )(core, *plan, data, side, before)
 
@@ -254,28 +273,14 @@
     gap = jnp.asarray(np.abs(discount[:, None] - discount[None, :]))
     discount = jnp.asarray(discount[None])
     f32 = jnp.float32
-    parts, packed = pl.pallas_call(
+    sent = pl.pallas_call(
         pair_kernel,
-        out_shape=(
-            jax.ShapeDtypeStruct((2, POS), f32),
-            jax.ShapeDtypeStruct(bins.shape, jnp.bfloat16),
-        ),
+        out_shape=jax.ShapeDtypeStruct((shards, 2, slots + 2 * POS), jnp.bfloat16),
         in_specs=[VMEM, VMEM, VMEM, VMEM, SMEM, VMEM, VMEM, VMEM],
-        out_specs=(VMEM, VMEM),
+        out_specs=VMEM,
         scratch_shapes=[pltpu.VMEM((slots // POS + 1, bins.shape[0], POS), f32)],
         name="pair_terms",
     )(gap, discount, scores, clicks, lengths, t_plus_old[None], t_minus_old[None], bins)
-    parts = parts.reshape(2 * POS)
-    parts_high = parts.astype(jnp.bfloat16)
-    parts_rest = (parts - parts_high.astype(f32)).astype(jnp.bfloat16)
-    parts = jnp.stack([parts_high, parts_rest])
-    sent = jnp.concatenate(
-        [
-            packed.reshape(shards, 2, slots),
-            jnp.broadcast_to(parts[None], (shards,) + parts.shape),
-        ],
-        axis=2,
-    )
     data = lax.all_to_all(sent, "doc", 0, 0, tiled=True)
     sums = jnp.sum(data[:, :, slots:].astype(f32), axis=(0, 1))
     t_plus, t_minus, gradients, side = pl.pallas_call(
@@ -284,7 +289,7 @@
             jax.ShapeDtypeStruct((1, POS), f32),
             jax.ShapeDtypeStruct((1, POS), f32),
             jax.ShapeDtypeStruct((2, slots), f32),
-            jax.ShapeDtypeStruct((2, 3 * slots // 2), jnp.bfloat16),
+            jax.ShapeDtypeStruct((shards // 2, 2, 3 * slots // 2), jnp.bfloat16),
         ),
         in_specs=[VMEM, VMEM, VMEM, VMEM, SMEM, VMEM, VMEM],
         out_specs=(VMEM,) * 4,
@@ -295,14 +300,7 @@
         name="lambdas",
     )(gap, discount, scores, clicks, lengths, leaf.reshape(queries, POS), sums[None])
     same_core = [[2 * chip + core for chip in range(shards // 2)] for core in range(2)]
-    side = lax.all_to_all(
-        jnp.broadcast_to(side[None], (shards // 2,) + side.shape),
-        "doc",
-        0,
-        0,
-        axis_index_groups=same_core,
-        tiled=True,
-    )
+    side = lax.all_to_all(side, "doc", 0, 0, axis_index_groups=same_core, tiled=True)
     shown = jnp.sum((data[:, 0, :slots] >= 0).astype(f32), axis=1).astype(jnp.int32)
     plan = pl.pallas_call(
         plan_kernel,
@@ -316,6 +314,9 @@
     )((shown + (TILE - 1)) // TILE)
     other_side = lax.ppermute(side, "doc", [(at, at ^ 1) for at in range(shards)])
     core = lax.axis_index("doc") % 2
+    data, side, other_side = (
+        pltpu.with_memory_space_constraint(array, pltpu.VMEM) for array in (data, side, other_side)
+    )
     partial = hist_of(core.reshape(1), plan, data, side)
     hist = hist_of((1 - core).reshape(1), plan, data, other_side, partial)
     return (t_plus[0], t_minus[0], gradients, hist)

time: 89 us -> 75.6 us (0.85)
  Pallas kernels: 33.4 us -> 24.4 us
  local copies, waits for them, and re-layouts: 4.13 us -> 0 us
    pallas_call x1, Pallas kernels: 12.9 us -> 7.83 us  [hist_of(): pl.pallas_call(first_kernel, out_shape=jax.ShapeDtypeStruct(part, jnp.flo...]
    pallas_call x1, Pallas kernels: 12.3 us -> 8.06 us  [hist_of(): pl.pallas_call(second_kernel, out_shape=jax.ShapeDtypeStruct((2, 2 * LEAV...]
    broadcast_in_dim x2 -> x0, local copies, waits for them, and re-layouts: 1.6 us -> none  [the longest x1 1.56 us: body(): jnp.broadcast_to(side[None], (shards // 2,) + side.shape)]
    unnamed x8 -> x0, local copies, waits for them, and re-layouts: 1.39 us -> none
    reshape x1 -> x0, local copies, waits for them, and re-layouts: 1.14 us -> none  [body(): packed.reshape(shards, 2, slots)]
  transfers between devices with their start and end apart: 2 -> 2, of which waited for: 1 -> 1; matrix products, arithmetic and copies ran while one was open for 2% -> 2% of each run, Pallas kernels for 17% -> 13%
where the time goes in v4:
time: 75.6 us; the launch traced here: 75.3 us
  blocking collectives  29.5 us (39%)
  Pallas kernels  24.4 us (32%)
  waiting for transfers between devices  12.1 us (16%)
  starting transfers between devices  6.62 us (9%)
  other arithmetic  2.01 us (3%)
    all_to_all x1, blocking collectives, body(): data = lax.all_to_all(sent, 'doc', 0, 0, tiled=True)  29.5 us
    all_to_all x1, waiting for transfers between devices, body(): lax.all_to_all(side, 'doc', 0, 0, axis_index_groups=same_core, tiled=True)  12 us
    pallas_call x1, Pallas kernels, hist_of(): pl.pallas_call(second_kernel, out_shape=jax.ShapeDtypeStruct((2, 2 * LEAV...  8.06 us
    pallas_call x1, Pallas kernels, hist_of(): pl.pallas_call(first_kernel, out_shape=jax.ShapeDtypeStruct(part, jnp.flo...  7.83 us
    all_to_all x1, starting transfers between devices, body(): lax.all_to_all(side, 'doc', 0, 0, axis_index_groups=same_core, tiled=True)  4.45 us
    pallas_call x1, Pallas kernels, body(): pl.pallas_call(pair_kernel, out_shape=jax.ShapeDtypeStruct((shards, 2, sl...  3.35 us
    pallas_call x1, Pallas kernels, body(): pl.pallas_call(lambda_kernel, out_shape=(jax.ShapeDtypeStruct((1, POS), f...  2.9 us
    pallas_call x1, Pallas kernels, body(): pl.pallas_call(plan_kernel, out_shape=(jax.ShapeDtypeStruct((shards * til...  2.29 us
  transfers between devices with their start and end apart: 2, of which 1 were waited for; matrix products, arithmetic and copies ran while one was open for 2% of the time, Pallas kernels for 13%

profile of v4, /device:TPU:1, one launch (start us, length us, event | category | flops | bytes accessed | tf_op | source)
XLA Modules:
  0.0 75.3 jit_solution(12742169425084737838)
XLA Ops:
  0.6 3.3 %pair_terms.1 = bf16[64,2,1792]{2,1,0:T(2,128)(2,1)} custom-call(f32[128,128]{1,0:T(8,128)} %constant.43.clone.gap_ref, f32[1,128]{1,0:T(1,128)} %constant.44.clone.discount_ref, f32[12,128]{1,0:T(8,128)} %scores_ref.3, s32[12,128]{1,0:T(8,128)} %clicks_ref.3, s32[12]{0:T(128)} %lengths_ref.3, f32[1,128]{1,0:T(1,128)} %bitcast.10, f32[1,128]{1,0:T(1,128)} %bitcast.11, ...), custom_call_target="tpu_custom_call" | custom-call | tf_op jit(solution)/shard_map/pair_terms/pallas_call | solution.py:276
  4.0 29.5 %all_to_all.10.data_ref = bf16[64,2,1792]{2,1,0:T(2,128)(2,1)S(1)} all-to-all(bf16[64,2,1792]{2,1,0:T(2,128)(2,1)} %pair_terms.1), channel_id=1, replica_groups=mesh['doc'=64,'feat'=4] {'doc'}, dimensions={0} | all-to-all | bytes 917504 | tf_op jit(solution)/shard_map/all_to_all | solution.py:284
  33.5 0.7 convert_reduce_fusion
  34.1 2.9 %lambdas.1 = (f32[1,128]{1,0:T(1,128)}, f32[1,128]{1,0:T(1,128)}, f32[2,1536]{1,0:T(2,128)}, bf16[32,2,2304]{2,1,0:T(2,128)(2,1)}) custom-call(f32[128,128]{1,0:T(8,128)} %constant.43.clone.gap_ref, f32[1,128]{1,0:T(1,128)} %constant.44.clone.discount_ref, f32[12,128]{1,0:T(8,128)} %scores_ref.3, s32[12,128]{1,0:T(8,128)} %clicks_ref.3, s32[12]{0:T(128)} %lengths_ref.3, ...), custom_call_target="tpu_custom_call" | custom-call | tf_op jit(solution)/shard_map/lambdas/pallas_call | solution.py:286
  37.0 4.4 %all-to-all-start.1 = ((bf16[32,2,2304]{2,1,0:T(2,128)(2,1)}), bf16[32,2,2304]{2,1,0:T(2,128)(2,1)S(1)}, u32[]{:S(2)}, u32[]{:S(2)}) async-start(bf16[32,2,2304]{2,1,0:T(2,128)(2,1)} %get-tuple-element.15), calls=%async_computation.1 | async-start | bytes 589824 | tf_op jit(solution)/shard_map/all_to_all | solution.py:303
  41.5 12.0 %all-to-all-done.1.side_ref = bf16[32,2,2304]{2,1,0:T(2,128)(2,1)S(1)} async-done(((bf16[32,2,2304]{2,1,0:T(2,128)(2,1)}), bf16[32,2,2304]{2,1,0:T(2,128)(2,1)S(1)}, u32[]{:S(2)}, u32[]{:S(2)}) %all-to-all-start.1) | async-done | bytes 294944 | tf_op jit(solution)/shard_map/all_to_all | solution.py:303
  53.6 2.2 %collective-permute-start = (bf16[32,2,2304]{2,1,0:T(2,128)(2,1)S(1)}, bf16[32,2,2304]{2,1,0:T(2,128)(2,1)S(1)}, u32[]{:S(2)}, u32[]{:S(2)}) collective-permute-start(bf16[32,2,2304]{2,1,0:T(2,128)(2,1)S(1)} %all-to-all-done.1.side_ref), channel_id=1, source_target_pairs={{0,4},{4,0},{8,12},{12,8},{16,20},{20,16},{24,28},{28,24},{32,36},... | collective-permute-start | bytes 884744 | tf_op jit(solution)/shard_map/ppermute | solution.py:315
  55.7 0.7 fusion
  56.5 0.6 and_select_fusion.filled_ref
  57.1 2.3 %plan.1 = (s32[400]{0:T(512)}, s32[2]{0:T(128)}) custom-call(s32[64]{0:T(128)} %and_select_fusion.filled_ref), custom_call_target="tpu_custom_call" | custom-call | tf_op jit(solution)/shard_map/plan/pallas_call | solution.py:305
  59.4 7.8 %first_half.1.before_ref = f32[2,128,128]{2,1,0:T(8,128)} custom-call(s32[1]{0:T(128)} %bitcast.7.core_ref, s32[400]{0:T(512)} %get-tuple-element.13.list_ref, s32[2]{0:T(128)} %get-tuple-element.14.total_ref, bf16[64,2,1792]{2,1,0:T(2,128)(2,1)S(1)} %all_to_all.10.data_ref, bf16[32,2,2304]{2,1,0:T(2,128)(2,1)S(1)} %all-to-all-done.1.side_ref), custom_call_target="tpu_custom_call" | custom-call | tf_op jit(solution)/shard_map/first_half/pallas_call | solution.py:250
  67.2 0.0 collective-permute-done.side_ref
  67.2 8.1 %second_half.1 = f32[2,64,256]{2,1,0:T(8,128)} custom-call(s32[1]{0:T(128)} %bitcast.6.core_ref, s32[400]{0:T(512)} %get-tuple-element.13.list_ref, s32[2]{0:T(128)} %get-tuple-element.14.total_ref, bf16[64,2,1792]{2,1,0:T(2,128)(2,1)S(1)} %all_to_all.10.data_ref, bf16[32,2,2304]{2,1,0:T(2,128)(2,1)S(1)} %collective-permute-done.side_ref, ...), custom_call_target="tpu_custom_call" | custom-call | tf_op jit(solution)/shard_map/second_half/pallas_call | solution.py:257
Async XLA Ops:
  37.0 16.5 %all-to-all-start.1 = ((bf16[32,2,2304]{2,1,0:T(2,128)(2,1)}), bf16[32,2,2304]{2,1,0:T(2,128)(2,1)S(1)}, u32[]{:S(2)}, u32[]{:S(2)}) async-start(bf16[32,2,2304]{2,1,0:T(2,128)(2,1)} %get-tuple-element.15), calls=%async_computation.1 | async-start | bytes 589824 | tf_op jit(solution)/shard_map/all_to_all | solution.py:303
  53.6 13.7 %collective-permute-start = (bf16[32,2,2304]{2,1,0:T(2,128)(2,1)S(1)}, bf16[32,2,2304]{2,1,0:T(2,128)(2,1)S(1)}, u32[]{:S(2)}, u32[]{:S(2)}) collective-permute-start(bf16[32,2,2304]{2,1,0:T(2,128)(2,1)S(1)} %all-to-all-done.1.side_ref), channel_id=1, source_target_pairs={{0,4},{4,0},{8,12},{12,8},{16,20},{20,16},{24,28},{28,24},{32,36},... | collective-permute-start | bytes 884744 | tf_op jit(solution)/shard_map/ppermute | solution.py:315

commit v5 on v4

--- a/solution.py
+++ b/solution.py
@@ -90,12 +90,15 @@
             ].astype(jnp.bfloat16)
 
 
-def lambda_kernel(gap_ref, discount_ref, scores_ref, clicks_ref, lengths_ref, leaf_ref, sums_ref, plus_ref, minus_ref,
+def lambda_kernel(gap_ref, discount_ref, scores_ref, clicks_ref, lengths_ref, leaf_ref, data_ref, plus_ref, minus_ref,
                   grad_ref, side_ref, packed, flat):
     queries = scores_ref.shape[0]
     discount_row = discount_ref[...]
-    plus_sum = sums_ref[:, :POS]
-    minus_sum = sums_ref[:, POS:]
+    slots = grad_ref.shape[1]
+    sums = jnp.sum(data_ref[:, :, slots:].astype(jnp.float32), axis=0)
+    sums = sums[0:1] + sums[1:2]
+    plus_sum = sums[:, :POS]
+    minus_sum = sums[:, POS:]
     plus = jnp.sqrt(plus_sum / plus_sum[:, 0:1])
     minus = jnp.sqrt(minus_sum / minus_sum[:, 0:1])
     plus_ref[...] = plus
@@ -244,12 +247,16 @@
 SMEM = pl.BlockSpec(memory_space=pltpu.SMEM)
 
 
+def in_vmem(array):
+    return pltpu.with_memory_space_constraint(array, pltpu.VMEM)
+
+
 def hist_of(core, plan, data, side, before=None):
     part = (2, 4 * LEAVES, HALF)
     if before is None:
         return pl.pallas_call(
             first_kernel,
-            out_shape=jax.ShapeDtypeStruct(part, jnp.float32),
+            out_shape=pltpu.VMEM(part, jnp.float32),
             in_specs=[SMEM, SMEM, SMEM, VMEM, VMEM],
             out_specs=VMEM,
             name="first_half",
@@ -275,21 +282,20 @@
     f32 = jnp.float32
     sent = pl.pallas_call(
         pair_kernel,
-        out_shape=jax.ShapeDtypeStruct((shards, 2, slots + 2 * POS), jnp.bfloat16),
+        out_shape=pltpu.VMEM((shards, 2, slots + 2 * POS), jnp.bfloat16),
         in_specs=[VMEM, VMEM, VMEM, VMEM, SMEM, VMEM, VMEM, VMEM],
         out_specs=VMEM,
         scratch_shapes=[pltpu.VMEM((slots // POS + 1, bins.shape[0], POS), f32)],
         name="pair_terms",
     )(gap, discount, scores, clicks, lengths, t_plus_old[None], t_minus_old[None], bins)
     data = lax.all_to_all(sent, "doc", 0, 0, tiled=True)
-    sums = jnp.sum(data[:, :, slots:].astype(f32), axis=(0, 1))
     t_plus, t_minus, gradients, side = pl.pallas_call(
         lambda_kernel,
         out_shape=(
-            jax.ShapeDtypeStruct((1, POS), f32),
-            jax.ShapeDtypeStruct((1, POS), f32),
-            jax.ShapeDtypeStruct((2, slots), f32),
-            jax.ShapeDtypeStruct((shards // 2, 2, 3 * slots // 2), jnp.bfloat16),
+            pltpu.VMEM((1, POS), f32),
+            pltpu.VMEM((1, POS), f32),
+            pltpu.VMEM((2, slots), f32),
+            pltpu.VMEM((shards // 2, 2, 3 * slots // 2), jnp.bfloat16),
         ),
         in_specs=[VMEM, VMEM, VMEM, VMEM, SMEM, VMEM, VMEM],
         out_specs=(VMEM,) * 4,
@@ -298,7 +304,15 @@
             pltpu.VMEM((2, 3 * slots // 2), f32),
         ],
         name="lambdas",
-    )(gap, discount, scores, clicks, lengths, leaf.reshape(queries, POS), sums[None])
+    )(
+        in_vmem(gap),
+        in_vmem(discount),
+        in_vmem(scores),
+        in_vmem(clicks),
+        lengths,
+        in_vmem(leaf.reshape(queries, POS)),
+        in_vmem(data),
+    )
     same_core = [[2 * chip + core for chip in range(shards // 2)] for core in range(2)]
     side = lax.all_to_all(side, "doc", 0, 0, axis_index_groups=same_core, tiled=True)
     shown = jnp.sum((data[:, 0, :slots] >= 0).astype(f32), axis=1).astype(jnp.int32)
@@ -314,11 +328,8 @@
     )((shown + (TILE - 1)) // TILE)
     other_side = lax.ppermute(side, "doc", [(at, at ^ 1) for at in range(shards)])
     core = lax.axis_index("doc") % 2
-    data, side, other_side = (
-        pltpu.with_memory_space_constraint(array, pltpu.VMEM) for array in (data, side, other_side)
-    )
-    partial = hist_of(core.reshape(1), plan, data, side)
-    hist = hist_of((1 - core).reshape(1), plan, data, other_side, partial)
+    partial = hist_of(core.reshape(1), plan, in_vmem(data), in_vmem(side))
+    hist = hist_of((1 - core).reshape(1), plan, in_vmem(data), in_vmem(other_side), partial)
     return (t_plus[0], t_minus[0], gradients, hist)
 
 

time: 75.6 us -> 76.2 us (level)
  local copies, waits for them, and re-layouts: 0 us -> 2.92 us
  Pallas kernels: 24.4 us -> 22.7 us
    unnamed x0 -> x15, local copies, waits for them, and re-layouts: none -> 2.92 us
    pallas_call x3, Pallas kernels: 14.1 us -> 12.4 us  [the longest x1 7.18 us: hist_of(): pl.pallas_call(first_kernel, out_shape=pltpu.VMEM(part, jnp.float32), in_...]
  transfers between devices with their start and end apart: 2 -> 2, of which waited for: 1 -> 1; matrix products, arithmetic and copies ran while one was open for 2% -> 4% of each run, Pallas kernels for 13% -> 12%
where the time goes in v5:
time: 76.2 us; the launch traced here: 75.8 us
  blocking collectives  29.4 us (39%)
  Pallas kernels  22.7 us (30%)
  waiting for transfers between devices  12.1 us (16%)
  starting transfers between devices  6.62 us (9%)
  local copies, waits for them, and re-layouts  2.92 us (4%)
  other arithmetic  1.34 us (2%)
    all_to_all x1, blocking collectives, body(): data = lax.all_to_all(sent, 'doc', 0, 0, tiled=True)  29.4 us
    all_to_all x1, waiting for transfers between devices, body(): lax.all_to_all(side, 'doc', 0, 0, axis_index_groups=same_core, tiled=True)  12 us
    pallas_call x1, Pallas kernels, hist_of(): pl.pallas_call(second_kernel, out_shape=jax.ShapeDtypeStruct((2, 2 * LEAV...  8.06 us
    pallas_call x1, Pallas kernels, hist_of(): pl.pallas_call(first_kernel, out_shape=pltpu.VMEM(part, jnp.float32), in_...  7.18 us
    all_to_all x1, starting transfers between devices, body(): lax.all_to_all(side, 'doc', 0, 0, axis_index_groups=same_core, tiled=True)  4.45 us
    unnamed x15, local copies, waits for them, and re-layouts  2.92 us
    pallas_call x1, Pallas kernels, body(): pl.pallas_call(lambda_kernel, out_shape=(pltpu.VMEM((1, POS), f32), pltpu...  2.63 us
    pallas_call x1, Pallas kernels, body(): pl.pallas_call(pair_kernel, out_shape=pltpu.VMEM((shards, 2, slots + 2 *...  2.57 us
  transfers between devices with their start and end apart: 2, of which 1 were waited for; matrix products, arithmetic and copies ran while one was open for 4% of the time, Pallas kernels for 12%

profile of v5, /device:TPU:1, one launch (start us, length us, event | category | flops | bytes accessed | tf_op | source)
XLA Modules:
  0.0 75.8 jit_solution(14373104034906887879)
XLA Ops:
  0.6 2.6 %pair_terms.1 = bf16[64,2,1792]{2,1,0:T(2,128)(2,1)S(1)} custom-call(f32[128,128]{1,0:T(8,128)} %constant.43.clone.gap_ref, f32[1,128]{1,0:T(1,128)} %constant.44.clone.discount_ref, f32[12,128]{1,0:T(8,128)} %scores_ref.3, s32[12,128]{1,0:T(8,128)} %clicks_ref.3, s32[12]{0:T(128)} %lengths_ref.3, f32[1,128]{1,0:T(1,128)} %bitcast.10, f32[1,128]{1,0:T(1,128)} %bitcast.11, ...), custom_call_target="tpu_custom_call" | custom-call | tf_op jit(solution)/shard_map/pair_terms/pallas_call | solution.py:283
  3.2 0.0 copy-start.1
  3.2 0.0 copy-start.2
  3.2 0.0 copy-start.3
  3.3 0.0 copy-start.4
  3.3 29.4 %all_to_all.10.data_ref = bf16[64,2,1792]{2,1,0:T(2,128)(2,1)S(1)} all-to-all(bf16[64,2,1792]{2,1,0:T(2,128)(2,1)S(1)} %pair_terms.1), channel_id=1, replica_groups=mesh['doc'=64,'feat'=4] {'doc'}, dimensions={0} | all-to-all | bytes 917504 | tf_op jit(solution)/shard_map/all_to_all | solution.py:291
  32.7 0.0 copy-start.5
  32.7 0.0 copy-done.1
  32.7 0.0 copy-done.2
  32.7 0.0 copy-done.3
  32.7 0.0 copy-done.4
  32.7 0.6 copy-done.5
  33.4 2.6 %lambdas.1 = (f32[1,128]{1,0:T(1,128)S(1)}, f32[1,128]{1,0:T(1,128)S(1)}, f32[2,1536]{1,0:T(2,128)S(1)}, bf16[32,2,2304]{2,1,0:T(2,128)(2,1)}) custom-call(f32[128,128]{1,0:T(8,128)S(1)} %copy-done.1, f32[1,128]{1,0:T(1,128)S(1)} %copy-done.5, f32[12,128]{1,0:T(8,128)S(1)} %copy-done.2, s32[12,128]{1,0:T(8,128)S(1)} %copy-done.3, s32[12]{0:T(128)} %lengths_ref.3, ...), custom_call_target="tpu_custom_call" | custom-call | tf_op jit(solution)/shard_map/lambdas/pallas_call | solution.py:292
  36.0 4.4 %all-to-all-start.1 = ((bf16[32,2,2304]{2,1,0:T(2,128)(2,1)}), bf16[32,2,2304]{2,1,0:T(2,128)(2,1)S(1)}, u32[]{:S(2)}, u32[]{:S(2)}) async-start(bf16[32,2,2304]{2,1,0:T(2,128)(2,1)} %get-tuple-element.15), calls=%async_computation.1 | async-start | bytes 589824 | tf_op jit(solution)/shard_map/all_to_all | solution.py:317
  40.5 12.0 %all-to-all-done.1.side_ref = bf16[32,2,2304]{2,1,0:T(2,128)(2,1)S(1)} async-done(((bf16[32,2,2304]{2,1,0:T(2,128)(2,1)}), bf16[32,2,2304]{2,1,0:T(2,128)(2,1)S(1)}, u32[]{:S(2)}, u32[]{:S(2)}) %all-to-all-start.1) | async-done | bytes 294944 | tf_op jit(solution)/shard_map/all_to_all | solution.py:317
  52.5 2.2 %collective-permute-start = (bf16[32,2,2304]{2,1,0:T(2,128)(2,1)S(1)}, bf16[32,2,2304]{2,1,0:T(2,128)(2,1)S(1)}, u32[]{:S(2)}, u32[]{:S(2)}) collective-permute-start(bf16[32,2,2304]{2,1,0:T(2,128)(2,1)S(1)} %all-to-all-done.1.side_ref), channel_id=1, source_target_pairs={{0,4},{4,0},{8,12},{12,8},{16,20},{20,16},{24,28},{28,24},{32,36},... | collective-permute-start | bytes 884744 | tf_op jit(solution)/shard_map/ppermute | solution.py:329
  54.7 0.7 fusion
  55.4 0.5 copy.13
  55.9 0.5 copy.14
  56.5 0.6 copy.15
  57.1 0.6 and_select_fusion.filled_ref
  57.6 2.3 %plan.1 = (s32[400]{0:T(512)}, s32[2]{0:T(128)}) custom-call(s32[64]{0:T(128)} %and_select_fusion.filled_ref), custom_call_target="tpu_custom_call" | custom-call | tf_op jit(solution)/shard_map/plan/pallas_call | solution.py:319
  59.9 7.2 %first_half.1.before_ref = f32[2,128,128]{2,1,0:T(8,128)S(1)} custom-call(s32[1]{0:T(128)} %bitcast.6.core_ref, s32[400]{0:T(512)} %get-tuple-element.13.list_ref, s32[2]{0:T(128)} %get-tuple-element.14.total_ref, bf16[64,2,1792]{2,1,0:T(2,128)(2,1)S(1)} %all_to_all.10.data_ref, bf16[32,2,2304]{2,1,0:T(2,128)(2,1)S(1)} %all-to-all-done.1.side_ref), custom_call_target="tpu_custom_call" | custom-call | tf_op jit(solution)/shard_map/first_half/pallas_call | solution.py:257
  67.1 0.0 copy-start
  67.1 0.6 copy-done
  67.8 0.0 collective-permute-done.side_ref
  67.8 8.1 %second_half.1 = f32[2,64,256]{2,1,0:T(8,128)} custom-call(s32[1]{0:T(128)} %bitcast.5.core_ref, s32[400]{0:T(512)} %get-tuple-element.13.list_ref, s32[2]{0:T(128)} %get-tuple-element.14.total_ref, bf16[64,2,1792]{2,1,0:T(2,128)(2,1)S(1)} %all_to_all.10.data_ref, bf16[32,2,2304]{2,1,0:T(2,128)(2,1)S(1)} %collective-permute-done.side_ref, f32[2,128,128]{2,1,0:T(8,128)} %copy-done), custom_call_target="tpu_custom_call" | custom-call | tf_op jit(solution)/shard_map/second_half/pallas_call | solution.py:264
Async XLA Ops:
  3.2 29.5 %copy-start.1 = (f32[128,128]{1,0:T(8,128)S(1)}, f32[128,128]{1,0:T(8,128)}, u32[]{:S(2)}) copy-start(f32[128,128]{1,0:T(8,128)} %constant.43.clone.gap_ref) | copy-start | bytes 196612
  3.2 29.5 %copy-start.2 = (f32[12,128]{1,0:T(8,128)S(1)}, f32[12,128]{1,0:T(8,128)}, u32[]{:S(2)}) copy-start(f32[12,128]{1,0:T(8,128)} %scores_ref.3) | copy-start | bytes 18436
  3.2 29.5 %copy-start.3 = (s32[12,128]{1,0:T(8,128)S(1)}, s32[12,128]{1,0:T(8,128)}, u32[]{:S(2)}) copy-start(s32[12,128]{1,0:T(8,128)} %clicks_ref.3) | copy-start | bytes 18436
  3.3 29.5 %copy-start.4 = (s32[1536]{0:T(1024)S(1)}, s32[1536]{0:T(1024)}, u32[]{:S(2)}) copy-start(s32[1536]{0:T(1024)} %param.14) | copy-start | bytes 18436
  32.7 0.7 copy-start.5
  36.0 16.5 %all-to-all-start.1 = ((bf16[32,2,2304]{2,1,0:T(2,128)(2,1)}), bf16[32,2,2304]{2,1,0:T(2,128)(2,1)S(1)}, u32[]{:S(2)}, u32[]{:S(2)}) async-start(bf16[32,2,2304]{2,1,0:T(2,128)(2,1)} %get-tuple-element.15), calls=%async_computation.1 | async-start | bytes 589824 | tf_op jit(solution)/shard_map/all_to_all | solution.py:317
  52.5 15.3 %collective-permute-start = (bf16[32,2,2304]{2,1,0:T(2,128)(2,1)S(1)}, bf16[32,2,2304]{2,1,0:T(2,128)(2,1)S(1)}, u32[]{:S(2)}, u32[]{:S(2)}) collective-permute-start(bf16[32,2,2304]{2,1,0:T(2,128)(2,1)S(1)} %all-to-all-done.1.side_ref), channel_id=1, source_target_pairs={{0,4},{4,0},{8,12},{12,8},{16,20},{20,16},{24,28},{28,24},{32,36},... | collective-permute-start | bytes 884744 | tf_op jit(solution)/shard_map/ppermute | solution.py:329
  67.1 0.7 copy-start

commit v6 on v5

--- a/solution.py
+++ b/solution.py
@@ -39,10 +39,10 @@
     return jnp.transpose(jnp.concatenate(list(rows) + [pad], axis=0))
 
 
-def pair_kernel(gap_ref, discount_ref, scores_ref, clicks_ref, lengths_ref, plus_ref, minus_ref, bins_ref,
+def pair_kernel(gap_ref, scores_ref, clicks_ref, lengths_ref, plus_ref, minus_ref, bins_ref,
                 sent_ref, packed):
     queries = scores_ref.shape[0]
-    discount_row = discount_ref[...]
+    discount_row = gap_ref[POS : POS + 1]
     clicked, skipped, side, signed, ideal = query_rows(
         scores_ref[...], clicks_ref[...], lengths_ref, queries, discount_row
     )
@@ -57,7 +57,7 @@
         spread = other + signed[query : query + 1]
         cross = jnp.maximum(strength * -side[query : query + 1], 0.0)
         loss = jnp.maximum(-spread, 0.0) + jnp.log1p(jnp.exp(-jnp.abs(spread)))
-        total = jnp.sum(cross * gap_ref[...] * loss, axis=0, keepdims=True)
+        total = jnp.sum(cross * gap_ref[:POS] * loss, axis=0, keepdims=True)
         total = total * scale[query : query + 1]
         plus += jnp.where(side[query : query + 1] > 0.0, total, 0.0)
         minus += jnp.where(side[query : query + 1] < 0.0, total, 0.0)
@@ -90,10 +90,10 @@
             ].astype(jnp.bfloat16)
 
 
-def lambda_kernel(gap_ref, discount_ref, scores_ref, clicks_ref, lengths_ref, leaf_ref, data_ref, plus_ref, minus_ref,
+def lambda_kernel(gap_ref, scores_ref, clicks_ref, lengths_ref, leaf_ref, data_ref, plus_ref, minus_ref,
                   grad_ref, side_ref, packed, flat):
     queries = scores_ref.shape[0]
-    discount_row = discount_ref[...]
+    discount_row = gap_ref[POS : POS + 1]
     slots = grad_ref.shape[1]
     sums = jnp.sum(data_ref[:, :, slots:].astype(jnp.float32), axis=0)
     sums = sums[0:1] + sums[1:2]
@@ -119,7 +119,7 @@
         cross = jnp.maximum(strength * -side[query : query + 1], 0.0)
         grown = jnp.exp(spread)
         chance = 1.0 / (1.0 + grown)
-        first = cross * gap_ref[...] * chance
+        first = cross * gap_ref[:POS] * chance
         second = first * (grown * chance)
         slope = jnp.sum(first, axis=0, keepdims=True) * outer[query : query + 1]
         slope = slope * -side[query : query + 1]
@@ -148,7 +148,12 @@
     side_ref[...] = jnp.broadcast_to(flat[...].astype(jnp.bfloat16)[None], side_ref.shape)
 
 
-def plan_kernel(filled_ref, list_ref, total_ref):
+def plan_kernel(
+    filled_ref, plus_in, minus_in, grad_in, list_ref, total_ref, plus_ref, minus_ref, grad_ref
+):
+    plus_ref[...] = plus_in[...]
+    minus_ref[...] = minus_in[...]
+    grad_ref[...] = grad_in[...]
     chips = filled_ref.shape[0] // 2
     tiles = (list_ref.shape[0] // 2 - STEP) // chips
     for core in range(2):
@@ -251,6 +256,10 @@
     return pltpu.with_memory_space_constraint(array, pltpu.VMEM)
 
 
+def in_smem(array):
+    return pltpu.with_memory_space_constraint(array, pltpu.SMEM)
+
+
 def hist_of(core, plan, data, side, before=None):
     part = (2, 4 * LEAVES, HALF)
     if before is None:
@@ -277,17 +286,17 @@
     tiles = slots // TILE
     places = np.arange(POS, dtype=np.float32)
     discount = (1.0 / np.log2(2.0 + places)).astype(np.float32)
-    gap = jnp.asarray(np.abs(discount[:, None] - discount[None, :]))
-    discount = jnp.asarray(discount[None])
+    gap = np.abs(discount[:, None] - discount[None, :])
+    gap = jnp.asarray(np.concatenate([gap, np.tile(discount[None], (8, 1))]))
     f32 = jnp.float32
     sent = pl.pallas_call(
         pair_kernel,
         out_shape=pltpu.VMEM((shards, 2, slots + 2 * POS), jnp.bfloat16),
-        in_specs=[VMEM, VMEM, VMEM, VMEM, SMEM, VMEM, VMEM, VMEM],
+        in_specs=[VMEM, VMEM, VMEM, SMEM, VMEM, VMEM, VMEM],
         out_specs=VMEM,
         scratch_shapes=[pltpu.VMEM((slots // POS + 1, bins.shape[0], POS), f32)],
         name="pair_terms",
-    )(gap, discount, scores, clicks, lengths, t_plus_old[None], t_minus_old[None], bins)
+    )(gap, scores, clicks, lengths, t_plus_old[None], t_minus_old[None], bins)
     data = lax.all_to_all(sent, "doc", 0, 0, tiled=True)
     t_plus, t_minus, gradients, side = pl.pallas_call(
         lambda_kernel,
@@ -297,7 +306,7 @@
             pltpu.VMEM((2, slots), f32),
             pltpu.VMEM((shards // 2, 2, 3 * slots // 2), jnp.bfloat16),
         ),
-        in_specs=[VMEM, VMEM, VMEM, VMEM, SMEM, VMEM, VMEM],
+        in_specs=[VMEM, VMEM, VMEM, SMEM, VMEM, VMEM],
         out_specs=(VMEM,) * 4,
         scratch_shapes=[
             pltpu.VMEM((queries + 1, 8, POS), f32),
@@ -306,30 +315,32 @@
         name="lambdas",
     )(
         in_vmem(gap),
-        in_vmem(discount),
         in_vmem(scores),
         in_vmem(clicks),
-        lengths,
+        in_smem(lengths),
         in_vmem(leaf.reshape(queries, POS)),
         in_vmem(data),
     )
     same_core = [[2 * chip + core for chip in range(shards // 2)] for core in range(2)]
     side = lax.all_to_all(side, "doc", 0, 0, axis_index_groups=same_core, tiled=True)
     shown = jnp.sum((data[:, 0, :slots] >= 0).astype(f32), axis=1).astype(jnp.int32)
-    plan = pl.pallas_call(
+    *plan, t_plus, t_minus, gradients = pl.pallas_call(
         plan_kernel,
         out_shape=(
-            jax.ShapeDtypeStruct((shards * tiles + 2 * STEP,), jnp.int32),
-            jax.ShapeDtypeStruct((2,), jnp.int32),
+            pltpu.SMEM((shards * tiles + 2 * STEP,), jnp.int32),
+            pltpu.SMEM((2,), jnp.int32),
+            jax.ShapeDtypeStruct((1, POS), f32),
+            jax.ShapeDtypeStruct((1, POS), f32),
+            jax.ShapeDtypeStruct((2, slots), f32),
         ),
-        in_specs=[SMEM],
-        out_specs=(SMEM, SMEM),
+        in_specs=[SMEM, VMEM, VMEM, VMEM],
+        out_specs=(SMEM, SMEM, VMEM, VMEM, VMEM),
         name="plan",
-    )((shown + (TILE - 1)) // TILE)
+    )((shown + (TILE - 1)) // TILE, in_vmem(t_plus), in_vmem(t_minus), in_vmem(gradients))
     other_side = lax.ppermute(side, "doc", [(at, at ^ 1) for at in range(shards)])
     core = lax.axis_index("doc") % 2
     partial = hist_of(core.reshape(1), plan, in_vmem(data), in_vmem(side))
-    hist = hist_of((1 - core).reshape(1), plan, in_vmem(data), in_vmem(other_side), partial)
+    hist = hist_of((1 - core).reshape(1), plan, in_vmem(data), in_vmem(other_side), in_vmem(partial))
     return (t_plus[0], t_minus[0], gradients, hist)
 
 

time: 76.2 us -> 71.6 us (0.940)
  local copies, waits for them, and re-layouts: 2.92 us -> 0.03 us
  Pallas kernels: 22.7 us -> 21.2 us
    unnamed x15 -> x8, local copies, waits for them, and re-layouts: 2.92 us -> 0.03 us
    pallas_call x1, Pallas kernels: 8.06 us -> 7.16 us  [hist_of(): pl.pallas_call(second_kernel, out_shape=jax.ShapeDtypeStruct((2, 2 * LEAV...]
  transfers between devices with their start and end apart: 2 -> 2, of which waited for: 1 -> 1; matrix products, arithmetic and copies ran while one was open for 4% -> 2% of each run, Pallas kernels for 12% -> 12%
where the time goes in v6:
time: 71.6 us; the launch traced here: 71.3 us
  blocking collectives  29.4 us (41%)
  Pallas kernels  21.2 us (30%)
  waiting for transfers between devices  12.1 us (17%)
  starting transfers between devices  6.63 us (9%)
  other arithmetic  1.27 us (2%)
  between operations  0.72 us (1%)
    all_to_all x1, blocking collectives, body(): data = lax.all_to_all(sent, 'doc', 0, 0, tiled=True)  29.4 us
    all_to_all x1, waiting for transfers between devices, body(): lax.all_to_all(side, 'doc', 0, 0, axis_index_groups=same_core, tiled=True)  12 us
    pallas_call x1, Pallas kernels, hist_of(): pl.pallas_call(second_kernel, out_shape=jax.ShapeDtypeStruct((2, 2 * LEAV...  7.16 us
    pallas_call x1, Pallas kernels, hist_of(): pl.pallas_call(first_kernel, out_shape=pltpu.VMEM(part, jnp.float32), in_...  6.54 us
    all_to_all x1, starting transfers between devices, body(): lax.all_to_all(side, 'doc', 0, 0, axis_index_groups=same_core, tiled=True)  4.45 us
    pallas_call x1, Pallas kernels, body(): pl.pallas_call(lambda_kernel, out_shape=(pltpu.VMEM((1, POS), f32), pltpu...  2.62 us
    pallas_call x1, Pallas kernels, body(): pl.pallas_call(pair_kernel, out_shape=pltpu.VMEM((shards, 2, slots + 2 *...  2.56 us
    pallas_call x1, Pallas kernels, body(): pl.pallas_call(plan_kernel, out_shape=(pltpu.SMEM((shards * tiles + 2 * S...  2.3 us
  transfers between devices with their start and end apart: 2, of which 1 were waited for; matrix products, arithmetic and copies ran while one was open for 2% of the time, Pallas kernels for 12%

profile of v6, /device:TPU:1, one launch (start us, length us, event | category | flops | bytes accessed | tf_op | source)
XLA Modules:
  0.0 71.3 jit_solution(1736507552551765742)
XLA Ops:
  0.6 2.6 %pair_terms.1 = bf16[64,2,1792]{2,1,0:T(2,128)(2,1)S(1)} custom-call(f32[136,128]{1,0:T(8,128)} %constant.41.clone.gap_ref, f32[12,128]{1,0:T(8,128)} %scores_ref.3, s32[12,128]{1,0:T(8,128)} %clicks_ref.3, s32[12]{0:T(128)} %lengths_ref.3, f32[1,128]{1,0:T(1,128)} %bitcast.8, f32[1,128]{1,0:T(1,128)} %bitcast.9, s32[128,1536]{1,0:T(8,128)} %bins_ref.1), custom_call_target="tpu_custom_call" | custom-call | tf_op jit(solution)/shard_map/pair_terms/pallas_call | solution.py:292
  3.2 0.0 copy-start
  3.2 0.0 copy-start.1
  3.2 0.0 copy-start.2
  3.2 0.0 copy-start.3
  3.2 29.4 %all_to_all.10.data_ref = bf16[64,2,1792]{2,1,0:T(2,128)(2,1)S(1)} all-to-all(bf16[64,2,1792]{2,1,0:T(2,128)(2,1)S(1)} %pair_terms.1), channel_id=1, replica_groups=mesh['doc'=64,'feat'=4] {'doc'}, dimensions={0} | all-to-all | bytes 917504 | tf_op jit(solution)/shard_map/all_to_all | solution.py:300
  32.7 0.0 copy-done
  32.7 0.0 copy-done.1
  32.7 0.0 copy-done.2
  32.7 0.0 copy-done.3
  32.7 2.6 %lambdas.1 = (f32[1,128]{1,0:T(1,128)S(1)}, f32[1,128]{1,0:T(1,128)S(1)}, f32[2,1536]{1,0:T(2,128)S(1)}, bf16[32,2,2304]{2,1,0:T(2,128)(2,1)}) custom-call(f32[136,128]{1,0:T(8,128)S(1)} %copy-done, f32[12,128]{1,0:T(8,128)S(1)} %copy-done.1, s32[12,128]{1,0:T(8,128)S(1)} %copy-done.2, s32[12]{0:T(128)} %lengths_ref.3, s32[12,128]{1,0:T(8,128)S(1)} %bitcast.7, ...), custom_call_target="tpu_custom_call" | custom-call | tf_op jit(solution)/shard_map/lambdas/pallas_call | solution.py:301
  35.3 4.4 %all-to-all-start.1 = ((bf16[32,2,2304]{2,1,0:T(2,128)(2,1)}), bf16[32,2,2304]{2,1,0:T(2,128)(2,1)S(1)}, u32[]{:S(2)}, u32[]{:S(2)}) async-start(bf16[32,2,2304]{2,1,0:T(2,128)(2,1)} %get-tuple-element.21), calls=%async_computation.1 | async-start | bytes 589824 | tf_op jit(solution)/shard_map/all_to_all | solution.py:325
  39.8 12.0 %all-to-all-done.1.side_ref = bf16[32,2,2304]{2,1,0:T(2,128)(2,1)S(1)} async-done(((bf16[32,2,2304]{2,1,0:T(2,128)(2,1)}), bf16[32,2,2304]{2,1,0:T(2,128)(2,1)S(1)}, u32[]{:S(2)}, u32[]{:S(2)}) %all-to-all-start.1) | async-done | bytes 294944 | tf_op jit(solution)/shard_map/all_to_all | solution.py:325
  51.8 2.2 %collective-permute-start = (bf16[32,2,2304]{2,1,0:T(2,128)(2,1)S(1)}, bf16[32,2,2304]{2,1,0:T(2,128)(2,1)S(1)}, u32[]{:S(2)}, u32[]{:S(2)}) collective-permute-start(bf16[32,2,2304]{2,1,0:T(2,128)(2,1)S(1)} %all-to-all-done.1.side_ref), channel_id=1, source_target_pairs={{0,4},{4,0},{8,12},{12,8},{16,20},{20,16},{24,28},{28,24},{32,36},... | collective-permute-start | bytes 884744 | tf_op jit(solution)/shard_map/ppermute | solution.py:340
  54.0 0.7 %fusion = f32[64]{0:T(128)S(1)} fusion(bf16[64,2,1792]{2,1,0:T(2,128)(2,1)S(1)} %all_to_all.10.data_ref), kind=kLoop, calls=%fused_computation.1 | loop fusion | flops 294848 | bytes 196864 | tf_op jit(solution)/shard_map/reduce_sum | solution.py:326
  54.8 0.5 and_select_fusion.filled_ref
  55.3 2.3 %plan.1 = (s32[400]{0:T(512)S(4)}, s32[2]{0:T(128)S(4)}, f32[1,128]{1,0:T(1,128)}, f32[1,128]{1,0:T(1,128)}, f32[2,1536]{1,0:T(2,128)}) custom-call(s32[64]{0:T(128)} %and_select_fusion.filled_ref, f32[1,128]{1,0:T(1,128)S(1)} %get-tuple-element.13.plus_in, f32[1,128]{1,0:T(1,128)S(1)} %get-tuple-element.14.minus_in, f32[2,1536]{1,0:T(2,128)S(1)} %get-tuple-element.15.grad_in), custom_call_target="tpu_custom_call" | custom-call | tf_op jit(solution)/shard_map/plan/pallas_call | solution.py:327
  57.6 6.5 %first_half.1.before_ref = f32[2,128,128]{2,1,0:T(8,128)S(1)} custom-call(s32[1]{0:T(128)} %bitcast.6.core_ref, s32[400]{0:T(512)S(4)} %get-tuple-element.19.list_ref, s32[2]{0:T(128)S(4)} %get-tuple-element.20.total_ref, bf16[64,2,1792]{2,1,0:T(2,128)(2,1)S(1)} %all_to_all.10.data_ref, bf16[32,2,2304]{2,1,0:T(2,128)(2,1)S(1)} %all-to-all-done.1.side_ref), custom_call_target="tpu_custom_call" | custom-call | tf_op jit(solution)/shard_map/first_half/pallas_call | solution.py:266
  64.1 0.0 collective-permute-done.side_ref
  64.2 7.2 %second_half.1 = f32[2,64,256]{2,1,0:T(8,128)} custom-call(s32[1]{0:T(128)} %bitcast.5.core_ref, s32[400]{0:T(512)S(4)} %get-tuple-element.19.list_ref, s32[2]{0:T(128)S(4)} %get-tuple-element.20.total_ref, bf16[64,2,1792]{2,1,0:T(2,128)(2,1)S(1)} %all_to_all.10.data_ref, bf16[32,2,2304]{2,1,0:T(2,128)(2,1)S(1)} %collective-permute-done.side_ref, ...), custom_call_target="tpu_custom_call" | custom-call | tf_op jit(solution)/shard_map/second_half/pallas_call | solution.py:273
Async XLA Ops:
  3.2 29.5 %copy-start = (f32[136,128]{1,0:T(8,128)S(1)}, f32[136,128]{1,0:T(8,128)}, u32[]{:S(2)}) copy-start(f32[136,128]{1,0:T(8,128)} %constant.41.clone.gap_ref) | copy-start | bytes 208900
  3.2 29.5 %copy-start.1 = (f32[12,128]{1,0:T(8,128)S(1)}, f32[12,128]{1,0:T(8,128)}, u32[]{:S(2)}) copy-start(f32[12,128]{1,0:T(8,128)} %scores_ref.3) | copy-start | bytes 18436
  3.2 29.5 %copy-start.2 = (s32[12,128]{1,0:T(8,128)S(1)}, s32[12,128]{1,0:T(8,128)}, u32[]{:S(2)}) copy-start(s32[12,128]{1,0:T(8,128)} %clicks_ref.3) | copy-start | bytes 18436
  3.2 29.5 %copy-start.3 = (s32[1536]{0:T(1024)S(1)}, s32[1536]{0:T(1024)}, u32[]{:S(2)}) copy-start(s32[1536]{0:T(1024)} %param.13) | copy-start | bytes 18436
  35.3 16.5 %all-to-all-start.1 = ((bf16[32,2,2304]{2,1,0:T(2,128)(2,1)}), bf16[32,2,2304]{2,1,0:T(2,128)(2,1)S(1)}, u32[]{:S(2)}, u32[]{:S(2)}) async-start(bf16[32,2,2304]{2,1,0:T(2,128)(2,1)} %get-tuple-element.21), calls=%async_computation.1 | async-start | bytes 589824 | tf_op jit(solution)/shard_map/all_to_all | solution.py:325
  51.8 12.3 %collective-permute-start = (bf16[32,2,2304]{2,1,0:T(2,128)(2,1)S(1)}, bf16[32,2,2304]{2,1,0:T(2,128)(2,1)S(1)}, u32[]{:S(2)}, u32[]{:S(2)}) collective-permute-start(bf16[32,2,2304]{2,1,0:T(2,128)(2,1)S(1)} %all-to-all-done.1.side_ref), channel_id=1, source_target_pairs={{0,4},{4,0},{8,12},{12,8},{16,20},{20,16},{24,28},{28,24},{32,36},... | collective-permute-start | bytes 884744 | tf_op jit(solution)/shard_map/ppermute | solution.py:340

commit v7 on v6

--- a/solution.py
+++ b/solution.py
@@ -90,10 +90,29 @@
             ].astype(jnp.bfloat16)
 
 
-def lambda_kernel(gap_ref, scores_ref, clicks_ref, lengths_ref, leaf_ref, data_ref, plus_ref, minus_ref,
-                  grad_ref, side_ref, packed, flat):
+def ready_kernel(gap_ref, scores_ref, clicks_ref, lengths_ref, first_ref, second_ref, side_ref,
+                 scale_ref, held_ref):
     queries = scores_ref.shape[0]
-    discount_row = gap_ref[POS : POS + 1]
+    _, _, side, signed, ideal = query_rows(
+        scores_ref[...], clicks_ref[...], lengths_ref, queries, gap_ref[POS : POS + 1]
+    )
+    side_ref[...] = side
+    scale_ref[...] = jnp.broadcast_to(1.0 / ideal, scale_ref.shape)
+    columns = turned([signed, side])
+    for query in range(queries):
+        held_ref[query] = lengths_ref[query]
+        spread = columns[:, query : query + 1] + signed[query : query + 1]
+        cross = columns[:, queries + query : queries + query + 1] * side[query : query + 1]
+        grown = jnp.exp(spread)
+        chance = 1.0 / (1.0 + grown)
+        first = jnp.where(cross < 0.0, gap_ref[:POS] * chance, 0.0)
+        first_ref[query] = first
+        second_ref[query] = first * (grown * chance)
+
+
+def lambda_kernel(first_ref, second_ref, own_ref, scale_ref, held_ref, leaf_ref, data_ref,
+                  plus_ref, minus_ref, grad_ref, side_ref, packed, flat):
+    queries = own_ref.shape[0]
     slots = grad_ref.shape[1]
     sums = jnp.sum(data_ref[:, :, slots:].astype(jnp.float32), axis=0)
     sums = sums[0:1] + sums[1:2]
@@ -103,32 +122,24 @@
     minus = jnp.sqrt(minus_sum / minus_sum[:, 0:1])
     plus_ref[...] = plus
     minus_ref[...] = minus
-    clicked, skipped, side, signed, ideal = query_rows(
-        scores_ref[...], clicks_ref[...], lengths_ref, queries, discount_row
-    )
-    weight = jnp.where(clicked, 1.0 / plus, jnp.where(skipped, -1.0 / minus, 0.0))
-    columns = turned([signed, weight])
-    outer = jnp.abs(weight) / ideal
+    side = own_ref[...]
+    weight = jnp.where(side > 0.0, 1.0 / plus, jnp.where(side < 0.0, 1.0 / minus, 0.0))
+    columns = turned([weight])
+    outer = weight * scale_ref[...]
     packed[...] = jnp.zeros_like(packed)
     lane = lax.broadcasted_iota(jnp.int32, (1, POS), 1)
     start = jnp.int32(0)
     for query in range(queries):
-        other = columns[:, query : query + 1]
-        strength = columns[:, queries + query : queries + query + 1]
-        spread = other + signed[query : query + 1]
-        cross = jnp.maximum(strength * -side[query : query + 1], 0.0)
-        grown = jnp.exp(spread)
-        chance = 1.0 / (1.0 + grown)
-        first = cross * gap_ref[:POS] * chance
-        second = first * (grown * chance)
-        slope = jnp.sum(first, axis=0, keepdims=True) * outer[query : query + 1]
-        slope = slope * -side[query : query + 1]
-        curve = jnp.sum(second, axis=0, keepdims=True) * outer[query : query + 1]
+        strength = columns[:, query : query + 1]
+        slope = jnp.sum(strength * first_ref[query], axis=0, keepdims=True)
+        curve = jnp.sum(strength * second_ref[query], axis=0, keepdims=True)
+        slope = slope * outer[query : query + 1] * -side[query : query + 1]
+        curve = curve * outer[query : query + 1]
         grad_ref[0:1, query * POS : (query + 1) * POS] = slope
         grad_ref[1:2, query * POS : (query + 1) * POS] = curve
         group = start // POS
         shift = start - group * POS
-        length = lengths_ref[query]
+        length = held_ref[query]
         rows = jnp.concatenate(
             [slope, curve, leaf_ref[query : query + 1].astype(jnp.float32),
              jnp.zeros((5, POS), jnp.float32)], axis=0
@@ -139,12 +150,12 @@
         packed[group] = jnp.where(here, moved, packed[group])
         packed[group + 1] = jnp.where(there, moved, packed[group + 1])
         start += length
-    for tile in range(queries * POS // TILE):
-        at = 3 * POS * tile
-        for half in range(2):
-            rows = packed[2 * tile + half]
-            flat[:, at + half * POS : at + (half + 1) * POS] = rows[0:2]
-            flat[half : half + 1, at + 2 * POS : at + 3 * POS] = rows[2:3]
+    for group in range(queries):
+        rows = packed[group]
+        row = group // (queries // 2)
+        at = (queries + group % (queries // 2)) * POS
+        flat[:, group * POS : (group + 1) * POS] = rows[0:2]
+        flat[row : row + 1, at : at + POS] = rows[2:3]
     side_ref[...] = jnp.broadcast_to(flat[...].astype(jnp.bfloat16)[None], side_ref.shape)
 
 
@@ -155,26 +166,27 @@
     minus_ref[...] = minus_in[...]
     grad_ref[...] = grad_in[...]
     chips = filled_ref.shape[0] // 2
-    tiles = (list_ref.shape[0] // 2 - STEP) // chips
+    groups = (list_ref.shape[0] // 2 - 2 * STEP) // chips
     for core in range(2):
-        base = core * (chips * tiles + STEP)
+        base = core * (chips * groups + 2 * STEP)
 
         def one_block(chip, carry):
             at, spare = carry
             used = filled_ref[2 * chip + core]
-            for tile in range(tiles):
-                list_ref[base + at] = chip * 8 + tile
-                at = at + jnp.where(tile < used, 1, 0)
-            return at, jnp.where(used < tiles, chip * 8 + tiles - 1, spare)
+            for group in range(groups):
+                list_ref[base + at] = chip * 16 + group
+                at = at + jnp.where(group < used, 1, 0)
+            return at, jnp.where(used < groups, chip * 16 + groups - 1, spare)
 
         at, spare = lax.fori_loop(0, chips, one_block, (jnp.int32(0), jnp.int32(0)))
-        for extra in range(STEP):
+        for extra in range(2 * STEP):
             list_ref[base + at + extra] = spare
-        total_ref[core] = (at + STEP - 1) // STEP
+        total_ref[core] = (at + 2 * STEP - 1) // (2 * STEP)
 
 
 def accumulate(core, list_ref, total_ref, data_ref, side_ref, accs):
     base = core * (list_ref.shape[0] // 2)
+    groups = side_ref.shape[2] * 2 // (3 * POS)
     rows_a = lax.broadcasted_iota(jnp.int32, (2 * LEAVES, TILE), 0).astype(jnp.bfloat16)
     rows_b = lax.broadcasted_iota(jnp.int32, (HALF, TILE), 0).astype(jnp.bfloat16)
     zero = jnp.zeros((), jnp.bfloat16)
@@ -182,12 +194,23 @@
 
     def some_tiles(step, carry):
         for at in range(STEP):
-            entry = list_ref[base + step * STEP + at]
-            chip = lax.shift_right_logical(entry, 3)
-            tile = lax.bitwise_and(entry, 7)
-            bins = data_ref[2 * chip + core, :, pl.ds(pl.multiple_of(tile * TILE, TILE), TILE)]
-            side = side_ref[chip, :, pl.ds(pl.multiple_of(tile * 3 * POS, POS), 3 * POS)]
-            leaf = jnp.concatenate([side[0:1, TILE:], side[1:2, TILE:]], axis=1)
+            bins = []
+            sides = []
+            leaves = []
+            for half in range(2):
+                entry = list_ref[base + (step * STEP + at) * 2 + half]
+                chip = lax.shift_right_logical(entry, 4)
+                group = lax.bitwise_and(entry, 15)
+                late = group >= groups // 2
+                place = groups + group - jnp.where(late, groups // 2, 0)
+                here = pl.ds(pl.multiple_of(group * POS, POS), POS)
+                bins.append(data_ref[2 * chip + core, :, here])
+                sides.append(side_ref[chip, :, here])
+                pair = side_ref[chip, :, pl.ds(pl.multiple_of(place * POS, POS), POS)]
+                leaves.append(jnp.where(late, pair[1:2], pair[0:1]))
+            bins = jnp.concatenate(bins, axis=1)
+            side = jnp.concatenate(sides, axis=1)
+            leaf = jnp.concatenate(leaves, axis=1)
             left = []
             right = []
             for feature in range(2):
@@ -195,8 +218,8 @@
                 high = row >= jnp.asarray(HALF, jnp.bfloat16)
                 hit = jnp.where(high, leaf + jnp.asarray(LEAVES, jnp.bfloat16), leaf) == rows_a
                 low = jnp.where(high, row - jnp.asarray(HALF, jnp.bfloat16), row)
-                left.append(jnp.where(hit, side[0:1, :TILE], zero))
-                left.append(jnp.where(hit, side[1:2, :TILE], zero))
+                left.append(jnp.where(hit, side[0:1], zero))
+                left.append(jnp.where(hit, side[1:2], zero))
                 right.append(jnp.where(low == rows_b, one, zero))
             unit = at % 2
             register = (at // 2) % 2
@@ -283,7 +306,7 @@
     shards = lax.axis_size("doc")
     queries = scores.shape[0]
     slots = leaf.shape[0]
-    tiles = slots // TILE
+    groups = slots // POS
     places = np.arange(POS, dtype=np.float32)
     discount = (1.0 / np.log2(2.0 + places)).astype(np.float32)
     gap = np.abs(discount[:, None] - discount[None, :])
@@ -298,6 +321,19 @@
         name="pair_terms",
     )(gap, scores, clicks, lengths, t_plus_old[None], t_minus_old[None], bins)
     data = lax.all_to_all(sent, "doc", 0, 0, tiled=True)
+    first, second, own, scale, held = pl.pallas_call(
+        ready_kernel,
+        out_shape=(
+            pltpu.VMEM((queries, POS, POS), f32),
+            pltpu.VMEM((queries, POS, POS), f32),
+            pltpu.VMEM((queries, POS), f32),
+            pltpu.VMEM((queries, POS), f32),
+            pltpu.SMEM((queries,), jnp.int32),
+        ),
+        in_specs=[VMEM, VMEM, VMEM, SMEM],
+        out_specs=(VMEM, VMEM, VMEM, VMEM, SMEM),
+        name="ready_pairs",
+    )(gap, scores, clicks, lengths)
     t_plus, t_minus, gradients, side = pl.pallas_call(
         lambda_kernel,
         out_shape=(
@@ -306,7 +342,7 @@
             pltpu.VMEM((2, slots), f32),
             pltpu.VMEM((shards // 2, 2, 3 * slots // 2), jnp.bfloat16),
         ),
-        in_specs=[VMEM, VMEM, VMEM, SMEM, VMEM, VMEM],
+        in_specs=[VMEM, VMEM, VMEM, VMEM, SMEM, VMEM, VMEM],
         out_specs=(VMEM,) * 4,
         scratch_shapes=[
             pltpu.VMEM((queries + 1, 8, POS), f32),
@@ -314,10 +350,11 @@
         ],
         name="lambdas",
     )(
-        in_vmem(gap),
-        in_vmem(scores),
-        in_vmem(clicks),
-        in_smem(lengths),
+        in_vmem(first),
+        in_vmem(second),
+        in_vmem(own),
+        in_vmem(scale),
+        in_smem(held),
         in_vmem(leaf.reshape(queries, POS)),
         in_vmem(data),
     )
@@ -327,7 +364,7 @@
     *plan, t_plus, t_minus, gradients = pl.pallas_call(
         plan_kernel,
         out_shape=(
-            pltpu.SMEM((shards * tiles + 2 * STEP,), jnp.int32),
+            pltpu.SMEM((shards * groups + 4 * STEP,), jnp.int32),
             pltpu.SMEM((2,), jnp.int32),
             jax.ShapeDtypeStruct((1, POS), f32),
             jax.ShapeDtypeStruct((1, POS), f32),
@@ -336,7 +373,7 @@
         in_specs=[SMEM, VMEM, VMEM, VMEM],
         out_specs=(SMEM, SMEM, VMEM, VMEM, VMEM),
         name="plan",
-    )((shown + (TILE - 1)) // TILE, in_vmem(t_plus), in_vmem(t_minus), in_vmem(gradients))
+    )((shown + (POS - 1)) // POS, in_vmem(t_plus), in_vmem(t_minus), in_vmem(gradients))
     other_side = lax.ppermute(side, "doc", [(at, at ^ 1) for at in range(shards)])
     core = lax.axis_index("doc") % 2
     partial = hist_of(core.reshape(1), plan, in_vmem(data), in_vmem(side))

time: 71.6 us -> 71.6 us (level)
  blocking collectives: 29.4 us -> 0 us
  waiting for transfers between devices: 12.1 us -> 26.8 us
  starting transfers between devices: 6.63 us -> 19.8 us
  Pallas kernels: 21.2 us -> 22.7 us
    all_to_all x1 -> x0, blocking collectives: 29.4 us -> none  [body(): data = lax.all_to_all(sent, 'doc', 0, 0, tiled=True)]
    all_to_all x0 -> x1, waiting for transfers between devices: none -> 14.7 us  [body(): data = lax.all_to_all(sent, 'doc', 0, 0, tiled=True)]
    all_to_all x0 -> x1, starting transfers between devices: none -> 13.1 us  [body(): data = lax.all_to_all(sent, 'doc', 0, 0, tiled=True)]
    pallas_call x1 -> x2, Pallas kernels: 2.3 us -> 4.87 us  [the longest x1 3.26 us: body(): pl.pallas_call(plan_kernel, out_shape=(pltpu.SMEM((shards * groups + 4 *...]
    pallas_call x1, Pallas kernels: 2.62 us -> 1.48 us  [body(): pl.pallas_call(lambda_kernel, out_shape=(pltpu.VMEM((1, POS), f32), pltpu...]
    pallas_call x1, Pallas kernels: 2.56 us -> 3.33 us  [body(): pl.pallas_call(pair_kernel, out_shape=pltpu.VMEM((shards, 2, slots + 2 *...]
  transfers between devices with their start and end apart: 2 -> 3, of which waited for: 1 -> 2; matrix products, arithmetic and copies ran while one was open for 2% -> 2% of each run, Pallas kernels for 12% -> 16%
where the time goes in v7:
time: 71.6 us; the launch traced here: 71.3 us
  waiting for transfers between devices  26.8 us (37%)
  Pallas kernels  22.7 us (32%)
  starting transfers between devices  19.8 us (28%)
  other arithmetic  1.27 us (2%)
    all_to_all x1, waiting for transfers between devices, body(): data = lax.all_to_all(sent, 'doc', 0, 0, tiled=True)  14.7 us
    all_to_all x1, starting transfers between devices, body(): data = lax.all_to_all(sent, 'doc', 0, 0, tiled=True)  13.1 us
    all_to_all x1, waiting for transfers between devices, body(): lax.all_to_all(side, 'doc', 0, 0, axis_index_groups=same_core, tiled=True)  12 us
    pallas_call x1, Pallas kernels, hist_of(): pl.pallas_call(second_kernel, out_shape=jax.ShapeDtypeStruct((2, 2 * LEAV...  6.86 us
    pallas_call x1, Pallas kernels, hist_of(): pl.pallas_call(first_kernel, out_shape=pltpu.VMEM(part, jnp.float32), in_...  6.19 us
    all_to_all x1, starting transfers between devices, body(): lax.all_to_all(side, 'doc', 0, 0, axis_index_groups=same_core, tiled=True)  4.45 us
    pallas_call x1, Pallas kernels, body(): pl.pallas_call(pair_kernel, out_shape=pltpu.VMEM((shards, 2, slots + 2 *...  3.33 us
    pallas_call x1, Pallas kernels, body(): pl.pallas_call(plan_kernel, out_shape=(pltpu.SMEM((shards * groups + 4 *...  3.26 us
  transfers between devices with their start and end apart: 3, of which 2 were waited for; matrix products, arithmetic and copies ran while one was open for 2% of the time, Pallas kernels for 16%

profile of v7, /device:TPU:1, one launch (start us, length us, event | category | flops | bytes accessed | tf_op | source)
XLA Modules:
  0.0 71.3 jit_solution(11967887534451667795)
XLA Ops:
  0.6 3.3 %pair_terms.1 = bf16[64,2,1792]{2,1,0:T(2,128)(2,1)} custom-call(f32[136,128]{1,0:T(8,128)} %constant.41.clone.gap_ref, f32[12,128]{1,0:T(8,128)} %scores_ref.3, s32[12,128]{1,0:T(8,128)} %clicks_ref.3, s32[12]{0:T(128)} %lengths_ref.3, f32[1,128]{1,0:T(1,128)} %bitcast.8, f32[1,128]{1,0:T(1,128)} %bitcast.9, s32[128,1536]{1,0:T(8,128)} %bins_ref.1), custom_call_target="tpu_custom_call" | custom-call | tf_op jit(solution)/shard_map/pair_terms/pallas_call | solution.py:315
  4.0 13.1 %all-to-all-start = ((bf16[64,2,1792]{2,1,0:T(2,128)(2,1)}), bf16[64,2,1792]{2,1,0:T(2,128)(2,1)S(1)}, u32[]{:S(2)}, u32[]{:S(2)}) async-start(bf16[64,2,1792]{2,1,0:T(2,128)(2,1)} %pair_terms.1), calls=%async_computation | async-start | bytes 917504 | tf_op jit(solution)/shard_map/all_to_all | solution.py:323
  17.1 1.6 %ready_pairs.1 = (f32[12,128,128]{2,1,0:T(8,128)S(1)}, f32[12,128,128]{2,1,0:T(8,128)S(1)}, f32[12,128]{1,0:T(8,128)S(1)}, f32[12,128]{1,0:T(8,128)S(1)}, s32[12]{0:T(128)S(4)}) custom-call(f32[136,128]{1,0:T(8,128)} %constant.41.clone.gap_ref, f32[12,128]{1,0:T(8,128)} %scores_ref.3, s32[12,128]{1,0:T(8,128)} %clicks_ref.3, s32[12]{0:T(128)} %lengths_ref.3), custom_call_target="tpu_custom_call" | custom-call | tf_op jit(solution)/shard_map/ready_pairs/pallas_call | solution.py:324
  18.7 0.0 copy-start
  18.7 14.7 %all-to-all-done.data_ref = bf16[64,2,1792]{2,1,0:T(2,128)(2,1)S(1)} async-done(((bf16[64,2,1792]{2,1,0:T(2,128)(2,1)}), bf16[64,2,1792]{2,1,0:T(2,128)(2,1)S(1)}, u32[]{:S(2)}, u32[]{:S(2)}) %all-to-all-start) | async-done | bytes 458784 | tf_op jit(solution)/shard_map/all_to_all | solution.py:323
  33.5 0.0 copy-done
  33.5 1.5 %lambdas.1 = (f32[1,128]{1,0:T(1,128)S(1)}, f32[1,128]{1,0:T(1,128)S(1)}, f32[2,1536]{1,0:T(2,128)S(1)}, bf16[32,2,2304]{2,1,0:T(2,128)(2,1)}) custom-call(f32[12,128,128]{2,1,0:T(8,128)S(1)} %get-tuple-element.18.first_ref, f32[12,128,128]{2,1,0:T(8,128)S(1)} %get-tuple-element.19.second_ref, f32[12,128]{1,0:T(8,128)S(1)} %get-tuple-element.20.own_ref, ...), custom_call_target="tpu_custom_call" | custom-call | tf_op jit(solution)/shard_map/lambdas/pallas_call | solution.py:337
  35.0 4.4 %all-to-all-start.1 = ((bf16[32,2,2304]{2,1,0:T(2,128)(2,1)}), bf16[32,2,2304]{2,1,0:T(2,128)(2,1)S(1)}, u32[]{:S(2)}, u32[]{:S(2)}) async-start(bf16[32,2,2304]{2,1,0:T(2,128)(2,1)} %get-tuple-element.31), calls=%async_computation.1 | async-start | bytes 589824 | tf_op jit(solution)/shard_map/all_to_all | solution.py:362
  39.4 12.0 %all-to-all-done.1.side_ref = bf16[32,2,2304]{2,1,0:T(2,128)(2,1)S(1)} async-done(((bf16[32,2,2304]{2,1,0:T(2,128)(2,1)}), bf16[32,2,2304]{2,1,0:T(2,128)(2,1)S(1)}, u32[]{:S(2)}, u32[]{:S(2)}) %all-to-all-start.1) | async-done | bytes 294944 | tf_op jit(solution)/shard_map/all_to_all | solution.py:362
  51.5 2.2 %collective-permute-start = (bf16[32,2,2304]{2,1,0:T(2,128)(2,1)S(1)}, bf16[32,2,2304]{2,1,0:T(2,128)(2,1)S(1)}, u32[]{:S(2)}, u32[]{:S(2)}) collective-permute-start(bf16[32,2,2304]{2,1,0:T(2,128)(2,1)S(1)} %all-to-all-done.1.side_ref), channel_id=1, source_target_pairs={{0,4},{4,0},{8,12},{12,8},{16,20},{20,16},{24,28},{28,24},{32,36},... | collective-permute-start | bytes 884744 | tf_op jit(solution)/shard_map/ppermute | solution.py:377
  53.7 0.7 %fusion = f32[64]{0:T(128)S(1)} fusion(bf16[64,2,1792]{2,1,0:T(2,128)(2,1)S(1)} %all-to-all-done.data_ref), kind=kLoop, calls=%fused_computation.1 | loop fusion | flops 294848 | bytes 196864 | tf_op jit(solution)/shard_map/reduce_sum | solution.py:363
  54.4 0.5 and_select_fusion.filled_ref
  54.9 3.3 %plan.1 = (s32[800]{0:T(1024)S(4)}, s32[2]{0:T(128)S(4)}, f32[1,128]{1,0:T(1,128)}, f32[1,128]{1,0:T(1,128)}, f32[2,1536]{1,0:T(2,128)}) custom-call(s32[64]{0:T(128)} %and_select_fusion.filled_ref, f32[1,128]{1,0:T(1,128)S(1)} %get-tuple-element.23.plus_in, f32[1,128]{1,0:T(1,128)S(1)} %get-tuple-element.24.minus_in, f32[2,1536]{1,0:T(2,128)S(1)} %get-tuple-element.25.grad_in), custom_call_target="tpu_custom_call" | custom-call | tf_op jit(solution)/shard_map/plan/pallas_call | solution.py:364
  58.2 6.2 %first_half.1.before_ref = f32[2,128,128]{2,1,0:T(8,128)S(1)} custom-call(s32[1]{0:T(128)} %bitcast.6.core_ref, s32[800]{0:T(1024)S(4)} %get-tuple-element.29.list_ref, s32[2]{0:T(128)S(4)} %get-tuple-element.30.total_ref, bf16[64,2,1792]{2,1,0:T(2,128)(2,1)S(1)} %all-to-all-done.data_ref, bf16[32,2,2304]{2,1,0:T(2,128)(2,1)S(1)} %all-to-all-done.1.side_ref), custom_call_target="tpu_custom_call" | custom-call | tf_op jit(solution)/shard_map/first_half/pallas_call | solution.py:289
  64.4 0.0 collective-permute-done.side_ref
  64.4 6.9 %second_half.1 = f32[2,64,256]{2,1,0:T(8,128)} custom-call(s32[1]{0:T(128)} %bitcast.5.core_ref, s32[800]{0:T(1024)S(4)} %get-tuple-element.29.list_ref, s32[2]{0:T(128)S(4)} %get-tuple-element.30.total_ref, bf16[64,2,1792]{2,1,0:T(2,128)(2,1)S(1)} %all-to-all-done.data_ref, bf16[32,2,2304]{2,1,0:T(2,128)(2,1)S(1)} %collective-permute-done.side_ref, ...), custom_call_target="tpu_custom_call" | custom-call | tf_op jit(solution)/shard_map/second_half/pallas_call | solution.py:296
Async XLA Ops:
  4.0 29.5 %all-to-all-start = ((bf16[64,2,1792]{2,1,0:T(2,128)(2,1)}), bf16[64,2,1792]{2,1,0:T(2,128)(2,1)S(1)}, u32[]{:S(2)}, u32[]{:S(2)}) async-start(bf16[64,2,1792]{2,1,0:T(2,128)(2,1)} %pair_terms.1), calls=%async_computation | async-start | bytes 917504 | tf_op jit(solution)/shard_map/all_to_all | solution.py:323
  18.7 14.8 %copy-start = (s32[1536]{0:T(1024)S(1)}, s32[1536]{0:T(1024)}, u32[]{:S(2)}) copy-start(s32[1536]{0:T(1024)} %param.13) | copy-start | bytes 18436
  35.0 16.5 %all-to-all-start.1 = ((bf16[32,2,2304]{2,1,0:T(2,128)(2,1)}), bf16[32,2,2304]{2,1,0:T(2,128)(2,1)S(1)}, u32[]{:S(2)}, u32[]{:S(2)}) async-start(bf16[32,2,2304]{2,1,0:T(2,128)(2,1)} %get-tuple-element.31), calls=%async_computation.1 | async-start | bytes 589824 | tf_op jit(solution)/shard_map/all_to_all | solution.py:362
  51.5 12.9 %collective-permute-start = (bf16[32,2,2304]{2,1,0:T(2,128)(2,1)S(1)}, bf16[32,2,2304]{2,1,0:T(2,128)(2,1)S(1)}, u32[]{:S(2)}, u32[]{:S(2)}) collective-permute-start(bf16[32,2,2304]{2,1,0:T(2,128)(2,1)S(1)} %all-to-all-done.1.side_ref), channel_id=1, source_target_pairs={{0,4},{4,0},{8,12},{12,8},{16,20},{20,16},{24,28},{28,24},{32,36},... | collective-permute-start | bytes 884744 | tf_op jit(solution)/shard_map/ppermute | solution.py:377

commit v8 on v7

--- a/solution.py
+++ b/solution.py
@@ -12,7 +12,8 @@
 POS = 128
 HALF = BINS // 2
 TILE = 256
-STEP = 8
+STEP = 4
+WIDE = 4
 
 
 def query_rows(scores, clicks, lengths_ref, queries, discount_row):
@@ -39,19 +40,20 @@
     return jnp.transpose(jnp.concatenate(list(rows) + [pad], axis=0))
 
 
-def pair_kernel(gap_ref, scores_ref, clicks_ref, lengths_ref, plus_ref, minus_ref, bins_ref,
-                sent_ref, packed):
+def pair_kernel(gap_ref, scores_ref, clicks_ref, lengths_ref, plus_ref, minus_ref, bins_from,
+                sent_to, bins_ref, sent_ref, packed, took, gave):
+    take = pltpu.make_async_copy(bins_from, bins_ref, took)
+    take.start()
     queries = scores_ref.shape[0]
-    discount_row = gap_ref[POS : POS + 1]
     clicked, skipped, side, signed, ideal = query_rows(
-        scores_ref[...], clicks_ref[...], lengths_ref, queries, discount_row
+        scores_ref[...], clicks_ref[...], lengths_ref, queries, gap_ref[POS : POS + 1]
     )
     weight = jnp.where(clicked, 1.0 / plus_ref[...], jnp.where(skipped, -1.0 / minus_ref[...], 0.0))
     columns = turned([signed, weight])
     scale = 1.0 / ideal
-    plus = jnp.zeros((1, POS), jnp.float32)
-    minus = jnp.zeros((1, POS), jnp.float32)
-    for query in range(queries):
+    sums = [jnp.zeros((1, POS), jnp.float32), jnp.zeros((1, POS), jnp.float32)]
+
+    def add_query(query):
         other = columns[:, query : query + 1]
         strength = columns[:, queries + query : queries + query + 1]
         spread = other + signed[query : query + 1]
@@ -59,16 +61,15 @@
         loss = jnp.maximum(-spread, 0.0) + jnp.log1p(jnp.exp(-jnp.abs(spread)))
         total = jnp.sum(cross * gap_ref[:POS] * loss, axis=0, keepdims=True)
         total = total * scale[query : query + 1]
-        plus += jnp.where(side[query : query + 1] > 0.0, total, 0.0)
-        minus += jnp.where(side[query : query + 1] < 0.0, total, 0.0)
+        sums[0] += jnp.where(side[query : query + 1] > 0.0, total, 0.0)
+        sums[1] += jnp.where(side[query : query + 1] < 0.0, total, 0.0)
+
+    for query in range(queries // 2):
+        add_query(query)
+
     features, slots = bins_ref.shape
-    for at, part in enumerate((plus, minus)):
-        high = part.astype(jnp.bfloat16).astype(jnp.float32)
-        pieces = jnp.concatenate([high, part - high], axis=0).astype(jnp.bfloat16)
-        sent_ref[:, :, slots + at * POS : slots + (at + 1) * POS] = jnp.broadcast_to(
-            pieces[None], (features // 2, 2, POS)
-        )
     packed[...] = jnp.full(packed.shape, -1.0, jnp.float32)
+    take.wait()
     lane = lax.broadcasted_iota(jnp.int32, (1, POS), 1)
     start = jnp.int32(0)
     for query in range(queries):
@@ -88,6 +89,24 @@
             sent_ref[owner, :, group * POS : (group + 1) * POS] = packed[
                 group, 2 * owner : 2 * owner + 2
             ].astype(jnp.bfloat16)
+    bulk = pl.ds(0, slots)
+    give = pltpu.make_async_copy(sent_ref.at[:, :, bulk], sent_to.at[:, :, bulk], gave.at[0])
+    give.start()
+    for query in range(queries // 2, queries):
+        add_query(query)
+    for at, part in enumerate(sums):
+        high = part.astype(jnp.bfloat16).astype(jnp.float32)
+        pieces = jnp.concatenate([high, part - high], axis=0).astype(jnp.bfloat16)
+        sent_ref[:, :, slots + at * POS : slots + (at + 1) * POS] = jnp.broadcast_to(
+            pieces[None], (features // 2, 2, POS)
+        )
+    small = pl.ds(slots, 2 * POS)
+    give_sums = pltpu.make_async_copy(
+        sent_ref.at[:, :, small], sent_to.at[:, :, small], gave.at[1]
+    )
+    give_sums.start()
+    give.wait()
+    give_sums.wait()
 
 
 def ready_kernel(gap_ref, scores_ref, clicks_ref, lengths_ref, first_ref, second_ref, side_ref,
@@ -192,13 +211,13 @@
     zero = jnp.zeros((), jnp.bfloat16)
     one = jnp.ones((), jnp.bfloat16)
 
-    def some_tiles(step, carry):
-        for at in range(STEP):
+    def tiles_at(first, count):
+        for at in range(count):
             bins = []
             sides = []
             leaves = []
             for half in range(2):
-                entry = list_ref[base + (step * STEP + at) * 2 + half]
+                entry = list_ref[base + (first + at) * 2 + half]
                 chip = lax.shift_right_logical(entry, 4)
                 group = lax.bitwise_and(entry, 15)
                 late = group >= groups // 2
@@ -225,9 +244,19 @@
             register = (at // 2) % 2
             pltpu.matmul_push_rhs(jnp.concatenate(right, axis=0), register, unit, transpose=True)
             pltpu.matmul_acc_lhs(accs[unit], jnp.concatenate(left, axis=0), register)
+
+    def wide_step(step, carry):
+        tiles_at(step * (STEP * WIDE), STEP * WIDE)
         return carry
 
-    lax.fori_loop(0, total_ref[core], some_tiles, 0)
+    def step(step, carry):
+        tiles_at(step * STEP, STEP)
+        return carry
+
+    total = total_ref[core]
+    wide = total // WIDE
+    lax.fori_loop(0, wide, wide_step, 0)
+    lax.fori_loop(wide * WIDE, total, step, 0)
 
 
 def summed(core, list_ref, total_ref, data_ref, side_ref, finish):
@@ -312,12 +341,19 @@
     gap = np.abs(discount[:, None] - discount[None, :])
     gap = jnp.asarray(np.concatenate([gap, np.tile(discount[None], (8, 1))]))
     f32 = jnp.float32
+    sent_shape = (shards, 2, slots + 2 * POS)
     sent = pl.pallas_call(
         pair_kernel,
-        out_shape=pltpu.VMEM((shards, 2, slots + 2 * POS), jnp.bfloat16),
-        in_specs=[VMEM, VMEM, VMEM, SMEM, VMEM, VMEM, VMEM],
-        out_specs=VMEM,
-        scratch_shapes=[pltpu.VMEM((slots // POS + 1, bins.shape[0], POS), f32)],
+        out_shape=jax.ShapeDtypeStruct(sent_shape, jnp.bfloat16),
+        in_specs=[VMEM, VMEM, VMEM, SMEM, VMEM, VMEM, pl.BlockSpec(memory_space=pl.ANY)],
+        out_specs=pl.BlockSpec(memory_space=pl.ANY),
+        scratch_shapes=[
+            pltpu.VMEM(bins.shape, jnp.int32),
+            pltpu.VMEM(sent_shape, jnp.bfloat16),
+            pltpu.VMEM((slots // POS + 1, bins.shape[0], POS), f32),
+            pltpu.SemaphoreType.DMA,
+            pltpu.SemaphoreType.DMA((2,)),
+        ],
         name="pair_terms",
     )(gap, scores, clicks, lengths, t_plus_old[None], t_minus_old[None], bins)
     data = lax.all_to_all(sent, "doc", 0, 0, tiled=True)

time: 71.6 us -> 70.7 us (0.987)
  Pallas kernels: 22.7 us -> 21.7 us
  transfers between devices with their start and end apart: 3 -> 3, of which waited for: 2 -> 2; matrix products, arithmetic and copies ran while one was open for 2% -> 2% of each run, Pallas kernels for 16% -> 15%
where the time goes in v8:
time: 70.7 us; the launch traced here: 70.3 us
  waiting for transfers between devices  26.8 us (38%)
  Pallas kernels  21.7 us (31%)
  starting transfers between devices  19.8 us (28%)
  other arithmetic  1.27 us (2%)
    all_to_all x1, waiting for transfers between devices, body(): data = lax.all_to_all(sent, 'doc', 0, 0, tiled=True)  14.7 us
    all_to_all x1, starting transfers between devices, body(): data = lax.all_to_all(sent, 'doc', 0, 0, tiled=True)  13.2 us
    all_to_all x1, waiting for transfers between devices, body(): lax.all_to_all(side, 'doc', 0, 0, axis_index_groups=same_core, tiled=True)  12 us
    pallas_call x1, Pallas kernels, hist_of(): pl.pallas_call(second_kernel, out_shape=jax.ShapeDtypeStruct((2, 2 * LEAV...  6.17 us
    pallas_call x1, Pallas kernels, hist_of(): pl.pallas_call(first_kernel, out_shape=pltpu.VMEM(part, jnp.float32), in_...  5.5 us
    all_to_all x1, starting transfers between devices, body(): lax.all_to_all(side, 'doc', 0, 0, axis_index_groups=same_core, tiled=True)  4.45 us
    pallas_call x1, Pallas kernels, body(): pl.pallas_call(pair_kernel, out_shape=jax.ShapeDtypeStruct(sent_shape, jn...  3.7 us
    pallas_call x1, Pallas kernels, body(): pl.pallas_call(plan_kernel, out_shape=(pltpu.SMEM((shards * groups + 4 *...  3.25 us
  transfers between devices with their start and end apart: 3, of which 2 were waited for; matrix products, arithmetic and copies ran while one was open for 2% of the time, Pallas kernels for 15%

profile of v8, /device:TPU:1, one launch (start us, length us, event | category | flops | bytes accessed | tf_op | source)
XLA Modules:
  0.0 70.3 jit_solution(10939705566832555922)
XLA Ops:
  0.6 3.7 %pair_terms.1 = bf16[64,2,1792]{2,1,0:T(2,128)(2,1)} custom-call(f32[136,128]{1,0:T(8,128)} %constant.41.clone.gap_ref, f32[12,128]{1,0:T(8,128)} %scores_ref.3, s32[12,128]{1,0:T(8,128)} %clicks_ref.3, s32[12]{0:T(128)} %lengths_ref.3, f32[1,128]{1,0:T(1,128)} %bitcast.8, f32[1,128]{1,0:T(1,128)} %bitcast.9, s32[128,1536]{1,0:T(8,128)} %bins_from.1), custom_call_target="tpu_custom_call" | custom-call | tf_op jit(solution)/shard_map/pair_terms/pallas_call | solution.py:345
  4.3 13.2 %all-to-all-start = ((bf16[64,2,1792]{2,1,0:T(2,128)(2,1)}), bf16[64,2,1792]{2,1,0:T(2,128)(2,1)S(1)}, u32[]{:S(2)}, u32[]{:S(2)}) async-start(bf16[64,2,1792]{2,1,0:T(2,128)(2,1)} %pair_terms.1), calls=%async_computation | async-start | bytes 917504 | tf_op jit(solution)/shard_map/all_to_all | solution.py:359
  17.5 1.6 %ready_pairs.1 = (f32[12,128,128]{2,1,0:T(8,128)S(1)}, f32[12,128,128]{2,1,0:T(8,128)S(1)}, f32[12,128]{1,0:T(8,128)S(1)}, f32[12,128]{1,0:T(8,128)S(1)}, s32[12]{0:T(128)S(4)}) custom-call(f32[136,128]{1,0:T(8,128)} %constant.41.clone.gap_ref, f32[12,128]{1,0:T(8,128)} %scores_ref.3, s32[12,128]{1,0:T(8,128)} %clicks_ref.3, s32[12]{0:T(128)} %lengths_ref.3), custom_call_target="tpu_custom_call" | custom-call | tf_op jit(solution)/shard_map/ready_pairs/pallas_call | solution.py:360
  19.1 0.0 copy-start
  19.1 14.7 %all-to-all-done.data_ref = bf16[64,2,1792]{2,1,0:T(2,128)(2,1)S(1)} async-done(((bf16[64,2,1792]{2,1,0:T(2,128)(2,1)}), bf16[64,2,1792]{2,1,0:T(2,128)(2,1)S(1)}, u32[]{:S(2)}, u32[]{:S(2)}) %all-to-all-start) | async-done | bytes 458784 | tf_op jit(solution)/shard_map/all_to_all | solution.py:359
  33.9 0.0 copy-done
  33.9 1.5 %lambdas.1 = (f32[1,128]{1,0:T(1,128)S(1)}, f32[1,128]{1,0:T(1,128)S(1)}, f32[2,1536]{1,0:T(2,128)S(1)}, bf16[32,2,2304]{2,1,0:T(2,128)(2,1)}) custom-call(f32[12,128,128]{2,1,0:T(8,128)S(1)} %get-tuple-element.18.first_ref, f32[12,128,128]{2,1,0:T(8,128)S(1)} %get-tuple-element.19.second_ref, f32[12,128]{1,0:T(8,128)S(1)} %get-tuple-element.20.own_ref, ...), custom_call_target="tpu_custom_call" | custom-call | tf_op jit(solution)/shard_map/lambdas/pallas_call | solution.py:373
  35.4 4.4 %all-to-all-start.1 = ((bf16[32,2,2304]{2,1,0:T(2,128)(2,1)}), bf16[32,2,2304]{2,1,0:T(2,128)(2,1)S(1)}, u32[]{:S(2)}, u32[]{:S(2)}) async-start(bf16[32,2,2304]{2,1,0:T(2,128)(2,1)} %get-tuple-element.31), calls=%async_computation.1 | async-start | bytes 589824 | tf_op jit(solution)/shard_map/all_to_all | solution.py:398
  39.8 12.0 %all-to-all-done.1.side_ref = bf16[32,2,2304]{2,1,0:T(2,128)(2,1)S(1)} async-done(((bf16[32,2,2304]{2,1,0:T(2,128)(2,1)}), bf16[32,2,2304]{2,1,0:T(2,128)(2,1)S(1)}, u32[]{:S(2)}, u32[]{:S(2)}) %all-to-all-start.1) | async-done | bytes 294944 | tf_op jit(solution)/shard_map/all_to_all | solution.py:398
  51.9 2.2 %collective-permute-start = (bf16[32,2,2304]{2,1,0:T(2,128)(2,1)S(1)}, bf16[32,2,2304]{2,1,0:T(2,128)(2,1)S(1)}, u32[]{:S(2)}, u32[]{:S(2)}) collective-permute-start(bf16[32,2,2304]{2,1,0:T(2,128)(2,1)S(1)} %all-to-all-done.1.side_ref), channel_id=1, source_target_pairs={{0,4},{4,0},{8,12},{12,8},{16,20},{20,16},{24,28},{28,24},{32,36},... | collective-permute-start | bytes 884744 | tf_op jit(solution)/shard_map/ppermute | solution.py:413
  54.1 0.7 %fusion = f32[64]{0:T(128)S(1)} fusion(bf16[64,2,1792]{2,1,0:T(2,128)(2,1)S(1)} %all-to-all-done.data_ref), kind=kLoop, calls=%fused_computation.1 | loop fusion | flops 294848 | bytes 196864 | tf_op jit(solution)/shard_map/reduce_sum | solution.py:399
  54.8 0.5 and_select_fusion.filled_ref
  55.3 3.3 %plan.1 = (s32[784]{0:T(1024)S(4)}, s32[2]{0:T(128)S(4)}, f32[1,128]{1,0:T(1,128)}, f32[1,128]{1,0:T(1,128)}, f32[2,1536]{1,0:T(2,128)}) custom-call(s32[64]{0:T(128)} %and_select_fusion.filled_ref, f32[1,128]{1,0:T(1,128)S(1)} %get-tuple-element.23.plus_in, f32[1,128]{1,0:T(1,128)S(1)} %get-tuple-element.24.minus_in, f32[2,1536]{1,0:T(2,128)S(1)} %get-tuple-element.25.grad_in), custom_call_target="tpu_custom_call" | custom-call | tf_op jit(solution)/shard_map/plan/pallas_call | solution.py:400
  58.6 5.5 %first_half.1.before_ref = f32[2,128,128]{2,1,0:T(8,128)S(1)} custom-call(s32[1]{0:T(128)} %bitcast.6.core_ref, s32[784]{0:T(1024)S(4)} %get-tuple-element.29.list_ref, s32[2]{0:T(128)S(4)} %get-tuple-element.30.total_ref, bf16[64,2,1792]{2,1,0:T(2,128)(2,1)S(1)} %all-to-all-done.data_ref, bf16[32,2,2304]{2,1,0:T(2,128)(2,1)S(1)} %all-to-all-done.1.side_ref), custom_call_target="tpu_custom_call" | custom-call | tf_op jit(solution)/shard_map/first_half/pallas_call | solution.py:318
  64.1 0.0 collective-permute-done.side_ref
  64.1 6.2 %second_half.1 = f32[2,64,256]{2,1,0:T(8,128)} custom-call(s32[1]{0:T(128)} %bitcast.5.core_ref, s32[784]{0:T(1024)S(4)} %get-tuple-element.29.list_ref, s32[2]{0:T(128)S(4)} %get-tuple-element.30.total_ref, bf16[64,2,1792]{2,1,0:T(2,128)(2,1)S(1)} %all-to-all-done.data_ref, bf16[32,2,2304]{2,1,0:T(2,128)(2,1)S(1)} %collective-permute-done.side_ref, ...), custom_call_target="tpu_custom_call" | custom-call | tf_op jit(solution)/shard_map/second_half/pallas_call | solution.py:325
Async XLA Ops:
  4.3 29.5 %all-to-all-start = ((bf16[64,2,1792]{2,1,0:T(2,128)(2,1)}), bf16[64,2,1792]{2,1,0:T(2,128)(2,1)S(1)}, u32[]{:S(2)}, u32[]{:S(2)}) async-start(bf16[64,2,1792]{2,1,0:T(2,128)(2,1)} %pair_terms.1), calls=%async_computation | async-start | bytes 917504 | tf_op jit(solution)/shard_map/all_to_all | solution.py:359
  19.1 14.8 %copy-start = (s32[1536]{0:T(1024)S(1)}, s32[1536]{0:T(1024)}, u32[]{:S(2)}) copy-start(s32[1536]{0:T(1024)} %param.13) | copy-start | bytes 18436
  35.4 16.5 %all-to-all-start.1 = ((bf16[32,2,2304]{2,1,0:T(2,128)(2,1)}), bf16[32,2,2304]{2,1,0:T(2,128)(2,1)S(1)}, u32[]{:S(2)}, u32[]{:S(2)}) async-start(bf16[32,2,2304]{2,1,0:T(2,128)(2,1)} %get-tuple-element.31), calls=%async_computation.1 | async-start | bytes 589824 | tf_op jit(solution)/shard_map/all_to_all | solution.py:398
  51.9 12.2 %collective-permute-start = (bf16[32,2,2304]{2,1,0:T(2,128)(2,1)S(1)}, bf16[32,2,2304]{2,1,0:T(2,128)(2,1)S(1)}, u32[]{:S(2)}, u32[]{:S(2)}) collective-permute-start(bf16[32,2,2304]{2,1,0:T(2,128)(2,1)S(1)} %all-to-all-done.1.side_ref), channel_id=1, source_target_pairs={{0,4},{4,0},{8,12},{12,8},{16,20},{20,16},{24,28},{28,24},{32,36},... | collective-permute-start | bytes 884744 | tf_op jit(solution)/shard_map/ppermute | solution.py:413

commit v9 on v8

--- a/solution.py
+++ b/solution.py
@@ -64,10 +64,17 @@
         sums[0] += jnp.where(side[query : query + 1] > 0.0, total, 0.0)
         sums[1] += jnp.where(side[query : query + 1] < 0.0, total, 0.0)
 
-    for query in range(queries // 2):
+    for query in range(queries):
         add_query(query)
 
     features, slots = bins_ref.shape
+    owners = features // 2
+    for at, part in enumerate(sums):
+        high = part.astype(jnp.bfloat16).astype(jnp.float32)
+        pieces = jnp.concatenate([high, part - high], axis=0).astype(jnp.bfloat16)
+        sent_ref[:, :, slots + at * POS : slots + (at + 1) * POS] = jnp.broadcast_to(
+            pieces[None], (owners, 2, POS)
+        )
     packed[...] = jnp.full(packed.shape, -1.0, jnp.float32)
     take.wait()
     lane = lax.broadcasted_iota(jnp.int32, (1, POS), 1)
@@ -84,29 +91,20 @@
         packed[group] = jnp.where(here, moved, packed[group])
         packed[group + 1] = jnp.where(there, moved, packed[group + 1])
         start += length
-    for group in range(slots // POS):
-        for owner in range(features // 2):
-            sent_ref[owner, :, group * POS : (group + 1) * POS] = packed[
-                group, 2 * owner : 2 * owner + 2
-            ].astype(jnp.bfloat16)
-    bulk = pl.ds(0, slots)
-    give = pltpu.make_async_copy(sent_ref.at[:, :, bulk], sent_to.at[:, :, bulk], gave.at[0])
-    give.start()
-    for query in range(queries // 2, queries):
-        add_query(query)
-    for at, part in enumerate(sums):
-        high = part.astype(jnp.bfloat16).astype(jnp.float32)
-        pieces = jnp.concatenate([high, part - high], axis=0).astype(jnp.bfloat16)
-        sent_ref[:, :, slots + at * POS : slots + (at + 1) * POS] = jnp.broadcast_to(
-            pieces[None], (features // 2, 2, POS)
-        )
-    small = pl.ds(slots, 2 * POS)
-    give_sums = pltpu.make_async_copy(
-        sent_ref.at[:, :, small], sent_to.at[:, :, small], gave.at[1]
-    )
-    give_sums.start()
-    give.wait()
-    give_sums.wait()
+    chunks = gave.shape[0]
+    gives = []
+    for chunk in range(chunks):
+        first = chunk * owners // chunks
+        for owner in range(first, first + owners // chunks):
+            for group in range(slots // POS):
+                sent_ref[owner, :, group * POS : (group + 1) * POS] = packed[
+                    group, 2 * owner : 2 * owner + 2
+                ].astype(jnp.bfloat16)
+        some = pl.ds(first, owners // chunks)
+        gives.append(pltpu.make_async_copy(sent_ref.at[some], sent_to.at[some], gave.at[chunk]))
+        gives[-1].start()
+    for give in gives:
+        give.wait()
 
 
 def ready_kernel(gap_ref, scores_ref, clicks_ref, lengths_ref, first_ref, second_ref, side_ref,
@@ -352,7 +350,7 @@
             pltpu.VMEM(sent_shape, jnp.bfloat16),
             pltpu.VMEM((slots // POS + 1, bins.shape[0], POS), f32),
             pltpu.SemaphoreType.DMA,
-            pltpu.SemaphoreType.DMA((2,)),
+            pltpu.SemaphoreType.DMA((4,)),
         ],
         name="pair_terms",
     )(gap, scores, clicks, lengths, t_plus_old[None], t_minus_old[None], bins)

time: 70.7 us -> 70.3 us (level)
  no operation moved by 1% of the time
where the time goes in v9:
time: 70.3 us; the launch traced here: 69.9 us
  waiting for transfers between devices  26.8 us (38%)
  Pallas kernels  21.3 us (30%)
  starting transfers between devices  19.8 us (28%)
  other arithmetic  1.27 us (2%)
    all_to_all x1, waiting for transfers between devices, body(): data = lax.all_to_all(sent, 'doc', 0, 0, tiled=True)  14.7 us
    all_to_all x1, starting transfers between devices, body(): data = lax.all_to_all(sent, 'doc', 0, 0, tiled=True)  13.2 us
    all_to_all x1, waiting for transfers between devices, body(): lax.all_to_all(side, 'doc', 0, 0, axis_index_groups=same_core, tiled=True)  12 us
    pallas_call x1, Pallas kernels, hist_of(): pl.pallas_call(second_kernel, out_shape=jax.ShapeDtypeStruct((2, 2 * LEAV...  6.17 us
    pallas_call x1, Pallas kernels, hist_of(): pl.pallas_call(first_kernel, out_shape=pltpu.VMEM(part, jnp.float32), in_...  5.5 us
    all_to_all x1, starting transfers between devices, body(): lax.all_to_all(side, 'doc', 0, 0, axis_index_groups=same_core, tiled=True)  4.45 us
    pallas_call x1, Pallas kernels, body(): pl.pallas_call(pair_kernel, out_shape=jax.ShapeDtypeStruct(sent_shape, jn...  3.3 us
    pallas_call x1, Pallas kernels, body(): pl.pallas_call(plan_kernel, out_shape=(pltpu.SMEM((shards * groups + 4 *...  3.25 us
  transfers between devices with their start and end apart: 3, of which 2 were waited for; matrix products, arithmetic and copies ran while one was open for 2% of the time, Pallas kernels for 15%

profile of v9, /device:TPU:1, one launch (start us, length us, event | category | flops | bytes accessed | tf_op | source)
XLA Modules:
  0.0 69.9 jit_solution(13054635090320633907)
XLA Ops:
  0.6 3.3 %pair_terms.1 = bf16[64,2,1792]{2,1,0:T(2,128)(2,1)} custom-call(f32[136,128]{1,0:T(8,128)} %constant.41.clone.gap_ref, f32[12,128]{1,0:T(8,128)} %scores_ref.3, s32[12,128]{1,0:T(8,128)} %clicks_ref.3, s32[12]{0:T(128)} %lengths_ref.3, f32[1,128]{1,0:T(1,128)} %bitcast.8, f32[1,128]{1,0:T(1,128)} %bitcast.9, s32[128,1536]{1,0:T(8,128)} %bins_from.1), custom_call_target="tpu_custom_call" | custom-call | tf_op jit(solution)/shard_map/pair_terms/pallas_call | solution.py:343
  3.9 13.2 %all-to-all-start = ((bf16[64,2,1792]{2,1,0:T(2,128)(2,1)}), bf16[64,2,1792]{2,1,0:T(2,128)(2,1)S(1)}, u32[]{:S(2)}, u32[]{:S(2)}) async-start(bf16[64,2,1792]{2,1,0:T(2,128)(2,1)} %pair_terms.1), calls=%async_computation | async-start | bytes 917504 | tf_op jit(solution)/shard_map/all_to_all | solution.py:357
  17.1 1.6 %ready_pairs.1 = (f32[12,128,128]{2,1,0:T(8,128)S(1)}, f32[12,128,128]{2,1,0:T(8,128)S(1)}, f32[12,128]{1,0:T(8,128)S(1)}, f32[12,128]{1,0:T(8,128)S(1)}, s32[12]{0:T(128)S(4)}) custom-call(f32[136,128]{1,0:T(8,128)} %constant.41.clone.gap_ref, f32[12,128]{1,0:T(8,128)} %scores_ref.3, s32[12,128]{1,0:T(8,128)} %clicks_ref.3, s32[12]{0:T(128)} %lengths_ref.3), custom_call_target="tpu_custom_call" | custom-call | tf_op jit(solution)/shard_map/ready_pairs/pallas_call | solution.py:358
  18.7 0.0 copy-start
  18.7 14.7 %all-to-all-done.data_ref = bf16[64,2,1792]{2,1,0:T(2,128)(2,1)S(1)} async-done(((bf16[64,2,1792]{2,1,0:T(2,128)(2,1)}), bf16[64,2,1792]{2,1,0:T(2,128)(2,1)S(1)}, u32[]{:S(2)}, u32[]{:S(2)}) %all-to-all-start) | async-done | bytes 458784 | tf_op jit(solution)/shard_map/all_to_all | solution.py:357
  33.5 0.0 copy-done
  33.5 1.5 %lambdas.1 = (f32[1,128]{1,0:T(1,128)S(1)}, f32[1,128]{1,0:T(1,128)S(1)}, f32[2,1536]{1,0:T(2,128)S(1)}, bf16[32,2,2304]{2,1,0:T(2,128)(2,1)}) custom-call(f32[12,128,128]{2,1,0:T(8,128)S(1)} %get-tuple-element.18.first_ref, f32[12,128,128]{2,1,0:T(8,128)S(1)} %get-tuple-element.19.second_ref, f32[12,128]{1,0:T(8,128)S(1)} %get-tuple-element.20.own_ref, ...), custom_call_target="tpu_custom_call" | custom-call | tf_op jit(solution)/shard_map/lambdas/pallas_call | solution.py:371
  35.0 4.4 %all-to-all-start.1 = ((bf16[32,2,2304]{2,1,0:T(2,128)(2,1)}), bf16[32,2,2304]{2,1,0:T(2,128)(2,1)S(1)}, u32[]{:S(2)}, u32[]{:S(2)}) async-start(bf16[32,2,2304]{2,1,0:T(2,128)(2,1)} %get-tuple-element.31), calls=%async_computation.1 | async-start | bytes 589824 | tf_op jit(solution)/shard_map/all_to_all | solution.py:396
  39.4 12.0 %all-to-all-done.1.side_ref = bf16[32,2,2304]{2,1,0:T(2,128)(2,1)S(1)} async-done(((bf16[32,2,2304]{2,1,0:T(2,128)(2,1)}), bf16[32,2,2304]{2,1,0:T(2,128)(2,1)S(1)}, u32[]{:S(2)}, u32[]{:S(2)}) %all-to-all-start.1) | async-done | bytes 294944 | tf_op jit(solution)/shard_map/all_to_all | solution.py:396
  51.5 2.2 %collective-permute-start = (bf16[32,2,2304]{2,1,0:T(2,128)(2,1)S(1)}, bf16[32,2,2304]{2,1,0:T(2,128)(2,1)S(1)}, u32[]{:S(2)}, u32[]{:S(2)}) collective-permute-start(bf16[32,2,2304]{2,1,0:T(2,128)(2,1)S(1)} %all-to-all-done.1.side_ref), channel_id=1, source_target_pairs={{0,4},{4,0},{8,12},{12,8},{16,20},{20,16},{24,28},{28,24},{32,36},... | collective-permute-start | bytes 884744 | tf_op jit(solution)/shard_map/ppermute | solution.py:411
  53.7 0.7 %fusion = f32[64]{0:T(128)S(1)} fusion(bf16[64,2,1792]{2,1,0:T(2,128)(2,1)S(1)} %all-to-all-done.data_ref), kind=kLoop, calls=%fused_computation.1 | loop fusion | flops 294848 | bytes 196864 | tf_op jit(solution)/shard_map/reduce_sum | solution.py:397
  54.4 0.5 and_select_fusion.filled_ref
  54.9 3.3 %plan.1 = (s32[784]{0:T(1024)S(4)}, s32[2]{0:T(128)S(4)}, f32[1,128]{1,0:T(1,128)}, f32[1,128]{1,0:T(1,128)}, f32[2,1536]{1,0:T(2,128)}) custom-call(s32[64]{0:T(128)} %and_select_fusion.filled_ref, f32[1,128]{1,0:T(1,128)S(1)} %get-tuple-element.23.plus_in, f32[1,128]{1,0:T(1,128)S(1)} %get-tuple-element.24.minus_in, f32[2,1536]{1,0:T(2,128)S(1)} %get-tuple-element.25.grad_in), custom_call_target="tpu_custom_call" | custom-call | tf_op jit(solution)/shard_map/plan/pallas_call | solution.py:398
  58.2 5.5 %first_half.1.before_ref = f32[2,128,128]{2,1,0:T(8,128)S(1)} custom-call(s32[1]{0:T(128)} %bitcast.6.core_ref, s32[784]{0:T(1024)S(4)} %get-tuple-element.29.list_ref, s32[2]{0:T(128)S(4)} %get-tuple-element.30.total_ref, bf16[64,2,1792]{2,1,0:T(2,128)(2,1)S(1)} %all-to-all-done.data_ref, bf16[32,2,2304]{2,1,0:T(2,128)(2,1)S(1)} %all-to-all-done.1.side_ref), custom_call_target="tpu_custom_call" | custom-call | tf_op jit(solution)/shard_map/first_half/pallas_call | solution.py:316
  63.7 0.0 collective-permute-done.side_ref
  63.7 6.2 %second_half.1 = f32[2,64,256]{2,1,0:T(8,128)} custom-call(s32[1]{0:T(128)} %bitcast.5.core_ref, s32[784]{0:T(1024)S(4)} %get-tuple-element.29.list_ref, s32[2]{0:T(128)S(4)} %get-tuple-element.30.total_ref, bf16[64,2,1792]{2,1,0:T(2,128)(2,1)S(1)} %all-to-all-done.data_ref, bf16[32,2,2304]{2,1,0:T(2,128)(2,1)S(1)} %collective-permute-done.side_ref, ...), custom_call_target="tpu_custom_call" | custom-call | tf_op jit(solution)/shard_map/second_half/pallas_call | solution.py:323
Async XLA Ops:
  3.9 29.5 %all-to-all-start = ((bf16[64,2,1792]{2,1,0:T(2,128)(2,1)}), bf16[64,2,1792]{2,1,0:T(2,128)(2,1)S(1)}, u32[]{:S(2)}, u32[]{:S(2)}) async-start(bf16[64,2,1792]{2,1,0:T(2,128)(2,1)} %pair_terms.1), calls=%async_computation | async-start | bytes 917504 | tf_op jit(solution)/shard_map/all_to_all | solution.py:357
  18.7 14.8 %copy-start = (s32[1536]{0:T(1024)S(1)}, s32[1536]{0:T(1024)}, u32[]{:S(2)}) copy-start(s32[1536]{0:T(1024)} %param.13) | copy-start | bytes 18436
  35.0 16.5 %all-to-all-start.1 = ((bf16[32,2,2304]{2,1,0:T(2,128)(2,1)}), bf16[32,2,2304]{2,1,0:T(2,128)(2,1)S(1)}, u32[]{:S(2)}, u32[]{:S(2)}) async-start(bf16[32,2,2304]{2,1,0:T(2,128)(2,1)} %get-tuple-element.31), calls=%async_computation.1 | async-start | bytes 589824 | tf_op jit(solution)/shard_map/all_to_all | solution.py:396
  51.5 12.2 %collective-permute-start = (bf16[32,2,2304]{2,1,0:T(2,128)(2,1)S(1)}, bf16[32,2,2304]{2,1,0:T(2,128)(2,1)S(1)}, u32[]{:S(2)}, u32[]{:S(2)}) collective-permute-start(bf16[32,2,2304]{2,1,0:T(2,128)(2,1)S(1)} %all-to-all-done.1.side_ref), channel_id=1, source_target_pairs={{0,4},{4,0},{8,12},{12,8},{16,20},{20,16},{24,28},{28,24},{32,36},... | collective-permute-start | bytes 884744 | tf_op jit(solution)/shard_map/ppermute | solution.py:411

commit v10 on v9

--- a/solution.py
+++ b/solution.py
@@ -14,6 +14,7 @@
 TILE = 256
 STEP = 4
 WIDE = 4
+PARTS = 4
 
 
 def query_rows(scores, clicks, lengths_ref, queries, discount_row):
@@ -182,14 +183,14 @@
     plus_ref[...] = plus_in[...]
     minus_ref[...] = minus_in[...]
     grad_ref[...] = grad_in[...]
-    chips = filled_ref.shape[0] // 2
-    groups = (list_ref.shape[0] // 2 - 2 * STEP) // chips
-    for core in range(2):
+    chips = filled_ref.shape[0] // PARTS
+    groups = (list_ref.shape[0] // PARTS - 2 * STEP) // chips
+    for core in range(PARTS):
         base = core * (chips * groups + 2 * STEP)
 
         def one_block(chip, carry):
             at, spare = carry
-            used = filled_ref[2 * chip + core]
+            used = filled_ref[PARTS * chip + core]
             for group in range(groups):
                 list_ref[base + at] = chip * 16 + group
                 at = at + jnp.where(group < used, 1, 0)
@@ -202,7 +203,7 @@
 
 
 def accumulate(core, list_ref, total_ref, data_ref, side_ref, accs):
-    base = core * (list_ref.shape[0] // 2)
+    base = core * (list_ref.shape[0] // PARTS)
     groups = side_ref.shape[2] * 2 // (3 * POS)
     rows_a = lax.broadcasted_iota(jnp.int32, (2 * LEAVES, TILE), 0).astype(jnp.bfloat16)
     rows_b = lax.broadcasted_iota(jnp.int32, (HALF, TILE), 0).astype(jnp.bfloat16)
@@ -221,7 +222,7 @@
                 late = group >= groups // 2
                 place = groups + group - jnp.where(late, groups // 2, 0)
                 here = pl.ds(pl.multiple_of(group * POS, POS), POS)
-                bins.append(data_ref[2 * chip + core, :, here])
+                bins.append(data_ref[PARTS * chip + core, :, here])
                 sides.append(side_ref[chip, :, here])
                 pair = side_ref[chip, :, pl.ds(pl.multiple_of(place * POS, POS), POS)]
                 leaves.append(jnp.where(late, pair[1:2], pair[0:1]))
@@ -266,19 +267,21 @@
     pl.run_scoped(run, pltpu.ACC(0)(shape, jnp.float32), pltpu.ACC(1)(shape, jnp.float32))
 
 
-def first_kernel(core_ref, list_ref, total_ref, data_ref, side_ref, out_ref):
+def part_kernel(core_ref, list_ref, total_ref, data_ref, side_ref, *refs):
     rows = 4 * LEAVES
+    out_ref = refs[-1]
 
     def finish(total):
         for feature in range(2):
-            out_ref[feature] = total[
+            mine = total[
                 feature * rows : (feature + 1) * rows, feature * HALF : (feature + 1) * HALF
             ]
+            out_ref[feature] = mine if len(refs) == 1 else mine + refs[0][feature]
 
     summed(core_ref[0], list_ref, total_ref, data_ref, side_ref, finish)
 
 
-def second_kernel(core_ref, list_ref, total_ref, data_ref, side_ref, before_ref, out_ref):
+def last_kernel(core_ref, list_ref, total_ref, data_ref, side_ref, before_ref, out_ref):
     rows = 4 * LEAVES
 
     def finish(total):
@@ -310,23 +313,21 @@
     return pltpu.with_memory_space_constraint(array, pltpu.SMEM)
 
 
-def hist_of(core, plan, data, side, before=None):
-    part = (2, 4 * LEAVES, HALF)
-    if before is None:
-        return pl.pallas_call(
-            first_kernel,
-            out_shape=pltpu.VMEM(part, jnp.float32),
-            in_specs=[SMEM, SMEM, SMEM, VMEM, VMEM],
-            out_specs=VMEM,
-            name="first_half",
-        )(core, *plan, data, side)
+def hist_of(core, plan, data, side, before=None, last=False):
+    given = [in_vmem(data), in_vmem(side)]
+    if before is not None:
+        given.append(in_vmem(before))
+    if last:
+        out_shape = jax.ShapeDtypeStruct((2, 2 * LEAVES, BINS), jnp.float32)
+    else:
+        out_shape = pltpu.VMEM((2, 4 * LEAVES, HALF), jnp.float32)
     return pl.pallas_call(
-        second_kernel,
-        out_shape=jax.ShapeDtypeStruct((2, 2 * LEAVES, BINS), jnp.float32),
-        in_specs=[SMEM, SMEM, SMEM, VMEM, VMEM, VMEM],
+        last_kernel if last else part_kernel,
+        out_shape=out_shape,
+        in_specs=[SMEM, SMEM, SMEM] + [VMEM] * len(given),
         out_specs=VMEM,
-        name="second_half",
-    )(core, *plan, data, side, before)
+        name="last_part" if last else "part",
+    )(core.reshape(1), *plan, *given)
 
 
 def body(scores, clicks, lengths, t_plus_old, t_minus_old, leaf, bins):
@@ -374,7 +375,7 @@
             pltpu.VMEM((1, POS), f32),
             pltpu.VMEM((1, POS), f32),
             pltpu.VMEM((2, slots), f32),
-            pltpu.VMEM((shards // 2, 2, 3 * slots // 2), jnp.bfloat16),
+            pltpu.VMEM((shards // PARTS, 2, 3 * slots // 2), jnp.bfloat16),
         ),
         in_specs=[VMEM, VMEM, VMEM, VMEM, SMEM, VMEM, VMEM],
         out_specs=(VMEM,) * 4,
@@ -392,14 +393,14 @@
         in_vmem(leaf.reshape(queries, POS)),
         in_vmem(data),
     )
-    same_core = [[2 * chip + core for chip in range(shards // 2)] for core in range(2)]
-    side = lax.all_to_all(side, "doc", 0, 0, axis_index_groups=same_core, tiled=True)
+    alike = [list(range(part, shards, PARTS)) for part in range(PARTS)]
+    side = lax.all_to_all(side, "doc", 0, 0, axis_index_groups=alike, tiled=True)
     shown = jnp.sum((data[:, 0, :slots] >= 0).astype(f32), axis=1).astype(jnp.int32)
     *plan, t_plus, t_minus, gradients = pl.pallas_call(
         plan_kernel,
         out_shape=(
-            pltpu.SMEM((shards * groups + 4 * STEP,), jnp.int32),
-            pltpu.SMEM((2,), jnp.int32),
+            pltpu.SMEM((shards * groups + 2 * PARTS * STEP,), jnp.int32),
+            pltpu.SMEM((PARTS,), jnp.int32),
             jax.ShapeDtypeStruct((1, POS), f32),
             jax.ShapeDtypeStruct((1, POS), f32),
             jax.ShapeDtypeStruct((2, slots), f32),
@@ -408,10 +409,15 @@
         out_specs=(SMEM, SMEM, VMEM, VMEM, VMEM),
         name="plan",
     )((shown + (POS - 1)) // POS, in_vmem(t_plus), in_vmem(t_minus), in_vmem(gradients))
-    other_side = lax.ppermute(side, "doc", [(at, at ^ 1) for at in range(shards)])
-    core = lax.axis_index("doc") % 2
-    partial = hist_of(core.reshape(1), plan, in_vmem(data), in_vmem(side))
-    hist = hist_of((1 - core).reshape(1), plan, in_vmem(data), in_vmem(other_side), in_vmem(partial))
+    swap = [[(at, at ^ bit) for at in range(shards)] for bit in (1, 2)]
+    own = lax.rem(lax.axis_index("doc"), PARTS)
+    side_far = lax.ppermute(side, "doc", swap[1])
+    side_near = lax.ppermute(side, "doc", swap[0])
+    side_last = lax.ppermute(side_far, "doc", swap[0])
+    partial = hist_of(own, plan, data, side)
+    partial = hist_of(lax.bitwise_xor(own, 1), plan, data, side_near, partial)
+    partial = hist_of(lax.bitwise_xor(own, 2), plan, data, side_far, partial)
+    hist = hist_of(lax.bitwise_xor(own, 3), plan, data, side_last, partial, True)
     return (t_plus[0], t_minus[0], gradients, hist)
 
 

time: 70.3 us -> 72.8 us (1.036)
  starting transfers between devices: 19.8 us -> 23.8 us
  waiting for transfers between devices: 26.8 us -> 25 us
    ppermute x1 -> x3, starting transfers between devices: 2.18 us -> 6.51 us  [the longest x1 3.42 us: body(): side_last = lax.ppermute(side_far, 'doc', swap[0])]
    all_to_all x1, waiting for transfers between devices: 12 us -> 10.1 us  [body(): lax.all_to_all(side, 'doc', 0, 0, axis_index_groups=alike, tiled=True)]
    pallas_call x3 -> x5, Pallas kernels: 14.9 us -> 15.3 us  [the longest x4 12 us: hist_of(): pl.pallas_call(last_kernel if last else part_kernel, out_shape=out_shape,...]
  transfers between devices with their start and end apart: 3 -> 5, of which waited for: 2 -> 3; matrix products, arithmetic and copies ran while one was open for 2% -> 2% of each run, Pallas kernels for 15% -> 19%
where the time goes in v10:
time: 72.8 us; the launch traced here: 72.4 us
  waiting for transfers between devices  25 us (34%)
  starting transfers between devices  23.8 us (33%)
  Pallas kernels  21.6 us (30%)
  other arithmetic  1.27 us (2%)
    all_to_all x1, waiting for transfers between devices, body(): data = lax.all_to_all(sent, 'doc', 0, 0, tiled=True)  14.7 us
    all_to_all x1, starting transfers between devices, body(): data = lax.all_to_all(sent, 'doc', 0, 0, tiled=True)  13.2 us
    pallas_call x4, Pallas kernels, hist_of(): pl.pallas_call(last_kernel if last else part_kernel, out_shape=out_shape,...  12 us
    all_to_all x1, waiting for transfers between devices, body(): lax.all_to_all(side, 'doc', 0, 0, axis_index_groups=alike, tiled=True)  10.1 us
    all_to_all x1, starting transfers between devices, body(): lax.all_to_all(side, 'doc', 0, 0, axis_index_groups=alike, tiled=True)  4.16 us
    ppermute x1, starting transfers between devices, body(): side_last = lax.ppermute(side_far, 'doc', swap[0])  3.42 us
    pallas_call x1, Pallas kernels, body(): pl.pallas_call(plan_kernel, out_shape=(pltpu.SMEM((shards * groups + 2 *...  3.31 us
    pallas_call x1, Pallas kernels, body(): pl.pallas_call(pair_kernel, out_shape=jax.ShapeDtypeStruct(sent_shape, jn...  3.3 us
  transfers between devices with their start and end apart: 5, of which 3 were waited for; matrix products, arithmetic and copies ran while one was open for 2% of the time, Pallas kernels for 19%

profile of v10, /device:TPU:1, one launch (start us, length us, event | category | flops | bytes accessed | tf_op | source)
XLA Modules:
  0.0 72.4 jit_solution(9280796715170615417)
XLA Ops:
  0.6 3.3 %pair_terms.1 = bf16[64,2,1792]{2,1,0:T(2,128)(2,1)} custom-call(f32[136,128]{1,0:T(8,128)} %constant.37.clone.gap_ref, f32[12,128]{1,0:T(8,128)} %scores_ref.3, s32[12,128]{1,0:T(8,128)} %clicks_ref.3, s32[12]{0:T(128)} %lengths_ref.3, f32[1,128]{1,0:T(1,128)} %bitcast.10, f32[1,128]{1,0:T(1,128)} %bitcast.11, s32[128,1536]{1,0:T(8,128)} %bins_from.1), custom_call_target="tpu_custom_call" | custom-call | tf_op jit(solution)/shard_map/pair_terms/pallas_call | solution.py:344
  3.9 13.2 %all-to-all-start = ((bf16[64,2,1792]{2,1,0:T(2,128)(2,1)}), bf16[64,2,1792]{2,1,0:T(2,128)(2,1)S(1)}, u32[]{:S(2)}, u32[]{:S(2)}) async-start(bf16[64,2,1792]{2,1,0:T(2,128)(2,1)} %pair_terms.1), calls=%async_computation | async-start | bytes 917504 | tf_op jit(solution)/shard_map/all_to_all | solution.py:358
  17.1 1.6 %ready_pairs.1 = (f32[12,128,128]{2,1,0:T(8,128)S(1)}, f32[12,128,128]{2,1,0:T(8,128)S(1)}, f32[12,128]{1,0:T(8,128)S(1)}, f32[12,128]{1,0:T(8,128)S(1)}, s32[12]{0:T(128)S(4)}) custom-call(f32[136,128]{1,0:T(8,128)} %constant.37.clone.gap_ref, f32[12,128]{1,0:T(8,128)} %scores_ref.3, s32[12,128]{1,0:T(8,128)} %clicks_ref.3, s32[12]{0:T(128)} %lengths_ref.3), custom_call_target="tpu_custom_call" | custom-call | tf_op jit(solution)/shard_map/ready_pairs/pallas_call | solution.py:359
  18.7 0.0 copy-start
  18.7 14.7 %all-to-all-done.data_ref = bf16[64,2,1792]{2,1,0:T(2,128)(2,1)S(1)} async-done(((bf16[64,2,1792]{2,1,0:T(2,128)(2,1)}), bf16[64,2,1792]{2,1,0:T(2,128)(2,1)S(1)}, u32[]{:S(2)}, u32[]{:S(2)}) %all-to-all-start) | async-done | bytes 458784 | tf_op jit(solution)/shard_map/all_to_all | solution.py:358
  33.5 0.0 copy-done
  33.5 1.4 %lambdas.1 = (f32[1,128]{1,0:T(1,128)S(1)}, f32[1,128]{1,0:T(1,128)S(1)}, f32[2,1536]{1,0:T(2,128)S(1)}, bf16[16,2,2304]{2,1,0:T(2,128)(2,1)}) custom-call(f32[12,128,128]{2,1,0:T(8,128)S(1)} %get-tuple-element.18.first_ref, f32[12,128,128]{2,1,0:T(8,128)S(1)} %get-tuple-element.19.second_ref, f32[12,128]{1,0:T(8,128)S(1)} %get-tuple-element.20.own_ref, ...), custom_call_target="tpu_custom_call" | custom-call | tf_op jit(solution)/shard_map/lambdas/pallas_call | solution.py:372
  34.9 4.2 %all-to-all-start.1 = ((bf16[16,2,2304]{2,1,0:T(2,128)(2,1)}), bf16[16,2,2304]{2,1,0:T(2,128)(2,1)S(1)}, u32[]{:S(2)}, u32[]{:S(2)}) async-start(bf16[16,2,2304]{2,1,0:T(2,128)(2,1)} %get-tuple-element.31), calls=%async_computation.1 | async-start | bytes 294912 | tf_op jit(solution)/shard_map/all_to_all | solution.py:397
  39.1 10.1 %all-to-all-done.1.side_ref = bf16[16,2,2304]{2,1,0:T(2,128)(2,1)S(1)} async-done(((bf16[16,2,2304]{2,1,0:T(2,128)(2,1)}), bf16[16,2,2304]{2,1,0:T(2,128)(2,1)S(1)}, u32[]{:S(2)}, u32[]{:S(2)}) %all-to-all-start.1) | async-done | bytes 147488 | tf_op jit(solution)/shard_map/all_to_all | solution.py:397
  49.2 0.6 collective-permute-start
  49.8 0.7 %fusion = f32[64]{0:T(128)S(1)} fusion(bf16[64,2,1792]{2,1,0:T(2,128)(2,1)S(1)} %all-to-all-done.data_ref), kind=kLoop, calls=%fused_computation.1 | loop fusion | flops 294848 | bytes 196864 | tf_op jit(solution)/shard_map/reduce_sum | solution.py:398
  50.5 2.5 %collective-permute-start.2 = (bf16[16,2,2304]{2,1,0:T(2,128)(2,1)S(1)}, bf16[16,2,2304]{2,1,0:T(2,128)(2,1)S(1)}, u32[]{:S(2)}, u32[]{:S(2)}) collective-permute-start(bf16[16,2,2304]{2,1,0:T(2,128)(2,1)S(1)} %all-to-all-done.1.side_ref), channel_id=1, source_target_pairs={{0,4},{4,0},{8,12},{12,8},{16,20},{20,16},{24,28},{28,24},{32,36},... | collective-permute-start | bytes 442376 | tf_op jit(solution)/shard_map/ppermute | solution.py:415
  53.0 0.2 collective-permute-done.side_ref
  53.2 3.4 %collective-permute-start.1 = (bf16[16,2,2304]{2,1,0:T(2,128)(2,1)S(1)}, bf16[16,2,2304]{2,1,0:T(2,128)(2,1)S(1)}, u32[]{:S(2)}, u32[]{:S(2)}) collective-permute-start(bf16[16,2,2304]{2,1,0:T(2,128)(2,1)S(1)} %collective-permute-done.side_ref), channel_id=1, source_target_pairs={{0,4},{4,0},{8,12},{12,8},{16,20},{20,16},{24,28},{28,24},{32,36},... | collective-permute-start | bytes 442376 | tf_op jit(solution)/shard_map/ppermute | solution.py:416
  56.6 0.5 and_select_fusion.filled_ref
  57.1 3.3 %plan.1 = (s32[800]{0:T(1024)S(4)}, s32[4]{0:T(128)S(4)}, f32[1,128]{1,0:T(1,128)}, f32[1,128]{1,0:T(1,128)}, f32[2,1536]{1,0:T(2,128)}) custom-call(s32[64]{0:T(128)} %and_select_fusion.filled_ref, f32[1,128]{1,0:T(1,128)S(1)} %get-tuple-element.23.plus_in, f32[1,128]{1,0:T(1,128)S(1)} %get-tuple-element.24.minus_in, f32[2,1536]{1,0:T(2,128)S(1)} %get-tuple-element.25.grad_in), custom_call_target="tpu_custom_call" | custom-call | tf_op jit(solution)/shard_map/plan/pallas_call | solution.py:399
  60.4 2.8 %part.3.refs_0_ = f32[2,128,128]{2,1,0:T(8,128)S(1)} custom-call(s32[1]{0:T(128)} %bitcast.8.core_ref, s32[800]{0:T(1024)S(4)} %get-tuple-element.29.list_ref, s32[4]{0:T(128)S(4)} %get-tuple-element.30.total_ref, bf16[64,2,1792]{2,1,0:T(2,128)(2,1)S(1)} %all-to-all-done.data_ref, bf16[16,2,2304]{2,1,0:T(2,128)(2,1)S(1)} %all-to-all-done.1.side_ref), custom_call_target="tpu_custom_call" | custom-call | tf_op jit(solution)/shard_map/part/pallas_call | solution.py:324
  63.2 0.0 collective-permute-done.2.side_ref
  63.2 2.8 %part.4.refs_0_ = f32[2,128,128]{2,1,0:T(8,128)S(1)} custom-call(s32[1]{0:T(128)} %bitcast.7.core_ref, s32[800]{0:T(1024)S(4)} %get-tuple-element.29.list_ref, s32[4]{0:T(128)S(4)} %get-tuple-element.30.total_ref, bf16[64,2,1792]{2,1,0:T(2,128)(2,1)S(1)} %all-to-all-done.data_ref, bf16[16,2,2304]{2,1,0:T(2,128)(2,1)S(1)} %collective-permute-done.2.side_ref, ...), custom_call_target="tpu_custom_call" | custom-call | tf_op jit(solution)/shard_map/part/pallas_call | solution.py:324
  66.1 2.9 %part.5.before_ref = f32[2,128,128]{2,1,0:T(8,128)S(1)} custom-call(s32[1]{0:T(128)} %bitcast.6.core_ref, s32[800]{0:T(1024)S(4)} %get-tuple-element.29.list_ref, s32[4]{0:T(128)S(4)} %get-tuple-element.30.total_ref, bf16[64,2,1792]{2,1,0:T(2,128)(2,1)S(1)} %all-to-all-done.data_ref, bf16[16,2,2304]{2,1,0:T(2,128)(2,1)S(1)} %collective-permute-done.side_ref, ...), custom_call_target="tpu_custom_call" | custom-call | tf_op jit(solution)/shard_map/part/pallas_call | solution.py:324
  69.0 0.0 collective-permute-done.1.side_ref
  69.0 3.5 %last_part.1 = f32[2,64,256]{2,1,0:T(8,128)} custom-call(s32[1]{0:T(128)} %bitcast.5.core_ref, s32[800]{0:T(1024)S(4)} %get-tuple-element.29.list_ref, s32[4]{0:T(128)S(4)} %get-tuple-element.30.total_ref, bf16[64,2,1792]{2,1,0:T(2,128)(2,1)S(1)} %all-to-all-done.data_ref, bf16[16,2,2304]{2,1,0:T(2,128)(2,1)S(1)} %collective-permute-done.1.side_ref, ...), custom_call_target="tpu_custom_call" | custom-call | tf_op jit(solution)/shard_map/last_part/pallas_call | solution.py:324
Async XLA Ops:
  3.9 29.5 %all-to-all-start = ((bf16[64,2,1792]{2,1,0:T(2,128)(2,1)}), bf16[64,2,1792]{2,1,0:T(2,128)(2,1)S(1)}, u32[]{:S(2)}, u32[]{:S(2)}) async-start(bf16[64,2,1792]{2,1,0:T(2,128)(2,1)} %pair_terms.1), calls=%async_computation | async-start | bytes 917504 | tf_op jit(solution)/shard_map/all_to_all | solution.py:358
  18.7 14.8 %copy-start = (s32[1536]{0:T(1024)S(1)}, s32[1536]{0:T(1024)}, u32[]{:S(2)}) copy-start(s32[1536]{0:T(1024)} %param.13) | copy-start | bytes 18436
  34.9 14.3 %all-to-all-start.1 = ((bf16[16,2,2304]{2,1,0:T(2,128)(2,1)}), bf16[16,2,2304]{2,1,0:T(2,128)(2,1)S(1)}, u32[]{:S(2)}, u32[]{:S(2)}) async-start(bf16[16,2,2304]{2,1,0:T(2,128)(2,1)} %get-tuple-element.31), calls=%async_computation.1 | async-start | bytes 294912 | tf_op jit(solution)/shard_map/all_to_all | solution.py:397
  49.2 4.0 %collective-permute-start = (bf16[16,2,2304]{2,1,0:T(2,128)(2,1)S(1)}, bf16[16,2,2304]{2,1,0:T(2,128)(2,1)S(1)}, u32[]{:S(2)}, u32[]{:S(2)}) collective-permute-start(bf16[16,2,2304]{2,1,0:T(2,128)(2,1)S(1)} %all-to-all-done.1.side_ref), channel_id=1, source_target_pairs={{0,8},{4,12},{8,0},{12,4},{16,24},{20,28},{24,16},{28,20},{32,40},... | collective-permute-start | bytes 442376 | tf_op jit(solution)/shard_map/ppermute | solution.py:414
  50.5 12.7 %collective-permute-start.2 = (bf16[16,2,2304]{2,1,0:T(2,128)(2,1)S(1)}, bf16[16,2,2304]{2,1,0:T(2,128)(2,1)S(1)}, u32[]{:S(2)}, u32[]{:S(2)}) collective-permute-start(bf16[16,2,2304]{2,1,0:T(2,128)(2,1)S(1)} %all-to-all-done.1.side_ref), channel_id=1, source_target_pairs={{0,4},{4,0},{8,12},{12,8},{16,20},{20,16},{24,28},{28,24},{32,36},... | collective-permute-start | bytes 442376 | tf_op jit(solution)/shard_map/ppermute | solution.py:415
  53.2 15.8 %collective-permute-start.1 = (bf16[16,2,2304]{2,1,0:T(2,128)(2,1)S(1)}, bf16[16,2,2304]{2,1,0:T(2,128)(2,1)S(1)}, u32[]{:S(2)}, u32[]{:S(2)}) collective-permute-start(bf16[16,2,2304]{2,1,0:T(2,128)(2,1)S(1)} %collective-permute-done.side_ref), channel_id=1, source_target_pairs={{0,4},{4,0},{8,12},{12,8},{16,20},{20,16},{24,28},{28,24},{32,36},... | collective-permute-start | bytes 442376 | tf_op jit(solution)/shard_map/ppermute | solution.py:416

commit v11 on v10

--- a/solution.py
+++ b/solution.py
@@ -41,10 +41,27 @@
     return jnp.transpose(jnp.concatenate(list(rows) + [pad], axis=0))
 
 
-def pair_kernel(gap_ref, scores_ref, clicks_ref, lengths_ref, plus_ref, minus_ref, bins_from,
-                sent_to, bins_ref, sent_ref, packed, took, gave):
-    take = pltpu.make_async_copy(bins_from, bins_ref, took)
-    take.start()
+def pair_kernel(*refs):
+    small_from, bins_from, sent_to = refs[:6], refs[6], refs[7]
+    small, bins_ref, sent_ref, packed = refs[8:14], refs[14], refs[15], refs[16]
+    took_small, took, gave = refs[17:]
+    gap_ref, scores_ref, clicks_ref, lengths_ref, plus_ref, minus_ref = small
+    blocks = took.shape[0]
+    height = bins_ref.shape[0] // blocks
+    small_takes = [
+        pltpu.make_async_copy(there, here, took_small.at[at])
+        for at, (there, here) in enumerate(zip(small_from, small))
+    ]
+    takes = []
+    for block in range(blocks):
+        rows = pl.ds(block * height, height)
+        takes.append(
+            pltpu.make_async_copy(bins_from.at[rows], bins_ref.at[rows], took.at[block])
+        )
+    for take in small_takes + takes:
+        take.start()
+    for take in small_takes:
+        take.wait()
     queries = scores_ref.shape[0]
     clicked, skipped, side, signed, ideal = query_rows(
         scores_ref[...], clicks_ref[...], lengths_ref, queries, gap_ref[POS : POS + 1]
@@ -77,7 +94,8 @@
             pieces[None], (owners, 2, POS)
         )
     packed[...] = jnp.full(packed.shape, -1.0, jnp.float32)
-    take.wait()
+    for take in takes:
+        take.wait()
     lane = lax.broadcasted_iota(jnp.int32, (1, POS), 1)
     start = jnp.int32(0)
     for query in range(queries):
@@ -184,17 +202,16 @@
     minus_ref[...] = minus_in[...]
     grad_ref[...] = grad_in[...]
     chips = filled_ref.shape[0] // PARTS
-    groups = (list_ref.shape[0] // PARTS - 2 * STEP) // chips
+    groups = grad_in.shape[1] // POS
     for core in range(PARTS):
-        base = core * (chips * groups + 2 * STEP)
+        base = core * (list_ref.shape[0] // PARTS)
 
         def one_block(chip, carry):
             at, spare = carry
             used = filled_ref[PARTS * chip + core]
             for group in range(groups):
-                list_ref[base + at] = chip * 16 + group
-                at = at + jnp.where(group < used, 1, 0)
-            return at, jnp.where(used < groups, chip * 16 + groups - 1, spare)
+                list_ref[base + at + group] = chip * 16 + group
+            return at + used, jnp.where(used < groups, chip * 16 + groups - 1, spare)
 
         at, spare = lax.fori_loop(0, chips, one_block, (jnp.int32(0), jnp.int32(0)))
         for extra in range(2 * STEP):
@@ -341,20 +358,27 @@
     gap = jnp.asarray(np.concatenate([gap, np.tile(discount[None], (8, 1))]))
     f32 = jnp.float32
     sent_shape = (shards, 2, slots + 2 * POS)
+    given = (gap, scores, clicks, lengths, t_plus_old[None], t_minus_old[None])
+    anywhere = pl.BlockSpec(memory_space=pl.ANY)
     sent = pl.pallas_call(
         pair_kernel,
         out_shape=jax.ShapeDtypeStruct(sent_shape, jnp.bfloat16),
-        in_specs=[VMEM, VMEM, VMEM, SMEM, VMEM, VMEM, pl.BlockSpec(memory_space=pl.ANY)],
-        out_specs=pl.BlockSpec(memory_space=pl.ANY),
+        in_specs=[anywhere] * 7,
+        out_specs=anywhere,
         scratch_shapes=[
+            *(
+                (pltpu.SMEM if array.ndim == 1 else pltpu.VMEM)(array.shape, array.dtype)
+                for array in given
+            ),
             pltpu.VMEM(bins.shape, jnp.int32),
             pltpu.VMEM(sent_shape, jnp.bfloat16),
             pltpu.VMEM((slots // POS + 1, bins.shape[0], POS), f32),
-            pltpu.SemaphoreType.DMA,
+            pltpu.SemaphoreType.DMA((len(given),)),
+            pltpu.SemaphoreType.DMA((1,)),
             pltpu.SemaphoreType.DMA((4,)),
         ],
         name="pair_terms",
-    )(gap, scores, clicks, lengths, t_plus_old[None], t_minus_old[None], bins)
+    )(*given, bins)
     data = lax.all_to_all(sent, "doc", 0, 0, tiled=True)
     first, second, own, scale, held = pl.pallas_call(
         ready_kernel,
@@ -399,7 +423,7 @@
     *plan, t_plus, t_minus, gradients = pl.pallas_call(
         plan_kernel,
         out_shape=(
-            pltpu.SMEM((shards * groups + 2 * PARTS * STEP,), jnp.int32),
+            pltpu.SMEM((shards * groups + PARTS * 16,), jnp.int32),
             pltpu.SMEM((PARTS,), jnp.int32),
             jax.ShapeDtypeStruct((1, POS), f32),
             jax.ShapeDtypeStruct((1, POS), f32),

time: 72.8 us -> 71.6 us (0.984)
  Pallas kernels: 21.6 us -> 20.4 us
    pallas_call x1, Pallas kernels: 3.31 us -> 2.37 us  [body(): pl.pallas_call(plan_kernel, out_shape=(pltpu.SMEM((shards * groups + PART...]
  transfers between devices with their start and end apart: 5 -> 5, of which waited for: 3 -> 3; matrix products, arithmetic and copies ran while one was open for 2% -> 2% of each run, Pallas kernels for 19% -> 18%
where the time goes in v11:
time: 71.6 us; the launch traced here: 71.2 us
  waiting for transfers between devices  25 us (35%)
  starting transfers between devices  23.8 us (33%)
  Pallas kernels  20.4 us (28%)
  other arithmetic  1.27 us (2%)
  between operations  0.72 us (1%)
    all_to_all x1, waiting for transfers between devices, body(): data = lax.all_to_all(sent, 'doc', 0, 0, tiled=True)  14.7 us
    all_to_all x1, starting transfers between devices, body(): data = lax.all_to_all(sent, 'doc', 0, 0, tiled=True)  13.2 us
    pallas_call x4, Pallas kernels, hist_of(): pl.pallas_call(last_kernel if last else part_kernel, out_shape=out_shape,...  12 us
    all_to_all x1, waiting for transfers between devices, body(): lax.all_to_all(side, 'doc', 0, 0, axis_index_groups=alike, tiled=True)  10.1 us
    all_to_all x1, starting transfers between devices, body(): lax.all_to_all(side, 'doc', 0, 0, axis_index_groups=alike, tiled=True)  4.16 us
    ppermute x1, starting transfers between devices, body(): side_last = lax.ppermute(side_far, 'doc', swap[0])  3.42 us
    pallas_call x1, Pallas kernels, body(): pl.pallas_call(pair_kernel, out_shape=jax.ShapeDtypeStruct(sent_shape, jn...  3.06 us
    ppermute x1, starting transfers between devices, body(): side_near = lax.ppermute(side, 'doc', swap[0])  2.52 us
  transfers between devices with their start and end apart: 5, of which 3 were waited for; matrix products, arithmetic and copies ran while one was open for 2% of the time, Pallas kernels for 18%

profile of v11, /device:TPU:1, one launch (start us, length us, event | category | flops | bytes accessed | tf_op | source)
XLA Modules:
  0.0 71.2 jit_solution(333080309552174021)
XLA Ops:
  0.6 3.1 %pair_terms.1 = bf16[64,2,1792]{2,1,0:T(2,128)(2,1)} custom-call(f32[136,128]{1,0:T(8,128)} %constant.37.clone.refs_0_.gap_ref, f32[12,128]{1,0:T(8,128)} %scores_ref.1, s32[12,128]{1,0:T(8,128)} %clicks_ref.1, s32[12]{0:T(128)} %lengths_ref.1, f32[1,128]{1,0:T(1,128)} %bitcast.10, f32[1,128]{1,0:T(1,128)} %bitcast.11, s32[128,1536]{1,0:T(8,128)} %refs_6_.1), custom_call_target="tpu_custom_call" | custom-call | tf_op jit(solution)/shard_map/pair_terms/pallas_call | solution.py:363
  3.7 13.2 %all-to-all-start = ((bf16[64,2,1792]{2,1,0:T(2,128)(2,1)}), bf16[64,2,1792]{2,1,0:T(2,128)(2,1)S(1)}, u32[]{:S(2)}, u32[]{:S(2)}) async-start(bf16[64,2,1792]{2,1,0:T(2,128)(2,1)} %pair_terms.1), calls=%async_computation | async-start | bytes 917504 | tf_op jit(solution)/shard_map/all_to_all | solution.py:382
  16.9 1.6 %ready_pairs.1 = (f32[12,128,128]{2,1,0:T(8,128)S(1)}, f32[12,128,128]{2,1,0:T(8,128)S(1)}, f32[12,128]{1,0:T(8,128)S(1)}, f32[12,128]{1,0:T(8,128)S(1)}, s32[12]{0:T(128)S(4)}) custom-call(f32[136,128]{1,0:T(8,128)} %constant.37.clone.refs_0_.gap_ref, f32[12,128]{1,0:T(8,128)} %scores_ref.1, s32[12,128]{1,0:T(8,128)} %clicks_ref.1, s32[12]{0:T(128)} %lengths_ref.1), custom_call_target="tpu_custom_call" | custom-call | tf_op jit(solution)/shard_map/ready_pairs/pallas_call | solution.py:383
  18.5 0.0 copy-start
  18.5 14.7 %all-to-all-done.data_ref = bf16[64,2,1792]{2,1,0:T(2,128)(2,1)S(1)} async-done(((bf16[64,2,1792]{2,1,0:T(2,128)(2,1)}), bf16[64,2,1792]{2,1,0:T(2,128)(2,1)S(1)}, u32[]{:S(2)}, u32[]{:S(2)}) %all-to-all-start) | async-done | bytes 458784 | tf_op jit(solution)/shard_map/all_to_all | solution.py:382
  33.2 0.0 copy-done
  33.2 1.4 %lambdas.1 = (f32[1,128]{1,0:T(1,128)S(1)}, f32[1,128]{1,0:T(1,128)S(1)}, f32[2,1536]{1,0:T(2,128)S(1)}, bf16[16,2,2304]{2,1,0:T(2,128)(2,1)}) custom-call(f32[12,128,128]{2,1,0:T(8,128)S(1)} %get-tuple-element.18.first_ref, f32[12,128,128]{2,1,0:T(8,128)S(1)} %get-tuple-element.19.second_ref, f32[12,128]{1,0:T(8,128)S(1)} %get-tuple-element.20.own_ref, ...), custom_call_target="tpu_custom_call" | custom-call | tf_op jit(solution)/shard_map/lambdas/pallas_call | solution.py:396
  34.7 4.2 %all-to-all-start.1 = ((bf16[16,2,2304]{2,1,0:T(2,128)(2,1)}), bf16[16,2,2304]{2,1,0:T(2,128)(2,1)S(1)}, u32[]{:S(2)}, u32[]{:S(2)}) async-start(bf16[16,2,2304]{2,1,0:T(2,128)(2,1)} %get-tuple-element.31), calls=%async_computation.1 | async-start | bytes 294912 | tf_op jit(solution)/shard_map/all_to_all | solution.py:421
  38.8 10.1 %all-to-all-done.1.side_ref = bf16[16,2,2304]{2,1,0:T(2,128)(2,1)S(1)} async-done(((bf16[16,2,2304]{2,1,0:T(2,128)(2,1)}), bf16[16,2,2304]{2,1,0:T(2,128)(2,1)S(1)}, u32[]{:S(2)}, u32[]{:S(2)}) %all-to-all-start.1) | async-done | bytes 147488 | tf_op jit(solution)/shard_map/all_to_all | solution.py:421
  48.9 0.6 collective-permute-start
  49.5 0.7 %fusion = f32[64]{0:T(128)S(1)} fusion(bf16[64,2,1792]{2,1,0:T(2,128)(2,1)S(1)} %all-to-all-done.data_ref), kind=kLoop, calls=%fused_computation.1 | loop fusion | flops 294848 | bytes 196864 | tf_op jit(solution)/shard_map/reduce_sum | solution.py:422
  50.3 2.5 %collective-permute-start.2 = (bf16[16,2,2304]{2,1,0:T(2,128)(2,1)S(1)}, bf16[16,2,2304]{2,1,0:T(2,128)(2,1)S(1)}, u32[]{:S(2)}, u32[]{:S(2)}) collective-permute-start(bf16[16,2,2304]{2,1,0:T(2,128)(2,1)S(1)} %all-to-all-done.1.side_ref), channel_id=1, source_target_pairs={{0,4},{4,0},{8,12},{12,8},{16,20},{20,16},{24,28},{28,24},{32,36},... | collective-permute-start | bytes 442376 | tf_op jit(solution)/shard_map/ppermute | solution.py:439
  52.8 0.2 collective-permute-done.side_ref
  52.9 3.4 %collective-permute-start.1 = (bf16[16,2,2304]{2,1,0:T(2,128)(2,1)S(1)}, bf16[16,2,2304]{2,1,0:T(2,128)(2,1)S(1)}, u32[]{:S(2)}, u32[]{:S(2)}) collective-permute-start(bf16[16,2,2304]{2,1,0:T(2,128)(2,1)S(1)} %collective-permute-done.side_ref), channel_id=1, source_target_pairs={{0,4},{4,0},{8,12},{12,8},{16,20},{20,16},{24,28},{28,24},{32,36},... | collective-permute-start | bytes 442376 | tf_op jit(solution)/shard_map/ppermute | solution.py:440
  56.4 0.5 and_select_fusion.filled_ref
  56.9 2.4 %plan.1 = (s32[832]{0:T(1024)S(4)}, s32[4]{0:T(128)S(4)}, f32[1,128]{1,0:T(1,128)}, f32[1,128]{1,0:T(1,128)}, f32[2,1536]{1,0:T(2,128)}) custom-call(s32[64]{0:T(128)} %and_select_fusion.filled_ref, f32[1,128]{1,0:T(1,128)S(1)} %get-tuple-element.23.plus_in, f32[1,128]{1,0:T(1,128)S(1)} %get-tuple-element.24.minus_in, f32[2,1536]{1,0:T(2,128)S(1)} %get-tuple-element.25.grad_in), custom_call_target="tpu_custom_call" | custom-call | tf_op jit(solution)/shard_map/plan/pallas_call | solution.py:423
  59.2 2.8 %part.3.refs_0_ = f32[2,128,128]{2,1,0:T(8,128)S(1)} custom-call(s32[1]{0:T(128)} %bitcast.8.core_ref, s32[832]{0:T(1024)S(4)} %get-tuple-element.29.list_ref, s32[4]{0:T(128)S(4)} %get-tuple-element.30.total_ref, bf16[64,2,1792]{2,1,0:T(2,128)(2,1)S(1)} %all-to-all-done.data_ref, bf16[16,2,2304]{2,1,0:T(2,128)(2,1)S(1)} %all-to-all-done.1.side_ref), custom_call_target="tpu_custom_call" | custom-call | tf_op jit(solution)/shard_map/part/pallas_call | solution.py:341
  62.0 0.0 collective-permute-done.2.side_ref
  62.1 2.8 %part.4.refs_0_ = f32[2,128,128]{2,1,0:T(8,128)S(1)} custom-call(s32[1]{0:T(128)} %bitcast.7.core_ref, s32[832]{0:T(1024)S(4)} %get-tuple-element.29.list_ref, s32[4]{0:T(128)S(4)} %get-tuple-element.30.total_ref, bf16[64,2,1792]{2,1,0:T(2,128)(2,1)S(1)} %all-to-all-done.data_ref, bf16[16,2,2304]{2,1,0:T(2,128)(2,1)S(1)} %collective-permute-done.2.side_ref, ...), custom_call_target="tpu_custom_call" | custom-call | tf_op jit(solution)/shard_map/part/pallas_call | solution.py:341
  64.9 2.9 %part.5.before_ref = f32[2,128,128]{2,1,0:T(8,128)S(1)} custom-call(s32[1]{0:T(128)} %bitcast.6.core_ref, s32[832]{0:T(1024)S(4)} %get-tuple-element.29.list_ref, s32[4]{0:T(128)S(4)} %get-tuple-element.30.total_ref, bf16[64,2,1792]{2,1,0:T(2,128)(2,1)S(1)} %all-to-all-done.data_ref, bf16[16,2,2304]{2,1,0:T(2,128)(2,1)S(1)} %collective-permute-done.side_ref, ...), custom_call_target="tpu_custom_call" | custom-call | tf_op jit(solution)/shard_map/part/pallas_call | solution.py:341
  67.8 0.0 collective-permute-done.1.side_ref
  67.8 3.5 %last_part.1 = f32[2,64,256]{2,1,0:T(8,128)} custom-call(s32[1]{0:T(128)} %bitcast.5.core_ref, s32[832]{0:T(1024)S(4)} %get-tuple-element.29.list_ref, s32[4]{0:T(128)S(4)} %get-tuple-element.30.total_ref, bf16[64,2,1792]{2,1,0:T(2,128)(2,1)S(1)} %all-to-all-done.data_ref, bf16[16,2,2304]{2,1,0:T(2,128)(2,1)S(1)} %collective-permute-done.1.side_ref, ...), custom_call_target="tpu_custom_call" | custom-call | tf_op jit(solution)/shard_map/last_part/pallas_call | solution.py:341
Async XLA Ops:
  3.7 29.5 %all-to-all-start = ((bf16[64,2,1792]{2,1,0:T(2,128)(2,1)}), bf16[64,2,1792]{2,1,0:T(2,128)(2,1)S(1)}, u32[]{:S(2)}, u32[]{:S(2)}) async-start(bf16[64,2,1792]{2,1,0:T(2,128)(2,1)} %pair_terms.1), calls=%async_computation | async-start | bytes 917504 | tf_op jit(solution)/shard_map/all_to_all | solution.py:382
  18.5 14.8 %copy-start = (s32[1536]{0:T(1024)S(1)}, s32[1536]{0:T(1024)}, u32[]{:S(2)}) copy-start(s32[1536]{0:T(1024)} %param.13) | copy-start | bytes 18436
  34.7 14.3 %all-to-all-start.1 = ((bf16[16,2,2304]{2,1,0:T(2,128)(2,1)}), bf16[16,2,2304]{2,1,0:T(2,128)(2,1)S(1)}, u32[]{:S(2)}, u32[]{:S(2)}) async-start(bf16[16,2,2304]{2,1,0:T(2,128)(2,1)} %get-tuple-element.31), calls=%async_computation.1 | async-start | bytes 294912 | tf_op jit(solution)/shard_map/all_to_all | solution.py:421
  48.9 4.0 %collective-permute-start = (bf16[16,2,2304]{2,1,0:T(2,128)(2,1)S(1)}, bf16[16,2,2304]{2,1,0:T(2,128)(2,1)S(1)}, u32[]{:S(2)}, u32[]{:S(2)}) collective-permute-start(bf16[16,2,2304]{2,1,0:T(2,128)(2,1)S(1)} %all-to-all-done.1.side_ref), channel_id=1, source_target_pairs={{0,8},{4,12},{8,0},{12,4},{16,24},{20,28},{24,16},{28,20},{32,40},... | collective-permute-start | bytes 442376 | tf_op jit(solution)/shard_map/ppermute | solution.py:438
  50.3 11.8 %collective-permute-start.2 = (bf16[16,2,2304]{2,1,0:T(2,128)(2,1)S(1)}, bf16[16,2,2304]{2,1,0:T(2,128)(2,1)S(1)}, u32[]{:S(2)}, u32[]{:S(2)}) collective-permute-start(bf16[16,2,2304]{2,1,0:T(2,128)(2,1)S(1)} %all-to-all-done.1.side_ref), channel_id=1, source_target_pairs={{0,4},{4,0},{8,12},{12,8},{16,20},{20,16},{24,28},{28,24},{32,36},... | collective-permute-start | bytes 442376 | tf_op jit(solution)/shard_map/ppermute | solution.py:439
  52.9 14.8 %collective-permute-start.1 = (bf16[16,2,2304]{2,1,0:T(2,128)(2,1)S(1)}, bf16[16,2,2304]{2,1,0:T(2,128)(2,1)S(1)}, u32[]{:S(2)}, u32[]{:S(2)}) collective-permute-start(bf16[16,2,2304]{2,1,0:T(2,128)(2,1)S(1)} %collective-permute-done.side_ref), channel_id=1, source_target_pairs={{0,4},{4,0},{8,12},{12,8},{16,20},{20,16},{24,28},{28,24},{32,36},... | collective-permute-start | bytes 442376 | tf_op jit(solution)/shard_map/ppermute | solution.py:440

commit v12 on v11

--- a/solution.py
+++ b/solution.py
@@ -195,6 +195,11 @@
     side_ref[...] = jnp.broadcast_to(flat[...].astype(jnp.bfloat16)[None], side_ref.shape)
 
 
+def owner_of(chip, part):
+    high = lax.shift_right_logical(chip, 2)
+    return 16 * high + 2 * (chip - 4 * high) + part
+
+
 def plan_kernel(
     filled_ref, plus_in, minus_in, grad_in, list_ref, total_ref, plus_ref, minus_ref, grad_ref
 ):
@@ -208,7 +213,7 @@
 
         def one_block(chip, carry):
             at, spare = carry
-            used = filled_ref[PARTS * chip + core]
+            used = filled_ref[owner_of(chip, 8 * (core // 2) + core % 2)]
             for group in range(groups):
                 list_ref[base + at + group] = chip * 16 + group
             return at + used, jnp.where(used < groups, chip * 16 + groups - 1, spare)
@@ -222,6 +227,7 @@
 def accumulate(core, list_ref, total_ref, data_ref, side_ref, accs):
     base = core * (list_ref.shape[0] // PARTS)
     groups = side_ref.shape[2] * 2 // (3 * POS)
+    part = 8 * lax.shift_right_logical(core, 1) + lax.bitwise_and(core, 1)
     rows_a = lax.broadcasted_iota(jnp.int32, (2 * LEAVES, TILE), 0).astype(jnp.bfloat16)
     rows_b = lax.broadcasted_iota(jnp.int32, (HALF, TILE), 0).astype(jnp.bfloat16)
     zero = jnp.zeros((), jnp.bfloat16)
@@ -239,7 +245,7 @@
                 late = group >= groups // 2
                 place = groups + group - jnp.where(late, groups // 2, 0)
                 here = pl.ds(pl.multiple_of(group * POS, POS), POS)
-                bins.append(data_ref[PARTS * chip + core, :, here])
+                bins.append(data_ref[owner_of(chip, part), :, here])
                 sides.append(side_ref[chip, :, here])
                 pair = side_ref[chip, :, pl.ds(pl.multiple_of(place * POS, POS), POS)]
                 leaves.append(jnp.where(late, pair[1:2], pair[0:1]))
@@ -417,7 +423,10 @@
         in_vmem(leaf.reshape(queries, POS)),
         in_vmem(data),
     )
-    alike = [list(range(part, shards, PARTS)) for part in range(PARTS)]
+    alike = [
+        [16 * (chip // 4) + 2 * (chip % 4) + 8 * (part // 2) + part % 2 for chip in range(16)]
+        for part in range(PARTS)
+    ]
     side = lax.all_to_all(side, "doc", 0, 0, axis_index_groups=alike, tiled=True)
     shown = jnp.sum((data[:, 0, :slots] >= 0).astype(f32), axis=1).astype(jnp.int32)
     *plan, t_plus, t_minus, gradients = pl.pallas_call(
@@ -433,8 +442,9 @@
         out_specs=(SMEM, SMEM, VMEM, VMEM, VMEM),
         name="plan",
     )((shown + (POS - 1)) // POS, in_vmem(t_plus), in_vmem(t_minus), in_vmem(gradients))
-    swap = [[(at, at ^ bit) for at in range(shards)] for bit in (1, 2)]
-    own = lax.rem(lax.axis_index("doc"), PARTS)
+    swap = [[(at, at ^ bit) for at in range(shards)] for bit in (1, 8)]
+    index = lax.axis_index("doc")
+    own = 2 * lax.rem(index // 8, 2) + lax.rem(index, 2)
     side_far = lax.ppermute(side, "doc", swap[1])
     side_near = lax.ppermute(side, "doc", swap[0])
     side_last = lax.ppermute(side_far, "doc", swap[0])

time: 71.6 us -> 70.7 us (0.987)
  waiting for transfers between devices: 25 us -> 24.2 us
  transfers between devices with their start and end apart: 5 -> 5, of which waited for: 3 -> 2; matrix products, arithmetic and copies ran while one was open for 2% -> 2% of each run, Pallas kernels for 18% -> 18%
where the time goes in v12:
time: 70.7 us; the launch traced here: 70.4 us
  waiting for transfers between devices  24.2 us (34%)
  starting transfers between devices  24 us (34%)
  Pallas kernels  20.3 us (29%)
  other arithmetic  1.27 us (2%)
  between operations  0.74 us (1%)
    all_to_all x1, waiting for transfers between devices, body(): data = lax.all_to_all(sent, 'doc', 0, 0, tiled=True)  14.7 us
    all_to_all x1, starting transfers between devices, body(): data = lax.all_to_all(sent, 'doc', 0, 0, tiled=True)  13.2 us
    pallas_call x4, Pallas kernels, hist_of(): pl.pallas_call(last_kernel if last else part_kernel, out_shape=out_shape,...  11.7 us
    all_to_all x1, waiting for transfers between devices, body(): lax.all_to_all(side, 'doc', 0, 0, axis_index_groups=alike, tiled=True)  9.41 us
    all_to_all x1, starting transfers between devices, body(): lax.all_to_all(side, 'doc', 0, 0, axis_index_groups=alike, tiled=True)  4 us
    ppermute x1, starting transfers between devices, body(): side_last = lax.ppermute(side_far, 'doc', swap[0])  3.35 us
    pallas_call x1, Pallas kernels, body(): pl.pallas_call(pair_kernel, out_shape=jax.ShapeDtypeStruct(sent_shape, jn...  3.05 us
    ppermute x1, starting transfers between devices, body(): side_near = lax.ppermute(side, 'doc', swap[0])  2.62 us
  transfers between devices with their start and end apart: 5, of which 2 were waited for; matrix products, arithmetic and copies ran while one was open for 2% of the time, Pallas kernels for 18%

profile of v12, /device:TPU:1, one launch (start us, length us, event | category | flops | bytes accessed | tf_op | source)
XLA Modules:
  0.0 70.4 jit_solution(10860122128979312983)
XLA Ops:
  0.6 3.1 %pair_terms.1 = bf16[64,2,1792]{2,1,0:T(2,128)(2,1)} custom-call(f32[136,128]{1,0:T(8,128)} %constant.49.clone.refs_0_.gap_ref, f32[12,128]{1,0:T(8,128)} %scores_ref.1, s32[12,128]{1,0:T(8,128)} %clicks_ref.1, s32[12]{0:T(128)} %lengths_ref.1, f32[1,128]{1,0:T(1,128)} %bitcast.10, f32[1,128]{1,0:T(1,128)} %bitcast.11, s32[128,1536]{1,0:T(8,128)} %refs_6_.1), custom_call_target="tpu_custom_call" | custom-call | tf_op jit(solution)/shard_map/pair_terms/pallas_call | solution.py:369
  3.7 13.2 %all-to-all-start = ((bf16[64,2,1792]{2,1,0:T(2,128)(2,1)}), bf16[64,2,1792]{2,1,0:T(2,128)(2,1)S(1)}, u32[]{:S(2)}, u32[]{:S(2)}) async-start(bf16[64,2,1792]{2,1,0:T(2,128)(2,1)} %pair_terms.1), calls=%async_computation | async-start | bytes 917504 | tf_op jit(solution)/shard_map/all_to_all | solution.py:388
  16.9 1.6 %ready_pairs.1 = (f32[12,128,128]{2,1,0:T(8,128)S(1)}, f32[12,128,128]{2,1,0:T(8,128)S(1)}, f32[12,128]{1,0:T(8,128)S(1)}, f32[12,128]{1,0:T(8,128)S(1)}, s32[12]{0:T(128)S(4)}) custom-call(f32[136,128]{1,0:T(8,128)} %constant.49.clone.refs_0_.gap_ref, f32[12,128]{1,0:T(8,128)} %scores_ref.1, s32[12,128]{1,0:T(8,128)} %clicks_ref.1, s32[12]{0:T(128)} %lengths_ref.1), custom_call_target="tpu_custom_call" | custom-call | tf_op jit(solution)/shard_map/ready_pairs/pallas_call | solution.py:389
  18.5 0.0 copy-start
  18.5 14.7 %all-to-all-done.data_ref = bf16[64,2,1792]{2,1,0:T(2,128)(2,1)S(1)} async-done(((bf16[64,2,1792]{2,1,0:T(2,128)(2,1)}), bf16[64,2,1792]{2,1,0:T(2,128)(2,1)S(1)}, u32[]{:S(2)}, u32[]{:S(2)}) %all-to-all-start) | async-done | bytes 458784 | tf_op jit(solution)/shard_map/all_to_all | solution.py:388
  33.2 0.0 copy-done
  33.2 1.4 %lambdas.1 = (f32[1,128]{1,0:T(1,128)S(1)}, f32[1,128]{1,0:T(1,128)S(1)}, f32[2,1536]{1,0:T(2,128)S(1)}, bf16[16,2,2304]{2,1,0:T(2,128)(2,1)}) custom-call(f32[12,128,128]{2,1,0:T(8,128)S(1)} %get-tuple-element.18.first_ref, f32[12,128,128]{2,1,0:T(8,128)S(1)} %get-tuple-element.19.second_ref, f32[12,128]{1,0:T(8,128)S(1)} %get-tuple-element.20.own_ref, ...), custom_call_target="tpu_custom_call" | custom-call | tf_op jit(solution)/shard_map/lambdas/pallas_call | solution.py:402
  34.7 4.0 %all-to-all-start.1 = ((bf16[16,2,2304]{2,1,0:T(2,128)(2,1)}), bf16[16,2,2304]{2,1,0:T(2,128)(2,1)S(1)}, u32[]{:S(2)}, u32[]{:S(2)}) async-start(bf16[16,2,2304]{2,1,0:T(2,128)(2,1)} %get-tuple-element.31), calls=%async_computation.1 | async-start | bytes 294912 | tf_op jit(solution)/shard_map/all_to_all | solution.py:430
  38.7 9.4 %all-to-all-done.1.side_ref = bf16[16,2,2304]{2,1,0:T(2,128)(2,1)S(1)} async-done(((bf16[16,2,2304]{2,1,0:T(2,128)(2,1)}), bf16[16,2,2304]{2,1,0:T(2,128)(2,1)S(1)}, u32[]{:S(2)}, u32[]{:S(2)}) %all-to-all-start.1) | async-done | bytes 147488 | tf_op jit(solution)/shard_map/all_to_all | solution.py:430
  48.1 0.9 %collective-permute-start = (bf16[16,2,2304]{2,1,0:T(2,128)(2,1)S(1)}, bf16[16,2,2304]{2,1,0:T(2,128)(2,1)S(1)}, u32[]{:S(2)}, u32[]{:S(2)}) collective-permute-start(bf16[16,2,2304]{2,1,0:T(2,128)(2,1)S(1)} %all-to-all-done.1.side_ref), channel_id=1, source_target_pairs={{0,32},{4,36},{8,40},{12,44},{16,48},{20,52},{24,56},{28,60},{32,0... | collective-permute-start | bytes 442376 | tf_op jit(solution)/shard_map/ppermute | solution.py:448
  49.0 0.7 %fusion = f32[64]{0:T(128)S(1)} fusion(bf16[64,2,1792]{2,1,0:T(2,128)(2,1)S(1)} %all-to-all-done.data_ref), kind=kLoop, calls=%fused_computation.1 | loop fusion | flops 294848 | bytes 196864 | tf_op jit(solution)/shard_map/reduce_sum | solution.py:431
  49.7 2.6 %collective-permute-start.2 = (bf16[16,2,2304]{2,1,0:T(2,128)(2,1)S(1)}, bf16[16,2,2304]{2,1,0:T(2,128)(2,1)S(1)}, u32[]{:S(2)}, u32[]{:S(2)}) collective-permute-start(bf16[16,2,2304]{2,1,0:T(2,128)(2,1)S(1)} %all-to-all-done.1.side_ref), channel_id=1, source_target_pairs={{0,4},{4,0},{8,12},{12,8},{16,20},{20,16},{24,28},{28,24},{32,36},... | collective-permute-start | bytes 442376 | tf_op jit(solution)/shard_map/ppermute | solution.py:449
  52.3 0.0 collective-permute-done.side_ref
  52.3 3.4 %collective-permute-start.1 = (bf16[16,2,2304]{2,1,0:T(2,128)(2,1)S(1)}, bf16[16,2,2304]{2,1,0:T(2,128)(2,1)S(1)}, u32[]{:S(2)}, u32[]{:S(2)}) collective-permute-start(bf16[16,2,2304]{2,1,0:T(2,128)(2,1)S(1)} %collective-permute-done.side_ref), channel_id=1, source_target_pairs={{0,4},{4,0},{8,12},{12,8},{16,20},{20,16},{24,28},{28,24},{32,36},... | collective-permute-start | bytes 442376 | tf_op jit(solution)/shard_map/ppermute | solution.py:450
  55.7 0.5 and_select_fusion.filled_ref
  56.2 2.4 %plan.1 = (s32[832]{0:T(1024)S(4)}, s32[4]{0:T(128)S(4)}, f32[1,128]{1,0:T(1,128)}, f32[1,128]{1,0:T(1,128)}, f32[2,1536]{1,0:T(2,128)}) custom-call(s32[64]{0:T(128)} %and_select_fusion.filled_ref, f32[1,128]{1,0:T(1,128)S(1)} %get-tuple-element.23.plus_in, f32[1,128]{1,0:T(1,128)S(1)} %get-tuple-element.24.minus_in, f32[2,1536]{1,0:T(2,128)S(1)} %get-tuple-element.25.grad_in), custom_call_target="tpu_custom_call" | custom-call | tf_op jit(solution)/shard_map/plan/pallas_call | solution.py:432
  58.6 2.8 %part.3.refs_0_ = f32[2,128,128]{2,1,0:T(8,128)S(1)} custom-call(s32[1]{0:T(128)} %bitcast.8.core_ref, s32[832]{0:T(1024)S(4)} %get-tuple-element.29.list_ref, s32[4]{0:T(128)S(4)} %get-tuple-element.30.total_ref, bf16[64,2,1792]{2,1,0:T(2,128)(2,1)S(1)} %all-to-all-done.data_ref, bf16[16,2,2304]{2,1,0:T(2,128)(2,1)S(1)} %all-to-all-done.1.side_ref), custom_call_target="tpu_custom_call" | custom-call | tf_op jit(solution)/shard_map/part/pallas_call | solution.py:347
  61.4 0.0 collective-permute-done.2.side_ref
  61.4 2.8 %part.4.refs_0_ = f32[2,128,128]{2,1,0:T(8,128)S(1)} custom-call(s32[1]{0:T(128)} %bitcast.7.core_ref, s32[832]{0:T(1024)S(4)} %get-tuple-element.29.list_ref, s32[4]{0:T(128)S(4)} %get-tuple-element.30.total_ref, bf16[64,2,1792]{2,1,0:T(2,128)(2,1)S(1)} %all-to-all-done.data_ref, bf16[16,2,2304]{2,1,0:T(2,128)(2,1)S(1)} %collective-permute-done.2.side_ref, ...), custom_call_target="tpu_custom_call" | custom-call | tf_op jit(solution)/shard_map/part/pallas_call | solution.py:347
  64.2 2.8 %part.5.before_ref = f32[2,128,128]{2,1,0:T(8,128)S(1)} custom-call(s32[1]{0:T(128)} %bitcast.6.core_ref, s32[832]{0:T(1024)S(4)} %get-tuple-element.29.list_ref, s32[4]{0:T(128)S(4)} %get-tuple-element.30.total_ref, bf16[64,2,1792]{2,1,0:T(2,128)(2,1)S(1)} %all-to-all-done.data_ref, bf16[16,2,2304]{2,1,0:T(2,128)(2,1)S(1)} %collective-permute-done.side_ref, ...), custom_call_target="tpu_custom_call" | custom-call | tf_op jit(solution)/shard_map/part/pallas_call | solution.py:347
  67.0 0.0 collective-permute-done.1.side_ref
  67.0 3.4 %last_part.1 = f32[2,64,256]{2,1,0:T(8,128)} custom-call(s32[1]{0:T(128)} %bitcast.5.core_ref, s32[832]{0:T(1024)S(4)} %get-tuple-element.29.list_ref, s32[4]{0:T(128)S(4)} %get-tuple-element.30.total_ref, bf16[64,2,1792]{2,1,0:T(2,128)(2,1)S(1)} %all-to-all-done.data_ref, bf16[16,2,2304]{2,1,0:T(2,128)(2,1)S(1)} %collective-permute-done.1.side_ref, ...), custom_call_target="tpu_custom_call" | custom-call | tf_op jit(solution)/shard_map/last_part/pallas_call | solution.py:347
Async XLA Ops:
  3.7 29.5 %all-to-all-start = ((bf16[64,2,1792]{2,1,0:T(2,128)(2,1)}), bf16[64,2,1792]{2,1,0:T(2,128)(2,1)S(1)}, u32[]{:S(2)}, u32[]{:S(2)}) async-start(bf16[64,2,1792]{2,1,0:T(2,128)(2,1)} %pair_terms.1), calls=%async_computation | async-start | bytes 917504 | tf_op jit(solution)/shard_map/all_to_all | solution.py:388
  18.5 14.8 %copy-start = (s32[1536]{0:T(1024)S(1)}, s32[1536]{0:T(1024)}, u32[]{:S(2)}) copy-start(s32[1536]{0:T(1024)} %param.13) | copy-start | bytes 18436
  34.7 13.4 %all-to-all-start.1 = ((bf16[16,2,2304]{2,1,0:T(2,128)(2,1)}), bf16[16,2,2304]{2,1,0:T(2,128)(2,1)S(1)}, u32[]{:S(2)}, u32[]{:S(2)}) async-start(bf16[16,2,2304]{2,1,0:T(2,128)(2,1)} %get-tuple-element.31), calls=%async_computation.1 | async-start | bytes 294912 | tf_op jit(solution)/shard_map/all_to_all | solution.py:430
  48.1 4.2 %collective-permute-start = (bf16[16,2,2304]{2,1,0:T(2,128)(2,1)S(1)}, bf16[16,2,2304]{2,1,0:T(2,128)(2,1)S(1)}, u32[]{:S(2)}, u32[]{:S(2)}) collective-permute-start(bf16[16,2,2304]{2,1,0:T(2,128)(2,1)S(1)} %all-to-all-done.1.side_ref), channel_id=1, source_target_pairs={{0,32},{4,36},{8,40},{12,44},{16,48},{20,52},{24,56},{28,60},{32,0... | collective-permute-start | bytes 442376 | tf_op jit(solution)/shard_map/ppermute | solution.py:448
  49.7 11.7 %collective-permute-start.2 = (bf16[16,2,2304]{2,1,0:T(2,128)(2,1)S(1)}, bf16[16,2,2304]{2,1,0:T(2,128)(2,1)S(1)}, u32[]{:S(2)}, u32[]{:S(2)}) collective-permute-start(bf16[16,2,2304]{2,1,0:T(2,128)(2,1)S(1)} %all-to-all-done.1.side_ref), channel_id=1, source_target_pairs={{0,4},{4,0},{8,12},{12,8},{16,20},{20,16},{24,28},{28,24},{32,36},... | collective-permute-start | bytes 442376 | tf_op jit(solution)/shard_map/ppermute | solution.py:449
  52.3 14.7 %collective-permute-start.1 = (bf16[16,2,2304]{2,1,0:T(2,128)(2,1)S(1)}, bf16[16,2,2304]{2,1,0:T(2,128)(2,1)S(1)}, u32[]{:S(2)}, u32[]{:S(2)}) collective-permute-start(bf16[16,2,2304]{2,1,0:T(2,128)(2,1)S(1)} %collective-permute-done.side_ref), channel_id=1, source_target_pairs={{0,4},{4,0},{8,12},{12,8},{16,20},{20,16},{24,28},{28,24},{32,36},... | collective-permute-start | bytes 442376 | tf_op jit(solution)/shard_map/ppermute | solution.py:450

commit v13 on v12

--- a/solution.py
+++ b/solution.py
@@ -1,3 +1,5 @@
+import functools
+
 import jax
 import jax.numpy as jnp
 import numpy as np
@@ -224,7 +226,7 @@
         total_ref[core] = (at + 2 * STEP - 1) // (2 * STEP)
 
 
-def accumulate(core, list_ref, total_ref, data_ref, side_ref, accs):
+def accumulate(core, begin, end, list_ref, data_ref, side_ref, accs):
     base = core * (list_ref.shape[0] // PARTS)
     groups = side_ref.shape[2] * 2 // (3 * POS)
     part = 8 * lax.shift_right_logical(core, 1) + lax.bitwise_and(core, 1)
@@ -268,29 +270,35 @@
             pltpu.matmul_acc_lhs(accs[unit], jnp.concatenate(left, axis=0), register)
 
     def wide_step(step, carry):
-        tiles_at(step * (STEP * WIDE), STEP * WIDE)
+        tiles_at((begin + step * WIDE) * STEP, STEP * WIDE)
         return carry
 
     def step(step, carry):
         tiles_at(step * STEP, STEP)
         return carry
 
+    wide = (end - begin) // WIDE
+    lax.fori_loop(0, wide, wide_step, 0)
+    lax.fori_loop(begin + wide * WIDE, end, step, 0)
+
+
+def summed(share, core_ref, list_ref, total_ref, data_ref, side_ref, finish):
+    core = core_ref[0]
     total = total_ref[core]
-    wide = total // WIDE
-    lax.fori_loop(0, wide, wide_step, 0)
-    lax.fori_loop(wide * WIDE, total, step, 0)
-
-
-def summed(core, list_ref, total_ref, data_ref, side_ref, finish):
+    early = lax.shift_right_logical(total * lax.bitwise_and(core, 1), 1)
+    begin = early if share == "late" else 0
+    end = early if share == "early" else total
+
     def run(acc_a, acc_b):
-        accumulate(core, list_ref, total_ref, data_ref, side_ref, (acc_a, acc_b))
-        finish(pltpu.matmul_pop(acc_a) + pltpu.matmul_pop(acc_b))
+        accumulate(core, begin, end, list_ref, data_ref, side_ref, (acc_a, acc_b))
+        total = pltpu.matmul_pop(acc_a) + pltpu.matmul_pop(acc_b)
+        finish(jnp.where(end > begin, total, 0.0))
 
     shape = (8 * LEAVES, BINS)
     pl.run_scoped(run, pltpu.ACC(0)(shape, jnp.float32), pltpu.ACC(1)(shape, jnp.float32))
 
 
-def part_kernel(core_ref, list_ref, total_ref, data_ref, side_ref, *refs):
+def part_kernel(share, core_ref, list_ref, total_ref, data_ref, side_ref, *refs):
     rows = 4 * LEAVES
     out_ref = refs[-1]
 
@@ -301,10 +309,10 @@
             ]
             out_ref[feature] = mine if len(refs) == 1 else mine + refs[0][feature]
 
-    summed(core_ref[0], list_ref, total_ref, data_ref, side_ref, finish)
-
-
-def last_kernel(core_ref, list_ref, total_ref, data_ref, side_ref, before_ref, out_ref):
+    summed(share, core_ref, list_ref, total_ref, data_ref, side_ref, finish)
+
+
+def last_kernel(share, core_ref, list_ref, total_ref, data_ref, side_ref, before_ref, out_ref):
     rows = 4 * LEAVES
 
     def finish(total):
@@ -321,7 +329,7 @@
                         high * HALF : (high + 1) * HALF,
                     ] = mine[at : at + LEAVES]
 
-    summed(core_ref[0], list_ref, total_ref, data_ref, side_ref, finish)
+    summed(share, core_ref, list_ref, total_ref, data_ref, side_ref, finish)
 
 
 VMEM = pl.BlockSpec(memory_space=pltpu.VMEM)
@@ -336,7 +344,7 @@
     return pltpu.with_memory_space_constraint(array, pltpu.SMEM)
 
 
-def hist_of(core, plan, data, side, before=None, last=False):
+def hist_of(core, plan, data, side, before=None, last=False, share="all"):
     given = [in_vmem(data), in_vmem(side)]
     if before is not None:
         given.append(in_vmem(before))
@@ -345,7 +353,7 @@
     else:
         out_shape = pltpu.VMEM((2, 4 * LEAVES, HALF), jnp.float32)
     return pl.pallas_call(
-        last_kernel if last else part_kernel,
+        functools.partial(last_kernel if last else part_kernel, share),
         out_shape=out_shape,
         in_specs=[SMEM, SMEM, SMEM] + [VMEM] * len(given),
         out_specs=VMEM,
@@ -448,7 +456,8 @@
     side_far = lax.ppermute(side, "doc", swap[1])
     side_near = lax.ppermute(side, "doc", swap[0])
     side_last = lax.ppermute(side_far, "doc", swap[0])
-    partial = hist_of(own, plan, data, side)
+    partial = hist_of(own, plan, data, side, share="early")
+    partial = hist_of(own, plan, data, side, partial, share="late")
     partial = hist_of(lax.bitwise_xor(own, 1), plan, data, side_near, partial)
     partial = hist_of(lax.bitwise_xor(own, 2), plan, data, side_far, partial)
     hist = hist_of(lax.bitwise_xor(own, 3), plan, data, side_last, partial, True)

time: 70.7 us -> 70.9 us (level)
    pallas_call x4 -> x5, Pallas kernels: 11.7 us -> 11.9 us  [hist_of(): pl.pallas_call(functools.partial(last_kernel if last else part_kernel, sh...]
where the time goes in v13:
time: 70.9 us; the launch traced here: 70.6 us
  waiting for transfers between devices  24.2 us (34%)
  starting transfers between devices  24 us (34%)
  Pallas kernels  20.4 us (29%)
  other arithmetic  1.27 us (2%)
  between operations  0.75 us (1%)
    all_to_all x1, waiting for transfers between devices, body(): data = lax.all_to_all(sent, 'doc', 0, 0, tiled=True)  14.7 us
    all_to_all x1, starting transfers between devices, body(): data = lax.all_to_all(sent, 'doc', 0, 0, tiled=True)  13.2 us
    pallas_call x5, Pallas kernels, hist_of(): pl.pallas_call(functools.partial(last_kernel if last else part_kernel, sh...  11.9 us
    all_to_all x1, waiting for transfers between devices, body(): lax.all_to_all(side, 'doc', 0, 0, axis_index_groups=alike, tiled=True)  9.41 us
    all_to_all x1, starting transfers between devices, body(): lax.all_to_all(side, 'doc', 0, 0, axis_index_groups=alike, tiled=True)  4 us
    ppermute x1, starting transfers between devices, body(): side_last = lax.ppermute(side_far, 'doc', swap[0])  3.35 us
    pallas_call x1, Pallas kernels, body(): pl.pallas_call(pair_kernel, out_shape=jax.ShapeDtypeStruct(sent_shape, jn...  3.05 us
    ppermute x1, starting transfers between devices, body(): side_near = lax.ppermute(side, 'doc', swap[0])  2.62 us
  transfers between devices with their start and end apart: 5, of which 2 were waited for; matrix products, arithmetic and copies ran while one was open for 2% of the time, Pallas kernels for 18%

profile of v13, /device:TPU:1, one launch (start us, length us, event | category | flops | bytes accessed | tf_op | source)
XLA Modules:
  0.0 70.6 jit_solution(9268549184880358727)
XLA Ops:
  0.6 3.1 %pair_terms.1 = bf16[64,2,1792]{2,1,0:T(2,128)(2,1)} custom-call(f32[136,128]{1,0:T(8,128)} %constant.49.clone.refs_0_.gap_ref, f32[12,128]{1,0:T(8,128)} %scores_ref.1, s32[12,128]{1,0:T(8,128)} %clicks_ref.1, s32[12]{0:T(128)} %lengths_ref.1, f32[1,128]{1,0:T(1,128)} %bitcast.10, f32[1,128]{1,0:T(1,128)} %bitcast.11, s32[128,1536]{1,0:T(8,128)} %refs_6_.1), custom_call_target="tpu_custom_call" | custom-call | tf_op jit(solution)/shard_map/pair_terms/pallas_call | solution.py:377
  3.7 13.2 %all-to-all-start = ((bf16[64,2,1792]{2,1,0:T(2,128)(2,1)}), bf16[64,2,1792]{2,1,0:T(2,128)(2,1)S(1)}, u32[]{:S(2)}, u32[]{:S(2)}) async-start(bf16[64,2,1792]{2,1,0:T(2,128)(2,1)} %pair_terms.1), calls=%async_computation | async-start | bytes 917504 | tf_op jit(solution)/shard_map/all_to_all | solution.py:396
  16.9 1.6 %ready_pairs.1 = (f32[12,128,128]{2,1,0:T(8,128)S(1)}, f32[12,128,128]{2,1,0:T(8,128)S(1)}, f32[12,128]{1,0:T(8,128)S(1)}, f32[12,128]{1,0:T(8,128)S(1)}, s32[12]{0:T(128)S(4)}) custom-call(f32[136,128]{1,0:T(8,128)} %constant.49.clone.refs_0_.gap_ref, f32[12,128]{1,0:T(8,128)} %scores_ref.1, s32[12,128]{1,0:T(8,128)} %clicks_ref.1, s32[12]{0:T(128)} %lengths_ref.1), custom_call_target="tpu_custom_call" | custom-call | tf_op jit(solution)/shard_map/ready_pairs/pallas_call | solution.py:397
  18.5 0.0 copy-start
  18.5 14.7 %all-to-all-done.data_ref = bf16[64,2,1792]{2,1,0:T(2,128)(2,1)S(1)} async-done(((bf16[64,2,1792]{2,1,0:T(2,128)(2,1)}), bf16[64,2,1792]{2,1,0:T(2,128)(2,1)S(1)}, u32[]{:S(2)}, u32[]{:S(2)}) %all-to-all-start) | async-done | bytes 458784 | tf_op jit(solution)/shard_map/all_to_all | solution.py:396
  33.2 0.0 copy-done
  33.2 1.4 %lambdas.1 = (f32[1,128]{1,0:T(1,128)S(1)}, f32[1,128]{1,0:T(1,128)S(1)}, f32[2,1536]{1,0:T(2,128)S(1)}, bf16[16,2,2304]{2,1,0:T(2,128)(2,1)}) custom-call(f32[12,128,128]{2,1,0:T(8,128)S(1)} %get-tuple-element.18.first_ref, f32[12,128,128]{2,1,0:T(8,128)S(1)} %get-tuple-element.19.second_ref, f32[12,128]{1,0:T(8,128)S(1)} %get-tuple-element.20.own_ref, ...), custom_call_target="tpu_custom_call" | custom-call | tf_op jit(solution)/shard_map/lambdas/pallas_call | solution.py:410
  34.7 4.0 %all-to-all-start.1 = ((bf16[16,2,2304]{2,1,0:T(2,128)(2,1)}), bf16[16,2,2304]{2,1,0:T(2,128)(2,1)S(1)}, u32[]{:S(2)}, u32[]{:S(2)}) async-start(bf16[16,2,2304]{2,1,0:T(2,128)(2,1)} %get-tuple-element.31), calls=%async_computation.1 | async-start | bytes 294912 | tf_op jit(solution)/shard_map/all_to_all | solution.py:438
  38.7 9.4 %all-to-all-done.1.side_ref = bf16[16,2,2304]{2,1,0:T(2,128)(2,1)S(1)} async-done(((bf16[16,2,2304]{2,1,0:T(2,128)(2,1)}), bf16[16,2,2304]{2,1,0:T(2,128)(2,1)S(1)}, u32[]{:S(2)}, u32[]{:S(2)}) %all-to-all-start.1) | async-done | bytes 147488 | tf_op jit(solution)/shard_map/all_to_all | solution.py:438
  48.1 0.9 %collective-permute-start = (bf16[16,2,2304]{2,1,0:T(2,128)(2,1)S(1)}, bf16[16,2,2304]{2,1,0:T(2,128)(2,1)S(1)}, u32[]{:S(2)}, u32[]{:S(2)}) collective-permute-start(bf16[16,2,2304]{2,1,0:T(2,128)(2,1)S(1)} %all-to-all-done.1.side_ref), channel_id=1, source_target_pairs={{0,32},{4,36},{8,40},{12,44},{16,48},{20,52},{24,56},{28,60},{32,0... | collective-permute-start | bytes 442376 | tf_op jit(solution)/shard_map/ppermute | solution.py:456
  49.0 0.7 %fusion = f32[64]{0:T(128)S(1)} fusion(bf16[64,2,1792]{2,1,0:T(2,128)(2,1)S(1)} %all-to-all-done.data_ref), kind=kLoop, calls=%fused_computation.1 | loop fusion | flops 294848 | bytes 196864 | tf_op jit(solution)/shard_map/reduce_sum | solution.py:439
  49.7 2.6 %collective-permute-start.2 = (bf16[16,2,2304]{2,1,0:T(2,128)(2,1)S(1)}, bf16[16,2,2304]{2,1,0:T(2,128)(2,1)S(1)}, u32[]{:S(2)}, u32[]{:S(2)}) collective-permute-start(bf16[16,2,2304]{2,1,0:T(2,128)(2,1)S(1)} %all-to-all-done.1.side_ref), channel_id=1, source_target_pairs={{0,4},{4,0},{8,12},{12,8},{16,20},{20,16},{24,28},{28,24},{32,36},... | collective-permute-start | bytes 442376 | tf_op jit(solution)/shard_map/ppermute | solution.py:457
  52.3 0.0 collective-permute-done.side_ref
  52.3 3.4 %collective-permute-start.1 = (bf16[16,2,2304]{2,1,0:T(2,128)(2,1)S(1)}, bf16[16,2,2304]{2,1,0:T(2,128)(2,1)S(1)}, u32[]{:S(2)}, u32[]{:S(2)}) collective-permute-start(bf16[16,2,2304]{2,1,0:T(2,128)(2,1)S(1)} %collective-permute-done.side_ref), channel_id=1, source_target_pairs={{0,4},{4,0},{8,12},{12,8},{16,20},{20,16},{24,28},{28,24},{32,36},... | collective-permute-start | bytes 442376 | tf_op jit(solution)/shard_map/ppermute | solution.py:458
  55.7 0.5 and_select_fusion.filled_ref
  56.2 2.4 %plan.1 = (s32[832]{0:T(1024)S(4)}, s32[4]{0:T(128)S(4)}, f32[1,128]{1,0:T(1,128)}, f32[1,128]{1,0:T(1,128)}, f32[2,1536]{1,0:T(2,128)}) custom-call(s32[64]{0:T(128)} %and_select_fusion.filled_ref, f32[1,128]{1,0:T(1,128)S(1)} %get-tuple-element.23.plus_in, f32[1,128]{1,0:T(1,128)S(1)} %get-tuple-element.24.minus_in, f32[2,1536]{1,0:T(2,128)S(1)} %get-tuple-element.25.grad_in), custom_call_target="tpu_custom_call" | custom-call | tf_op jit(solution)/shard_map/plan/pallas_call | solution.py:440
  58.6 1.4 %part.4.refs_0_ = f32[2,128,128]{2,1,0:T(8,128)S(1)} custom-call(s32[1]{0:T(128)} %bitcast.8.core_ref, s32[832]{0:T(1024)S(4)} %get-tuple-element.29.list_ref, s32[4]{0:T(128)S(4)} %get-tuple-element.30.total_ref, bf16[64,2,1792]{2,1,0:T(2,128)(2,1)S(1)} %all-to-all-done.data_ref, bf16[16,2,2304]{2,1,0:T(2,128)(2,1)S(1)} %all-to-all-done.1.side_ref), custom_call_target="tpu_custom_call" | custom-call | tf_op jit(solution)/shard_map/part/pallas_call | solution.py:355
  60.1 1.5 %part.5.refs_0_ = f32[2,128,128]{2,1,0:T(8,128)S(1)} custom-call(s32[1]{0:T(128)} %bitcast.8.core_ref, s32[832]{0:T(1024)S(4)} %get-tuple-element.29.list_ref, s32[4]{0:T(128)S(4)} %get-tuple-element.30.total_ref, bf16[64,2,1792]{2,1,0:T(2,128)(2,1)S(1)} %all-to-all-done.data_ref, bf16[16,2,2304]{2,1,0:T(2,128)(2,1)S(1)} %all-to-all-done.1.side_ref, ...), custom_call_target="tpu_custom_call" | custom-call | tf_op jit(solution)/shard_map/part/pallas_call | solution.py:355
  61.6 0.0 collective-permute-done.2.side_ref
  61.6 2.8 %part.6.refs_0_ = f32[2,128,128]{2,1,0:T(8,128)S(1)} custom-call(s32[1]{0:T(128)} %bitcast.7.core_ref, s32[832]{0:T(1024)S(4)} %get-tuple-element.29.list_ref, s32[4]{0:T(128)S(4)} %get-tuple-element.30.total_ref, bf16[64,2,1792]{2,1,0:T(2,128)(2,1)S(1)} %all-to-all-done.data_ref, bf16[16,2,2304]{2,1,0:T(2,128)(2,1)S(1)} %collective-permute-done.2.side_ref, ...), custom_call_target="tpu_custom_call" | custom-call | tf_op jit(solution)/shard_map/part/pallas_call | solution.py:355
  64.4 2.8 %part.7.before_ref = f32[2,128,128]{2,1,0:T(8,128)S(1)} custom-call(s32[1]{0:T(128)} %bitcast.6.core_ref, s32[832]{0:T(1024)S(4)} %get-tuple-element.29.list_ref, s32[4]{0:T(128)S(4)} %get-tuple-element.30.total_ref, bf16[64,2,1792]{2,1,0:T(2,128)(2,1)S(1)} %all-to-all-done.data_ref, bf16[16,2,2304]{2,1,0:T(2,128)(2,1)S(1)} %collective-permute-done.side_ref, ...), custom_call_target="tpu_custom_call" | custom-call | tf_op jit(solution)/shard_map/part/pallas_call | solution.py:355
  67.1 0.0 collective-permute-done.1.side_ref
  67.2 3.4 %last_part.1 = f32[2,64,256]{2,1,0:T(8,128)} custom-call(s32[1]{0:T(128)} %bitcast.5.core_ref, s32[832]{0:T(1024)S(4)} %get-tuple-element.29.list_ref, s32[4]{0:T(128)S(4)} %get-tuple-element.30.total_ref, bf16[64,2,1792]{2,1,0:T(2,128)(2,1)S(1)} %all-to-all-done.data_ref, bf16[16,2,2304]{2,1,0:T(2,128)(2,1)S(1)} %collective-permute-done.1.side_ref, ...), custom_call_target="tpu_custom_call" | custom-call | tf_op jit(solution)/shard_map/last_part/pallas_call | solution.py:355
Async XLA Ops:
  3.7 29.5 %all-to-all-start = ((bf16[64,2,1792]{2,1,0:T(2,128)(2,1)}), bf16[64,2,1792]{2,1,0:T(2,128)(2,1)S(1)}, u32[]{:S(2)}, u32[]{:S(2)}) async-start(bf16[64,2,1792]{2,1,0:T(2,128)(2,1)} %pair_terms.1), calls=%async_computation | async-start | bytes 917504 | tf_op jit(solution)/shard_map/all_to_all | solution.py:396
  18.5 14.8 %copy-start = (s32[1536]{0:T(1024)S(1)}, s32[1536]{0:T(1024)}, u32[]{:S(2)}) copy-start(s32[1536]{0:T(1024)} %param.13) | copy-start | bytes 18436
  34.7 13.4 %all-to-all-start.1 = ((bf16[16,2,2304]{2,1,0:T(2,128)(2,1)}), bf16[16,2,2304]{2,1,0:T(2,128)(2,1)S(1)}, u32[]{:S(2)}, u32[]{:S(2)}) async-start(bf16[16,2,2304]{2,1,0:T(2,128)(2,1)} %get-tuple-element.31), calls=%async_computation.1 | async-start | bytes 294912 | tf_op jit(solution)/shard_map/all_to_all | solution.py:438
  48.1 4.2 %collective-permute-start = (bf16[16,2,2304]{2,1,0:T(2,128)(2,1)S(1)}, bf16[16,2,2304]{2,1,0:T(2,128)(2,1)S(1)}, u32[]{:S(2)}, u32[]{:S(2)}) collective-permute-start(bf16[16,2,2304]{2,1,0:T(2,128)(2,1)S(1)} %all-to-all-done.1.side_ref), channel_id=1, source_target_pairs={{0,32},{4,36},{8,40},{12,44},{16,48},{20,52},{24,56},{28,60},{32,0... | collective-permute-start | bytes 442376 | tf_op jit(solution)/shard_map/ppermute | solution.py:456
  49.7 11.9 %collective-permute-start.2 = (bf16[16,2,2304]{2,1,0:T(2,128)(2,1)S(1)}, bf16[16,2,2304]{2,1,0:T(2,128)(2,1)S(1)}, u32[]{:S(2)}, u32[]{:S(2)}) collective-permute-start(bf16[16,2,2304]{2,1,0:T(2,128)(2,1)S(1)} %all-to-all-done.1.side_ref), channel_id=1, source_target_pairs={{0,4},{4,0},{8,12},{12,8},{16,20},{20,16},{24,28},{28,24},{32,36},... | collective-permute-start | bytes 442376 | tf_op jit(solution)/shard_map/ppermute | solution.py:457
  52.3 14.8 %collective-permute-start.1 = (bf16[16,2,2304]{2,1,0:T(2,128)(2,1)S(1)}, bf16[16,2,2304]{2,1,0:T(2,128)(2,1)S(1)}, u32[]{:S(2)}, u32[]{:S(2)}) collective-permute-start(bf16[16,2,2304]{2,1,0:T(2,128)(2,1)S(1)} %collective-permute-done.side_ref), channel_id=1, source_target_pairs={{0,4},{4,0},{8,12},{12,8},{16,20},{20,16},{24,28},{28,24},{32,36},... | collective-permute-start | bytes 442376 | tf_op jit(solution)/shard_map/ppermute | solution.py:458

commit v14 on v13

--- a/solution.py
+++ b/solution.py
@@ -285,9 +285,11 @@
 def summed(share, core_ref, list_ref, total_ref, data_ref, side_ref, finish):
     core = core_ref[0]
     total = total_ref[core]
-    early = lax.shift_right_logical(total * lax.bitwise_and(core, 1), 1)
-    begin = early if share == "late" else 0
-    end = early if share == "early" else total
+    odd = lax.bitwise_and(lax.axis_index("doc"), 1)
+    quarters, late = share
+    early = lax.shift_right_logical(total * odd * quarters, 2)
+    begin = early if late else 0
+    end = total if late else early
 
     def run(acc_a, acc_b):
         accumulate(core, begin, end, list_ref, data_ref, side_ref, (acc_a, acc_b))
@@ -344,7 +346,7 @@
     return pltpu.with_memory_space_constraint(array, pltpu.SMEM)
 
 
-def hist_of(core, plan, data, side, before=None, last=False, share="all"):
+def hist_of(core, plan, data, side, before=None, last=False, share=(0, True)):
     given = [in_vmem(data), in_vmem(side)]
     if before is not None:
         given.append(in_vmem(before))
@@ -456,10 +458,12 @@
     side_far = lax.ppermute(side, "doc", swap[1])
     side_near = lax.ppermute(side, "doc", swap[0])
     side_last = lax.ppermute(side_far, "doc", swap[0])
-    partial = hist_of(own, plan, data, side, share="early")
-    partial = hist_of(own, plan, data, side, partial, share="late")
+    partial = hist_of(own, plan, data, side, share=(3, False))
+    partial = hist_of(own, plan, data, side, partial, share=(3, True))
     partial = hist_of(lax.bitwise_xor(own, 1), plan, data, side_near, partial)
-    partial = hist_of(lax.bitwise_xor(own, 2), plan, data, side_far, partial)
+    across = lax.bitwise_xor(own, 2)
+    partial = hist_of(across, plan, data, side_far, partial, share=(2, False))
+    partial = hist_of(across, plan, data, side_far, partial, share=(2, True))
     hist = hist_of(lax.bitwise_xor(own, 3), plan, data, side_last, partial, True)
     return (t_plus[0], t_minus[0], gradients, hist)
 

time: 70.9 us -> 71.1 us (level)
    pallas_call x5 -> x6, Pallas kernels: 11.9 us -> 12.1 us  [hist_of(): pl.pallas_call(functools.partial(last_kernel if last else part_kernel, sh...]
where the time goes in v14:
time: 71.1 us; the launch traced here: 70.8 us
  waiting for transfers between devices  24.2 us (34%)
  starting transfers between devices  24 us (34%)
  Pallas kernels  20.6 us (29%)
  other arithmetic  1.27 us (2%)
  between operations  0.75 us (1%)
    all_to_all x1, waiting for transfers between devices, body(): data = lax.all_to_all(sent, 'doc', 0, 0, tiled=True)  14.7 us
    all_to_all x1, starting transfers between devices, body(): data = lax.all_to_all(sent, 'doc', 0, 0, tiled=True)  13.2 us
    pallas_call x6, Pallas kernels, hist_of(): pl.pallas_call(functools.partial(last_kernel if last else part_kernel, sh...  12.1 us
    all_to_all x1, waiting for transfers between devices, body(): lax.all_to_all(side, 'doc', 0, 0, axis_index_groups=alike, tiled=True)  9.41 us
    all_to_all x1, starting transfers between devices, body(): lax.all_to_all(side, 'doc', 0, 0, axis_index_groups=alike, tiled=True)  4 us
    ppermute x1, starting transfers between devices, body(): side_last = lax.ppermute(side_far, 'doc', swap[0])  3.35 us
    pallas_call x1, Pallas kernels, body(): pl.pallas_call(pair_kernel, out_shape=jax.ShapeDtypeStruct(sent_shape, jn...  3.05 us
    ppermute x1, starting transfers between devices, body(): side_near = lax.ppermute(side, 'doc', swap[0])  2.62 us
  transfers between devices with their start and end apart: 5, of which 2 were waited for; matrix products, arithmetic and copies ran while one was open for 2% of the time, Pallas kernels for 18%

profile of v14, /device:TPU:1, one launch (start us, length us, event | category | flops | bytes accessed | tf_op | source)
XLA Modules:
  0.0 70.8 jit_solution(2320637931934342536)
XLA Ops:
  0.6 3.1 %pair_terms.1 = bf16[64,2,1792]{2,1,0:T(2,128)(2,1)} custom-call(f32[136,128]{1,0:T(8,128)} %constant.49.clone.refs_0_.gap_ref, f32[12,128]{1,0:T(8,128)} %scores_ref.1, s32[12,128]{1,0:T(8,128)} %clicks_ref.1, s32[12]{0:T(128)} %lengths_ref.1, f32[1,128]{1,0:T(1,128)} %bitcast.10, f32[1,128]{1,0:T(1,128)} %bitcast.11, s32[128,1536]{1,0:T(8,128)} %refs_6_.1), custom_call_target="tpu_custom_call" | custom-call | tf_op jit(solution)/shard_map/pair_terms/pallas_call | solution.py:379
  3.7 13.2 %all-to-all-start = ((bf16[64,2,1792]{2,1,0:T(2,128)(2,1)}), bf16[64,2,1792]{2,1,0:T(2,128)(2,1)S(1)}, u32[]{:S(2)}, u32[]{:S(2)}) async-start(bf16[64,2,1792]{2,1,0:T(2,128)(2,1)} %pair_terms.1), calls=%async_computation | async-start | bytes 917504 | tf_op jit(solution)/shard_map/all_to_all | solution.py:398
  16.9 1.6 %ready_pairs.1 = (f32[12,128,128]{2,1,0:T(8,128)S(1)}, f32[12,128,128]{2,1,0:T(8,128)S(1)}, f32[12,128]{1,0:T(8,128)S(1)}, f32[12,128]{1,0:T(8,128)S(1)}, s32[12]{0:T(128)S(4)}) custom-call(f32[136,128]{1,0:T(8,128)} %constant.49.clone.refs_0_.gap_ref, f32[12,128]{1,0:T(8,128)} %scores_ref.1, s32[12,128]{1,0:T(8,128)} %clicks_ref.1, s32[12]{0:T(128)} %lengths_ref.1), custom_call_target="tpu_custom_call" | custom-call | tf_op jit(solution)/shard_map/ready_pairs/pallas_call | solution.py:399
  18.5 0.0 copy-start
  18.5 14.7 %all-to-all-done.data_ref = bf16[64,2,1792]{2,1,0:T(2,128)(2,1)S(1)} async-done(((bf16[64,2,1792]{2,1,0:T(2,128)(2,1)}), bf16[64,2,1792]{2,1,0:T(2,128)(2,1)S(1)}, u32[]{:S(2)}, u32[]{:S(2)}) %all-to-all-start) | async-done | bytes 458784 | tf_op jit(solution)/shard_map/all_to_all | solution.py:398
  33.2 0.0 copy-done
  33.2 1.4 %lambdas.1 = (f32[1,128]{1,0:T(1,128)S(1)}, f32[1,128]{1,0:T(1,128)S(1)}, f32[2,1536]{1,0:T(2,128)S(1)}, bf16[16,2,2304]{2,1,0:T(2,128)(2,1)}) custom-call(f32[12,128,128]{2,1,0:T(8,128)S(1)} %get-tuple-element.18.first_ref, f32[12,128,128]{2,1,0:T(8,128)S(1)} %get-tuple-element.19.second_ref, f32[12,128]{1,0:T(8,128)S(1)} %get-tuple-element.20.own_ref, ...), custom_call_target="tpu_custom_call" | custom-call | tf_op jit(solution)/shard_map/lambdas/pallas_call | solution.py:412
  34.7 4.0 %all-to-all-start.1 = ((bf16[16,2,2304]{2,1,0:T(2,128)(2,1)}), bf16[16,2,2304]{2,1,0:T(2,128)(2,1)S(1)}, u32[]{:S(2)}, u32[]{:S(2)}) async-start(bf16[16,2,2304]{2,1,0:T(2,128)(2,1)} %get-tuple-element.31), calls=%async_computation.1 | async-start | bytes 294912 | tf_op jit(solution)/shard_map/all_to_all | solution.py:440
  38.7 9.4 %all-to-all-done.1.side_ref = bf16[16,2,2304]{2,1,0:T(2,128)(2,1)S(1)} async-done(((bf16[16,2,2304]{2,1,0:T(2,128)(2,1)}), bf16[16,2,2304]{2,1,0:T(2,128)(2,1)S(1)}, u32[]{:S(2)}, u32[]{:S(2)}) %all-to-all-start.1) | async-done | bytes 147488 | tf_op jit(solution)/shard_map/all_to_all | solution.py:440
  48.1 0.9 %collective-permute-start = (bf16[16,2,2304]{2,1,0:T(2,128)(2,1)S(1)}, bf16[16,2,2304]{2,1,0:T(2,128)(2,1)S(1)}, u32[]{:S(2)}, u32[]{:S(2)}) collective-permute-start(bf16[16,2,2304]{2,1,0:T(2,128)(2,1)S(1)} %all-to-all-done.1.side_ref), channel_id=1, source_target_pairs={{0,32},{4,36},{8,40},{12,44},{16,48},{20,52},{24,56},{28,60},{32,0... | collective-permute-start | bytes 442376 | tf_op jit(solution)/shard_map/ppermute | solution.py:458
  49.0 0.7 %fusion = f32[64]{0:T(128)S(1)} fusion(bf16[64,2,1792]{2,1,0:T(2,128)(2,1)S(1)} %all-to-all-done.data_ref), kind=kLoop, calls=%fused_computation.1 | loop fusion | flops 294848 | bytes 196864 | tf_op jit(solution)/shard_map/reduce_sum | solution.py:441
  49.7 2.6 %collective-permute-start.2 = (bf16[16,2,2304]{2,1,0:T(2,128)(2,1)S(1)}, bf16[16,2,2304]{2,1,0:T(2,128)(2,1)S(1)}, u32[]{:S(2)}, u32[]{:S(2)}) collective-permute-start(bf16[16,2,2304]{2,1,0:T(2,128)(2,1)S(1)} %all-to-all-done.1.side_ref), channel_id=1, source_target_pairs={{0,4},{4,0},{8,12},{12,8},{16,20},{20,16},{24,28},{28,24},{32,36},... | collective-permute-start | bytes 442376 | tf_op jit(solution)/shard_map/ppermute | solution.py:459
  52.3 0.0 collective-permute-done.side_ref
  52.3 3.4 %collective-permute-start.1 = (bf16[16,2,2304]{2,1,0:T(2,128)(2,1)S(1)}, bf16[16,2,2304]{2,1,0:T(2,128)(2,1)S(1)}, u32[]{:S(2)}, u32[]{:S(2)}) collective-permute-start(bf16[16,2,2304]{2,1,0:T(2,128)(2,1)S(1)} %collective-permute-done.side_ref), channel_id=1, source_target_pairs={{0,4},{4,0},{8,12},{12,8},{16,20},{20,16},{24,28},{28,24},{32,36},... | collective-permute-start | bytes 442376 | tf_op jit(solution)/shard_map/ppermute | solution.py:460
  55.7 0.5 and_select_fusion.filled_ref
  56.2 2.4 %plan.1 = (s32[832]{0:T(1024)S(4)}, s32[4]{0:T(128)S(4)}, f32[1,128]{1,0:T(1,128)}, f32[1,128]{1,0:T(1,128)}, f32[2,1536]{1,0:T(2,128)}) custom-call(s32[64]{0:T(128)} %and_select_fusion.filled_ref, f32[1,128]{1,0:T(1,128)S(1)} %get-tuple-element.23.plus_in, f32[1,128]{1,0:T(1,128)S(1)} %get-tuple-element.24.minus_in, f32[2,1536]{1,0:T(2,128)S(1)} %get-tuple-element.25.grad_in), custom_call_target="tpu_custom_call" | custom-call | tf_op jit(solution)/shard_map/plan/pallas_call | solution.py:442
  58.6 2.1 %part.5.refs_0_ = f32[2,128,128]{2,1,0:T(8,128)S(1)} custom-call(s32[1]{0:T(128)} %bitcast.8.core_ref, s32[832]{0:T(1024)S(4)} %get-tuple-element.29.list_ref, s32[4]{0:T(128)S(4)} %get-tuple-element.30.total_ref, bf16[64,2,1792]{2,1,0:T(2,128)(2,1)S(1)} %all-to-all-done.data_ref, bf16[16,2,2304]{2,1,0:T(2,128)(2,1)S(1)} %all-to-all-done.1.side_ref), custom_call_target="tpu_custom_call" | custom-call | tf_op jit(solution)/shard_map/part/pallas_call | solution.py:357
  60.8 0.8 %part.6.refs_0_ = f32[2,128,128]{2,1,0:T(8,128)S(1)} custom-call(s32[1]{0:T(128)} %bitcast.8.core_ref, s32[832]{0:T(1024)S(4)} %get-tuple-element.29.list_ref, s32[4]{0:T(128)S(4)} %get-tuple-element.30.total_ref, bf16[64,2,1792]{2,1,0:T(2,128)(2,1)S(1)} %all-to-all-done.data_ref, bf16[16,2,2304]{2,1,0:T(2,128)(2,1)S(1)} %all-to-all-done.1.side_ref, ...), custom_call_target="tpu_custom_call" | custom-call | tf_op jit(solution)/shard_map/part/pallas_call | solution.py:357
  61.6 0.0 collective-permute-done.2.side_ref
  61.6 2.8 %part.7.refs_0_ = f32[2,128,128]{2,1,0:T(8,128)S(1)} custom-call(s32[1]{0:T(128)} %bitcast.7.core_ref, s32[832]{0:T(1024)S(4)} %get-tuple-element.29.list_ref, s32[4]{0:T(128)S(4)} %get-tuple-element.30.total_ref, bf16[64,2,1792]{2,1,0:T(2,128)(2,1)S(1)} %all-to-all-done.data_ref, bf16[16,2,2304]{2,1,0:T(2,128)(2,1)S(1)} %collective-permute-done.2.side_ref, ...), custom_call_target="tpu_custom_call" | custom-call | tf_op jit(solution)/shard_map/part/pallas_call | solution.py:357
  64.4 1.5 %part.8.refs_0_ = f32[2,128,128]{2,1,0:T(8,128)S(1)} custom-call(s32[1]{0:T(128)} %bitcast.6.core_ref, s32[832]{0:T(1024)S(4)} %get-tuple-element.29.list_ref, s32[4]{0:T(128)S(4)} %get-tuple-element.30.total_ref, bf16[64,2,1792]{2,1,0:T(2,128)(2,1)S(1)} %all-to-all-done.data_ref, bf16[16,2,2304]{2,1,0:T(2,128)(2,1)S(1)} %collective-permute-done.side_ref, ...), custom_call_target="tpu_custom_call" | custom-call | tf_op jit(solution)/shard_map/part/pallas_call | solution.py:357
  65.9 1.5 %part.9.before_ref = f32[2,128,128]{2,1,0:T(8,128)S(1)} custom-call(s32[1]{0:T(128)} %bitcast.6.core_ref, s32[832]{0:T(1024)S(4)} %get-tuple-element.29.list_ref, s32[4]{0:T(128)S(4)} %get-tuple-element.30.total_ref, bf16[64,2,1792]{2,1,0:T(2,128)(2,1)S(1)} %all-to-all-done.data_ref, bf16[16,2,2304]{2,1,0:T(2,128)(2,1)S(1)} %collective-permute-done.side_ref, ...), custom_call_target="tpu_custom_call" | custom-call | tf_op jit(solution)/shard_map/part/pallas_call | solution.py:357
  67.3 0.0 collective-permute-done.1.side_ref
  67.3 3.4 %last_part.1 = f32[2,64,256]{2,1,0:T(8,128)} custom-call(s32[1]{0:T(128)} %bitcast.5.core_ref, s32[832]{0:T(1024)S(4)} %get-tuple-element.29.list_ref, s32[4]{0:T(128)S(4)} %get-tuple-element.30.total_ref, bf16[64,2,1792]{2,1,0:T(2,128)(2,1)S(1)} %all-to-all-done.data_ref, bf16[16,2,2304]{2,1,0:T(2,128)(2,1)S(1)} %collective-permute-done.1.side_ref, ...), custom_call_target="tpu_custom_call" | custom-call | tf_op jit(solution)/shard_map/last_part/pallas_call | solution.py:357
Async XLA Ops:
  3.7 29.5 %all-to-all-start = ((bf16[64,2,1792]{2,1,0:T(2,128)(2,1)}), bf16[64,2,1792]{2,1,0:T(2,128)(2,1)S(1)}, u32[]{:S(2)}, u32[]{:S(2)}) async-start(bf16[64,2,1792]{2,1,0:T(2,128)(2,1)} %pair_terms.1), calls=%async_computation | async-start | bytes 917504 | tf_op jit(solution)/shard_map/all_to_all | solution.py:398
  18.5 14.8 %copy-start = (s32[1536]{0:T(1024)S(1)}, s32[1536]{0:T(1024)}, u32[]{:S(2)}) copy-start(s32[1536]{0:T(1024)} %param.13) | copy-start | bytes 18436
  34.7 13.4 %all-to-all-start.1 = ((bf16[16,2,2304]{2,1,0:T(2,128)(2,1)}), bf16[16,2,2304]{2,1,0:T(2,128)(2,1)S(1)}, u32[]{:S(2)}, u32[]{:S(2)}) async-start(bf16[16,2,2304]{2,1,0:T(2,128)(2,1)} %get-tuple-element.31), calls=%async_computation.1 | async-start | bytes 294912 | tf_op jit(solution)/shard_map/all_to_all | solution.py:440
  48.1 4.2 %collective-permute-start = (bf16[16,2,2304]{2,1,0:T(2,128)(2,1)S(1)}, bf16[16,2,2304]{2,1,0:T(2,128)(2,1)S(1)}, u32[]{:S(2)}, u32[]{:S(2)}) collective-permute-start(bf16[16,2,2304]{2,1,0:T(2,128)(2,1)S(1)} %all-to-all-done.1.side_ref), channel_id=1, source_target_pairs={{0,32},{4,36},{8,40},{12,44},{16,48},{20,52},{24,56},{28,60},{32,0... | collective-permute-start | bytes 442376 | tf_op jit(solution)/shard_map/ppermute | solution.py:458
  49.7 11.9 %collective-permute-start.2 = (bf16[16,2,2304]{2,1,0:T(2,128)(2,1)S(1)}, bf16[16,2,2304]{2,1,0:T(2,128)(2,1)S(1)}, u32[]{:S(2)}, u32[]{:S(2)}) collective-permute-start(bf16[16,2,2304]{2,1,0:T(2,128)(2,1)S(1)} %all-to-all-done.1.side_ref), channel_id=1, source_target_pairs={{0,4},{4,0},{8,12},{12,8},{16,20},{20,16},{24,28},{28,24},{32,36},... | collective-permute-start | bytes 442376 | tf_op jit(solution)/shard_map/ppermute | solution.py:459
  52.3 15.0 %collective-permute-start.1 = (bf16[16,2,2304]{2,1,0:T(2,128)(2,1)S(1)}, bf16[16,2,2304]{2,1,0:T(2,128)(2,1)S(1)}, u32[]{:S(2)}, u32[]{:S(2)}) collective-permute-start(bf16[16,2,2304]{2,1,0:T(2,128)(2,1)S(1)} %collective-permute-done.side_ref), channel_id=1, source_target_pairs={{0,4},{4,0},{8,12},{12,8},{16,20},{20,16},{24,28},{28,24},{32,36},... | collective-permute-start | bytes 442376 | tf_op jit(solution)/shard_map/ppermute | solution.py:460
